TPU v7x, 128 devices: a whole 4x4x4 slice. The times are simulated.
128 devices in a mesh: patch: 32 (over y, z, x_lo), level: 4 (over x_hi, core).
Axes of the slice: x: 4 (x_hi: 2, x_lo: 2; x = x_hi * 2 + x_lo), y: 4, z: 4, core: 2. Of those that a mesh axis runs over, the one named last changes fastest.
Arguments:
- fields: float32 [6, 64, 32768], P(None, None, ('patch', 'level')), may hold values from -6 to 6
- inv_jacobian: float32 [32768], P(('patch', 'level')), may hold values from 0.5 to 2
- diff_matrix: float32 [3, 64, 64], replicated, may hold values from -0.75 to 0.75
- face_interp: float32 [6, 16, 64], replicated, may hold values from -0.75 to 0.75
- lift_matrix: float32 [6, 64, 16], replicated, may hold values from -1.5 to 1.5
- flux_couple: float32 [6, 6, 6], replicated, may hold values from -2.5 to 2.5
- neighbours: int32 [6, 32768], P(None, ('patch', 'level')), may hold values from 0 to 287
- send_index: int32 [2, 2048], P(None, ('patch', 'level')), may hold values from 0 to 255
- bound_coef: float32 [6], replicated, may hold values from 0.5 to 1.5
- current_coef: float32 [6], replicated, may hold values from -1 to 1
- time_interp: float32 [64], replicated, may hold values from -2 to 2
- current_history: bfloat16 [64, 16384], P(None, ('patch', 'level')), may hold values from -6 to 6
- group_weight: bfloat16 [128, 16384], P(None, ('patch', 'level')), may hold values from -0.1875 to 0.1875
- projection: bfloat16 [16384, 512], P(('patch', 'level')), may hold values from -6 to 6
- kernels: bfloat16 [4, 32, 16, 64], P('level', 'patch'), may hold values from -0.75 to 0.75
- pair_dest: int32 [4, 32, 16], P('level', 'patch'), may hold values from 0 to 31, as said below
- pair_count: int32 [4, 32], P('level', 'patch'), may hold values from 8 to 16
Outputs:
- field_rate: float32 [6, 64, 32768], P(None, None, ('patch', 'level'))
- boundary_field: float32 [64, 16384], P(None, ('patch', 'level'))
Inputs may be any that keep to these rules, and one draw needn't show every extreme that they name: `pair_dest`: in each row the 16 entries are distinct patches, none the row's own patch. Only the first pair_count slots of a group are live. `neighbours`: indices below 256 are the device's own elements, then 16 ghosts from the device below and 16 from the device above along patch+level, wrapping. `send_index`: local element indices of the device.
All inputs are finite; a program needn't handle non-finite values.
Results may differ from a plain program's by a relative error of at most 0.0049.
Values may be sent and summed in bfloat16 or wider, within the bound.
No kernel may reach another device: no remote copies, remote signals or barrier semaphores. Data moves between devices by JAX's collectives and lax.ppermute only.
A program may use at most 192 MiB of HBM per device.

v0:
```python
import math

import jax
import jax.numpy as jnp
from jax import lax
from jax.sharding import PartitionSpec as P

NFP = 16
BE = 8


HIGH = lax.Precision.HIGHEST


def padded_2(array, sides, width):
    edges = {}
    for axis, dim in sides:
        size, length = (lax.axis_size(axis), array.shape[dim])
        up = [(i, (i + 1) % size) for i in range(size)]
        last = lax.slice_in_dim(array, length - width, length, axis=dim)
        leading = lax.slice_in_dim(array, 0, width, axis=dim)
        edges[dim] = (
            lax.ppermute(last, axis, up),
            lax.ppermute(leading, axis, [(b, a) for a, b in up]),
        )
    done = []
    for _, dim in sides:
        low, high = edges[dim]
        around = [(width, width) if d in done else (0, 0) for d in range(array.ndim)]
        array = jnp.concatenate([jnp.pad(low, around), array, jnp.pad(high, around)], axis=dim)
        done.append(dim)
    return array


def side_by_side(arrays, axis, dim, along):
    widths = [math.prod(a.shape[along:]) for a in arrays]
    both = jnp.concatenate(
        [a.reshape(*a.shape[:along], w) for a, w in zip(arrays, widths)], axis=along
    )
    filled = lax.all_gather(both, axis, axis=dim, tiled=True)
    pieces = jnp.split(filled, [sum(widths[:k]) for k in range(1, len(widths))], axis=along)
    return tuple(
        (b.reshape(*filled.shape[:along], *a.shape[along:]) for a, b in zip(arrays, pieces))
    )


def toeplitz(rows):
    count = rows.shape[-1]
    lagged = jnp.arange(count)[:, None] - jnp.arange(count)[None, :]
    picked = jnp.take(rows, jnp.clip(lagged, 0, count - 1), axis=-1)
    return jnp.where(lagged >= 0, picked, jnp.zeros_like(picked))


def per_device(
    fields,
    inv_jacobian,
    diff_matrix,
    face_interp,
    lift_matrix,
    flux_couple,
    neighbours,
    send_index,
    bound_coef,
    current_coef,
    time_interp,
    current_history,
    group_weight,
    projection,
    kernels,
    pair_dest,
    pair_count,
):
    elements = fields.shape[2]
    listed = send_index.shape[1]
    directions = projection.shape[1]
    packed = jnp.take(fields, send_index.reshape(-1), axis=2)
    extended = padded_2(packed.astype(jnp.bfloat16), ((("patch", "level"), 2),), listed).astype(
        packed.dtype
    )
    own = jnp.einsum("fqn,cne->fcqe", face_interp, fields, precision=HIGH)
    newest = jnp.einsum("c,cqe->eq", current_coef, own[5, :, :, :BE], precision=HIGH)
    newest = newest.reshape(1, -1).astype(jnp.bfloat16)
    currents = jnp.concatenate([current_history[1:], newest], axis=0)
    grads = jnp.einsum("rmn,cne->rcme", diff_matrix, fields, precision=HIGH) * inv_jacobian
    electric = jnp.stack(
        [grads[1, 5] - grads[2, 4], grads[2, 3] - grads[0, 5], grads[0, 4] - grads[1, 3]]
    )
    magnetic = -jnp.stack(
        [grads[1, 2] - grads[2, 1], grads[2, 0] - grads[0, 2], grads[0, 1] - grads[1, 0]]
    )
    volume = jnp.concatenate([electric, magnetic], axis=0)
    owner = lax.axis_index("patch") * lax.axis_size("level") + lax.axis_index("level")
    shard_currents, shard_weights, shard_projection = side_by_side(
        (currents[None], group_weight[None], projection[None]), ("patch", "level"), 0, 1
    )
    row = lax.dynamic_index_in_dim(shard_weights, owner, 1, keepdims=False)
    weighted = (shard_currents.astype(jnp.float32) * row.astype(jnp.float32)[:, None, :]).astype(
        jnp.bfloat16
    )
    rays = jnp.einsum("ntb,nbk->tk", weighted, shard_projection, preferred_element_type=jnp.float32)
    rays = rays.astype(jnp.bfloat16)
    patches = lax.axis_size("patch")
    pairs = pair_dest.shape[2]
    live = jnp.arange(pairs) < pair_count[0, 0]
    slots = (pair_dest[0, 0][None, :] == jnp.arange(patches)[:, None]) & live[None, :]
    table = jnp.dot(
        slots.astype(jnp.float32), kernels[0, 0].astype(jnp.float32), precision=HIGH
    ).astype(jnp.bfloat16)
    blocks = jnp.einsum("dts,sk->dtk", toeplitz(table), rays, preferred_element_type=jnp.float32)
    received = lax.all_to_all(blocks, "patch", split_axis=0, concat_axis=0, tiled=True)
    incoming = jnp.sum(received, axis=0)
    incoming = incoming.astype(jnp.bfloat16)
    image = jnp.einsum(
        "ntk,bk->ntb",
        lax.all_gather(incoming[None], ("patch", "level"), axis=0, tiled=True),
        projection,
        preferred_element_type=jnp.float32,
    )
    boundary_field = jnp.einsum(
        "ntb,nb->tb", image, group_weight.astype(jnp.float32), precision=HIGH
    )
    boundary_field = boundary_field * (1.0 / jnp.sqrt(jnp.float32(directions)))
    ghosts = jnp.concatenate([extended[:, :, :listed], extended[:, :, 3 * listed :]], axis=2)
    pool = jnp.concatenate([fields, ghosts], axis=2)
    opposite = face_interp[jnp.array([1, 0, 3, 2, 5, 4])]
    across = pool[:, :, neighbours]
    neighbour = jnp.einsum("fqn,cnfe->fcqe", opposite, across, precision=HIGH)
    interp = jnp.dot(time_interp, boundary_field, precision=HIGH).reshape(BE, NFP)
    exterior = bound_coef[:, None, None] * interp.T[None]
    padded = jnp.pad(exterior, ((0, 0), (0, 0), (0, elements - BE)))
    isbound = (jnp.arange(6)[:, None, None, None] == 5) & (
        jnp.arange(elements)[None, None, None, :] < BE
    )
    neighbour = jnp.where(isbound, padded[None], neighbour)
    flux = jnp.einsum("fcd,fdqe->fcqe", flux_couple, neighbour - own, precision=HIGH)
    surface = jnp.einsum("fnq,fcqe->cne", lift_matrix, flux, precision=HIGH)
    return (volume + surface, boundary_field)


def solution(mesh):
    placed = (
        P(None, None, ("patch", "level")),
        P(("patch", "level")),
        P(),
        P(),
        P(),
        P(),
        P(None, ("patch", "level")),
        P(None, ("patch", "level")),
        P(),
        P(),
        P(),
        P(None, ("patch", "level")),
        P(None, ("patch", "level")),
        P(("patch", "level"), None),
        P("level", "patch", None, None),
        P("level", "patch", None),
        P("level", "patch"),
    )
    return jax.shard_map(
        per_device,
        mesh=mesh,
        in_specs=placed,
        out_specs=(P(None, None, ("patch", "level")), P(None, ("patch", "level"))),
        check_vma=False,
    )
```

profile of v0, /device:TPU:0, one launch (start us, length us, event | category | flops | bytes accessed | tf_op | source)
XLA Modules:
  0.0 635.2 jit_solution(1498488128393288354)
XLA Ops:
  7.2 1.6 convolution_bitcast_fusion.1
  8.8 0.7 fusion.43
  9.6 0.1 copy.72
  9.7 0.1 convert_element_type.61
  9.8 0.7 slice.66
  10.5 1.1 copy.98
  11.6 0.8 copy.118
  12.5 1.1 maximum_bitcast_fusion
  13.7 0.1 reshape.285
  14.4 0.8 convolution_convert_fusion
  15.2 0.1 copy.59
  15.4 12.1 %gather_fusion = bf16[4096,32]{1,0:T(8,128)(2,1)S(1)} fusion(bf16[32,64]{0,1:T(8,128)(2,1)S(1)} %copy.59, s32[4096]{0:T(1024)S(1)} %broadcast_clamp_fusion), kind=kCustom, calls=%fused_computation | custom fusion | bytes 540672 | tf_op jit(solution)/shard_map/jit(_take)/gather | solution.py:50
  27.5 1.0 copy.60
  28.5 247.1 %all-gather.7.cloned.1.call-done = bf16[128,1,90112]{2,1,0:T(2,128)(2,1)} async-done(((bf16[1,1,90112]{2,1,0:T(2,128)(2,1)}), bf16[128,1,90112]{2,1,0:T(2,128)(2,1)}) %all-gather.7.cloned.1.call-update) | async-done | bytes 23068688 | tf_op jit(solution)/shard_map/all_gather | solution.py:40
  275.6 39.5 %copy.117 = bf16[128,1,90112]{2,0,1:T(8,128)(2,1)} copy(bf16[128,1,90112]{2,1,0:T(2,128)(2,1)} %all-gather.7.cloned.1.call-done) | data formatting | bytes 46137344
  315.1 2.5 slice_bitcast_fusion
  317.6 2.0 convert_bitcast_fusion
  319.6 8.0 %split.14 = bf16[128,65536]{1,0:T(8,128)(2,1)S(1)} slice(bf16[128,90112]{1,0:T(8,128)(2,1)} %bitcast.199), slice={[0:128], [24576:90112]} | slice | bytes 33554432 | tf_op jit(solution)/shard_map/split | solution.py:41
  327.5 3.2 copy.100
  330.7 0.7 copy.99
  331.5 8.8 %copy.101 = bf16[16,8,128,512]{3,2,1,0:T(8,128)(2,1)} copy(bf16[16,8,128,512]{3,1,2,0:T(8,128)(2,1)S(1)} %bitcast.201) | data formatting | bytes 33554432
  340.2 1.0 dynamic-slice_convert_fusion
  341.2 0.7 fusion.2
  341.9 9.7 %fusion.16 = f32[32,64,512]{2,1,0:T(8,128)} fusion(bf16[128,64,128]{2,1,0:T(8,128)(2,1)S(1)} %fusion.2, bf16[128,128,512]{2,1,0:T(8,128)(2,1)} %bitcast.200, bf16[64,64,32]{1,0,2:T(8,128)(2,1)S(1)} %copy.60, pred[64,64]{1,0:T(8,128)(4,1)S(1)} %get-tuple-element.11, pred[64,64]{1,0:T(8,128)(4,1)S(1)} %get-tuple-element.12), kind=kOutput, calls=%fused_computation.25 | convolution fusion | flops 1208254464 | bytes 23339008 | tf_op jit(solution)/shard_map/dts,sk->dtk/dot_general | solution.py:109
  351.6 57.8 %all_to_all.5 = f32[32,64,512]{2,1,0:T(8,128)} all-to-all(f32[32,64,512]{2,1,0:T(8,128)} %fusion.16), channel_id=1, replica_groups=mesh['patch'=32,'level'=4] {'patch'}, dimensions={0} | all-to-all | bytes 8388608 | tf_op jit(solution)/shard_map/all_to_all | solution.py:110
  409.5 3.2 reduce_sum.9
  412.7 0.4 copy.63
  413.1 0.1 reshape.280
  413.2 0.1 reshape.279
  413.3 0.6 gather_fusion.1
  413.9 0.1 fusion.30
  414.1 0.1 collective-permute-start
  414.1 7.2 %collective-permute-start.1 = (bf16[6,64,16]{1,0,2:T(8,128)(2,1)S(1)}, bf16[6,64,16]{1,0,2:T(8,128)(2,1)S(1)}, u32[]{:S(2)}, u32[]{:S(2)}) collective-permute-start(bf16[6,64,16]{1,0,2:T(8,128)(2,1)S(1)} %get-tuple-element.10), channel_id=1, source_target_pairs={{1,0},{2,1},{3,2},{4,3},{5,4},{6,5},{7,6},{8,7},{9,8},{10,9},{11,1... | collective-permute-start | bytes 36872 | tf_op jit(solution)/shard_map/ppermute | solution.py:24
  421.3 0.6 pad_clamp_fusion
  421.9 1.1 fusion.3
  423.1 0.7 broadcast_and_fusion
  423.8 0.6 gather_fusion.3
  424.5 0.2 pad_maximum_fusion
  424.6 5.8 gather_fusion.2
  430.4 181.8 %all-gather.5.cloned.1.call-done = bf16[8192,512]{1,0:T(8,128)(2,1)} async-done(((bf16[64,512]{1,0:T(8,128)(2,1)}), bf16[8192,512]{1,0:T(8,128)(2,1)}) %all-gather.5.cloned.1.call-update) | async-done | bytes 8388624 | tf_op jit(solution)/shard_map/all_gather | solution.py:115
  612.2 5.8 multiply_reduce_fusion
  618.0 0.1 convolution_bitcast_fusion.4
  618.2 0.1 reshape.278
  618.2 0.1 copy.61
  618.3 0.1 broadcast_multiply_fusion
  618.4 7.4 %fusion.10 = f32[6,6,16,256]{3,2,0,1:T(8,128)S(1)} fusion(f32[6,6,16,256]{3,2,0,1:T(8,128)S(1)} %convolution_bitcast_fusion.1, f32[6,64,6,256]{1,0,3,2:T(8,128)} %bitcast.202, f32[6,16,256]{2,1,0:T(8,128)S(1)} %pad.4, pred[6,256]{1,0:T(8,128)(4,1)S(1)} %copy-done.8, f32[6,16,64]{2,1,0:T(8,128)S(1)} %gather_fusion.3), kind=kOutput, calls=%fused_computation.18 | convolution fusion | flops 113541120 | bytes 3663360 | tf_op jit(solution)/shard_map/fqn,cnfe->fcqe/dot_general | solution.py:127
  625.8 1.1 convolution_bitcast_fusion
  626.9 1.5 fusion.13
  (58 shorter events, 0.5 us)
Async XLA Ops:
  7.2 414.8 %copy-start = (f32[3,64,64]{2,1,0:T(8,128)S(1)}, f32[3,64,64]{2,1,0:T(8,128)}, u32[]{:S(2)}) copy-start(f32[3,64,64]{2,1,0:T(8,128)} %param.20) | copy-start | bytes 147460
  7.2 268.4 %all-gather.7.cloned.1.call-start = ((), (), s32[]{:S(2)}) async-start(), calls=%async_computation.2 | async-start | bytes 46497792 | tf_op jit(solution)/shard_map/all_gather | solution.py:40
  13.6 598.6 %all-gather.5.cloned.1.call-start = ((), (), s32[]{:S(2)}) async-start(), calls=%async_computation.1 | async-start | bytes 8454144 | tf_op jit(solution)/shard_map/all_gather | solution.py:115
  409.4 3.3 copy-start.1
  409.4 3.7 copy-start.14
  409.4 11.9 %copy-start.9 = (s32[6,256]{1,0:T(8,128)S(1)}, s32[6,256]{1,0:T(8,128)}, u32[]{:S(2)}) copy-start(s32[6,256]{1,0:T(8,128)} %param.24) | copy-start | bytes 18436
  409.4 12.5 %copy-start.10 = (f32[256]{0:T(256)S(1)}, f32[256]{0:T(256)}, u32[]{:S(2)}) copy-start(f32[256]{0:T(256)} %param.19) | copy-start | bytes 3076
  409.4 14.4 %copy-start.4 = (bf16[128,128]{1,0:T(8,128)(2,1)S(1)}, bf16[128,128]{1,0:T(8,128)(2,1)}, u32[]{:S(2)}) copy-start(bf16[128,128]{1,0:T(8,128)(2,1)} %param.30) | copy-start | bytes 98308
  409.4 14.4 %copy-start.13 = (s32[6]{0:T(128)S(1)}, s32[6]{0:T(128)}, u32[]{:S(2)}) copy-start(s32[6]{0:T(128)} %constant.80) | copy-start | bytes 76
  409.5 14.4 %copy-start.2 = (f32[6,16,64]{2,1,0:T(8,128)S(1)}, f32[6,16,64]{2,1,0:T(8,128)}, u32[]{:S(2)}) copy-start(f32[6,16,64]{2,1,0:T(8,128)} %param.21) | copy-start | bytes 73732
  414.1 10.3 %collective-permute-start = (bf16[6,64,16]{1,0,2:T(8,128)(2,1)S(1)}, bf16[6,64,16]{1,0,2:T(8,128)(2,1)S(1)}, u32[]{:S(2)}, u32[]{:S(2)}) collective-permute-start(bf16[6,64,16]{1,0,2:T(8,128)(2,1)S(1)} %get-tuple-element.9), channel_id=1, source_target_pairs={{0,1},{1,2},{2,3},{3,4},{4,5},{5,6},{6,7},{7,8},{8,9},{9,10},{10,1... | collective-permute-start | bytes 36872 | tf_op jit(solution)/shard_map/ppermute | solution.py:23
  414.1 10.3 %collective-permute-start.1 = (bf16[6,64,16]{1,0,2:T(8,128)(2,1)S(1)}, bf16[6,64,16]{1,0,2:T(8,128)(2,1)S(1)}, u32[]{:S(2)}, u32[]{:S(2)}) collective-permute-start(bf16[6,64,16]{1,0,2:T(8,128)(2,1)S(1)} %get-tuple-element.10), channel_id=1, source_target_pairs={{1,0},{2,1},{3,2},{4,3},{5,4},{6,5},{7,6},{8,7},{9,8},{10,9},{11,1... | collective-permute-start | bytes 36872 | tf_op jit(solution)/shard_map/ppermute | solution.py:24
  424.4 187.7 %copy-start.3 = (bf16[128,512]{1,0:T(8,128)(2,1)S(1)}, bf16[128,512]{1,0:T(8,128)(2,1)}, u32[]{:S(2)}) copy-start(bf16[128,512]{1,0:T(8,128)(2,1)} %param.31) | copy-start | bytes 393220
  612.2 5.8 copy-start.11
  612.2 6.1 copy-start.12
  612.2 6.2 copy-start.8
  618.0 7.8 %copy-start.7 = (f32[6,6,6]{2,1,0:T(8,128)S(1)}, f32[6,6,6]{2,1,0:T(8,128)}, u32[]{:S(2)}) copy-start(f32[6,6,6]{2,1,0:T(8,128)} %param.23) | copy-start | bytes 2596
  618.0 9.0 %copy-start.6 = (f32[6,64,16]{1,2,0:T(8,128)S(1)}, f32[6,64,16]{1,2,0:T(8,128)}, u32[]{:S(2)}) copy-start(f32[6,64,16]{1,2,0:T(8,128)} %param.22) | copy-start | bytes 73732
  618.0 10.4 %copy-start.5 = (f32[64,128]{1,0:T(8,128)}, f32[64,128]{1,0:T(8,128)S(1)}, u32[]{:S(2)}) copy-start(f32[64,128]{1,0:T(8,128)S(1)} %multiply_bitcast_fusion) | copy-start | bytes 98308
Sparse Core Ops, SparseCore 0:
  13.7 261.8 all-gather.6
  412.8 199.3 all-gather.4
where the time goes:
time: 636 us; the launch traced here: 635 us
  waiting for transfers between devices  429 us (67%)
  local copies, waits for them, and re-layouts  86.5 us (14%)
  blocking collectives  57.8 us (9%)
  matrix products  29.1 us (5%)
  between operations  15.1 us (2%)
  other arithmetic  10.5 us (2%)
  starting transfers between devices  7.32 us (1%)
    all_gather x1, waiting for transfers between devices, side_by_side(): filled = lax.all_gather(both, axis, axis=dim, tiled=True)  247 us
    all_gather x1, waiting for transfers between devices, per_device(): lax.all_gather(incoming[None], ('patch', 'level'), axis=0, tiled=True)  182 us
    all_to_all x1, blocking collectives, per_device(): lax.all_to_all(blocks, 'patch', split_axis=0, concat_axis=0, tiled=True)  57.8 us
    unnamed x39, local copies, waits for them, and re-layouts  57.1 us
    gather x2, local copies, waits for them, and re-layouts, toeplitz(): picked = jnp.take(rows, jnp.clip(lagged, 0, count - 1), axis=-1)  13.1 us
  transfers between devices with their start and end apart: 4, of which 2 were waited for; matrix products, arithmetic and copies ran while one was open for 4% of the time, Pallas kernels for 0%

commit v1 on v0

v1 whole, which is shorter than its diff:
```python
import functools

import jax
import jax.numpy as jnp
import numpy as np
from jax import lax
from jax.experimental import pallas as pl
from jax.experimental.pallas import tpu as pltpu
from jax.sharding import Mesh, PartitionSpec as P

F32 = jnp.float32
BF16 = jnp.bfloat16
HIGH = lax.Precision.HIGHEST
AXES = ("y", "z", "xl", "xh", "c")
VMEM = pl.BlockSpec(memory_space=pltpu.VMEM)
SMEM = pl.BlockSpec(memory_space=pltpu.SMEM)
ROW_C, ROW_W, ROW_T, ROWS = 128, 192, 256, 272
NN = (((1,), (0,)), ((), ()))
NT = (((1,), (1,)), ((), ()))
TN = (((0,), (0,)), ((), ()))


def iota(shape, dim):
    return lax.broadcasted_iota(jnp.int32, shape, dim)


def mm(a, b, dims=NN, precision=None):
    return lax.dot_general(a, b, dims, precision=precision, preferred_element_type=F32)


def one_hot(mask, dtype=F32):
    return jnp.where(mask, 1.0, 0.0).astype(dtype)


def halves(x):
    high = x.astype(BF16)
    return high, (x - high.astype(F32)).astype(BF16)


def lane_blocks_swapped(parts):
    parts = list(parts)
    shape = parts[0].shape
    block = iota(shape, 1) // 16
    for m in (4, 2, 1):
        upper = (block & m) != 0
        for j in range(8):
            if j & m:
                continue
            a, b = parts[j], parts[j + m]
            parts[j] = jnp.where(upper, pltpu.roll(b, 16 * m, 1), a)
            parts[j + m] = jnp.where(upper, b, pltpu.roll(a, 128 - 16 * m, 1))
    return parts


def pack_kernel(
    core_ref, send_ref, dest_ref, count_ref, coef_ref,
    fields_ref, interp_ref, history_ref, weight_ref, projection_ref, kernels_ref,
    message_ref, on_ref, off_ref,
):
    core = core_ref[0]
    elements = fields_ref.shape[2]
    flat = fields_ref[...].reshape(384, elements).astype(BF16)

    def picked(row):
        rows, lanes = iota((16, elements), 0), iota((16, elements), 1)
        wanted = jnp.zeros((16, elements), jnp.int32)
        for i in range(16):
            wanted = jnp.where(rows == i, send_ref[row, i], wanted)
        return mm(one_hot(lanes == wanted, BF16), flat, NT).astype(BF16)

    on_ref[...] = picked(1 - core)
    off_ref[...] = picked(core)
    mixed = jnp.zeros((64, 128), F32)
    for c in range(6):
        mixed = mixed + coef_ref[c] * fields_ref[c, :, 0:128]
    spread = one_hot(iota((128, 128), 1) // 16 == iota((128, 128), 0))
    chosen = one_hot(iota((16, 128), 1) % 16 == iota((16, 128), 0))
    by_element = mm(mixed, spread, NN, HIGH)
    by_node = mm(interp_ref[5], chosen, TN, HIGH)
    newest = jnp.sum(by_element * by_node, axis=0, keepdims=True)
    old = pltpu.roll(history_ref[...].astype(F32), 63, 0)
    currents = jnp.where(iota((64, 128), 0) == 63, newest, old).astype(BF16)
    lane_patch = iota((16, 128), 1) % 32
    wanted = jnp.full((16, 128), -1, jnp.int32)
    for j in range(16):
        to = jnp.where(j < count_ref[0, 0], dest_ref[0, 0, j], -1)
        wanted = jnp.where(iota((16, 128), 0) == j, to, wanted)
    spread_kernels = mm(kernels_ref[0, 0], one_hot(wanted == lane_patch, BF16), TN)
    group_of = iota((8, 128), 1) // 32
    table = []
    for h in range(2):
        rows = jnp.zeros((8, 128), F32)
        for a in range(4):
            at = 32 * h + 8 * a
            rows = jnp.where(group_of == a, spread_kernels[at : at + 8], rows)
        table.append(rows)
    table = jnp.concatenate(table, axis=0).astype(BF16)
    weights = []
    for level in range(4):
        pick = one_hot(iota((32, 128), 1) == 4 * iota((32, 128), 0) + level, BF16)
        weights.append(mm(pick, weight_ref[...]).astype(BF16))
    for i in range(8):
        z, xh = i // 2, i % 2
        message_ref[i, 0:128, :] = projection_ref[:, 128 * z : 128 * z + 128]
        message_ref[i, ROW_C : ROW_C + 64, :] = currents
        message_ref[i, ROW_W : ROW_W + 32, :] = weights[2 * xh]
        message_ref[i, ROW_W + 32 : ROW_W + 64, :] = weights[2 * xh + 1]
        message_ref[i, ROW_T:ROWS, :] = table


def own_weights(ref, i, core):
    return ref[i, pl.ds(pl.multiple_of(ROW_W + 32 * core, 32), 32), :]


def rays_kernel(core_ref, mine_ref, other_ref, out_ref, c_ref, w_ref, p_ref):
    core = core_ref[0]
    for i in range(8):
        for s, ref in ((0, mine_ref), (1, other_ref)):
            at = 256 * i + 128 * s
            c_ref[:, at : at + 128] = ref[i, ROW_C : ROW_C + 64, :].astype(F32)
            w_ref[:, at : at + 128] = own_weights(ref, i, core).astype(F32)
            p_ref[at : at + 128, :] = ref[i, 0:128, :]

    def step(high, carry):
        c = c_ref[pl.ds(pl.multiple_of(8 * high, 8), 8), :]
        w = w_ref[...]
        rows = [(c[t : t + 1] * w).astype(BF16) for t in range(8)]
        product = mm(jnp.concatenate(rows, axis=0), p_ref[...])
        parts = lane_blocks_swapped([product[32 * t : 32 * t + 32] for t in range(8)])
        for r in range(8):
            out_ref[r, pl.ds(pl.multiple_of(32 * high, 32), 32), :] = parts[r].astype(BF16)
        return carry

    lax.fori_loop(0, 8, step, 0)
    half = core_ref[1]
    for r in range(8):
        for z in range(4):
            out_ref[r, 256 + 16 * z : 272 + 16 * z, :] = mine_ref[2 * z + half, ROW_T:ROWS, :]


def translate_kernel(got_ref, out_ref, h_ref, s_ref):
    total = got_ref[0, 0:256, :].astype(F32)
    for r in range(1, 8):
        total = total + got_ref[r, 0:256, :].astype(F32)
    rays = total.astype(BF16).astype(F32)
    for r in range(8):
        y, xl = r // 2, r % 2
        for z in range(4):
            patch = 8 * y + 2 * z + xl
            tile = got_ref[r, 256 + 16 * z : 272 + 16 * z, :].astype(F32)
            for h in range(2):
                h_ref[h, pl.ds(patch, 8, stride=32), :] = tile[8 * h : 8 * h + 8]
    table = jnp.concatenate([h_ref[0], h_ref[1]], axis=1).astype(BF16)
    by_high = [rays[32 * t : 32 * t + 32] for t in range(8)]
    lane = iota((32, 128), 1)
    columns = []
    for t in range(8):
        rows = [by_high[t]]
        for b in range(1, 8):
            here = pltpu.roll(by_high[t], 16 * b, 1)
            before = pltpu.roll(by_high[t - 1], 16 * b, 1) if t > 0 else jnp.zeros((32, 128), F32)
            rows.append(jnp.where(lane < 16 * b, before, here))
        columns.append(jnp.concatenate(rows, axis=0).astype(BF16))
    lagged = [mm(table, column, TN) for column in columns]
    for t in range(8):
        incoming = lagged[t][0:32]
        for a in range(1, t + 1):
            incoming = incoming + lagged[t - a][32 * a : 32 * a + 32]
        s_ref[pl.ds(t, 32, stride=8), :] = incoming
    incoming = s_ref[...].astype(BF16)
    for r in range(8):
        out_ref[r] = incoming


def image_kernel(core_ref, got_ref, mine_ref, other_ref, own_ref, partner_ref, rows_ref):
    core = core_ref[0]
    parts = lane_blocks_swapped([got_ref[r].astype(F32) for r in range(8)])
    for t in range(8):
        rows_ref[256 * t : 256 * t + 256, :] = parts[t].astype(BF16)

    def step(i, carry):
        for ref, out in ((mine_ref, own_ref), (other_ref, partner_ref)):
            image = mm(rows_ref[...], ref[i, 0:128, :], NT)
            weight = own_weights(ref, i, core).astype(F32)
            weight = jnp.broadcast_to(weight[:, None, :], (32, 8, 128))
            for t in range(8):
                block = image[256 * t : 256 * t + 256].reshape(32, 8, 128)
                out[i, 8 * t : 8 * t + 8, :] = jnp.sum(block * weight, axis=0)
        return carry

    lax.fori_loop(0, 8, step, 0)


def element_kernel(
    core_ref, couple_ref, fields_ref, scale_ref, diff_ref, interp_ref, lift_ref, links_ref,
    on_ref, off_ref, out_ref,
):
    core = core_ref[0]
    elements = fields_ref.shape[2]
    interp = interp_ref[...].reshape(96, 64)
    diff = diff_ref[...].reshape(192, 64)
    ghosts = jnp.concatenate([on_ref[...], off_ref[...]], axis=0).astype(F32)
    own, ghost = [], []
    grads = []
    for c in range(6):
        local = fields_ref[c]
        own.append(mm(interp, local, NN, HIGH))
        ghost.append(mm(interp, ghosts[:, 64 * c : 64 * c + 64], NT, HIGH))
        grads.append(mm(diff, local, NN, HIGH))
    surface = [jnp.zeros((64, elements), F32) for _ in range(6)]
    bound = iota((16, elements), 1) < 8
    for f in range(6):
        at, to = 16 * f, 16 * (f ^ 1)
        pool = jnp.concatenate([own[c][to : to + 16] for c in range(6)], axis=0)
        beyond = jnp.concatenate([ghost[c][to : to + 16] for c in range(6)], axis=0)
        links = links_ref[f : f + 1, :]
        inside = one_hot(iota((elements, elements), 0) == links, BF16)
        outer = links - elements
        outer = jnp.where(core == 0, outer ^ 16, outer)
        outside = one_hot(iota((32, elements), 0) == outer, BF16)
        high, low = halves(pool)
        ghost_high, ghost_low = halves(beyond)
        across = mm(high, inside) + mm(low, inside) + mm(ghost_high, outside) + mm(ghost_low, outside)
        jumps = []
        for c in range(6):
            there = across[16 * c : 16 * c + 16]
            if f == 5:
                there = jnp.where(bound, 0.0, there)
            jumps.append(there - own[c][at : at + 16])
        for c in range(6):
            flux = couple_ref[f, c, 0] * jumps[0]
            for k in range(1, 6):
                flux = flux + couple_ref[f, c, k] * jumps[k]
            surface[c] = surface[c] + mm(lift_ref[f], flux, NN, HIGH)

    def grad(r, c):
        return grads[c][64 * r : 64 * r + 64]

    curls = (
        grad(1, 5) - grad(2, 4),
        grad(2, 3) - grad(0, 5),
        grad(0, 4) - grad(1, 3),
        grad(2, 1) - grad(1, 2),
        grad(0, 2) - grad(2, 0),
        grad(1, 0) - grad(0, 1),
    )
    scale = scale_ref[...]
    for c in range(6):
        out_ref[c] = curls[c] * scale + surface[c]


def finish_kernel(
    bound_ref, couple_ref, parts_ref, rate_ref, lift_ref, time_ref, rate_out, field_out,
):
    total = parts_ref[0]
    for i in range(1, 8):
        total = total + parts_ref[i]
    total = total * jnp.float32(1.0 / np.sqrt(np.float32(512)))
    for t in range(8):
        field_out[pl.ds(t, 8, stride=8), :] = total[8 * t : 8 * t + 8]
    now = mm(time_ref[...], field_out[...], NN, HIGH)
    node = iota((16, 128), 1) % 16 == iota((16, 128), 0)
    by_node = jnp.where(node, now, 0.0)
    collect = one_hot(iota((128, 128), 0) // 16 == iota((128, 128), 1))
    lifted = mm(lift_ref[5], mm(by_node, collect, NN, HIGH), NN, HIGH)
    for c in range(6):
        factor = couple_ref[5, c, 0] * bound_ref[0]
        for k in range(1, 6):
            factor = factor + couple_ref[5, c, k] * bound_ref[k]
        rate_out[c, :, 0:128] = rate_ref[c, :, 0:128] + factor * lifted
        rate_out[c, :, 128:256] = rate_ref[c, :, 128:256]


def call(kernel, out, in_specs, scratch=(), **options):
    return pl.pallas_call(
        kernel,
        out_shape=out,
        in_specs=in_specs,
        out_specs=jax.tree.map(lambda _: VMEM, out),
        scratch_shapes=list(scratch),
        **options,
    )


def shaped(shape, dtype):
    return jax.ShapeDtypeStruct(shape, dtype)


def per_device(
    fields, inv_jacobian, diff_matrix, face_interp, lift_matrix, flux_couple, neighbours,
    send_index, bound_coef, current_coef, time_interp, current_history, group_weight, projection,
    kernels, pair_dest, pair_count,
):
    place = jnp.stack([lax.axis_index("c"), lax.axis_index("xh")]).astype(jnp.int32)
    message, on_chip, off_chip = call(
        pack_kernel,
        (shaped((8, ROWS, 128), BF16), shaped((16, 384), BF16), shaped((16, 384), BF16)),
        [SMEM] * 5 + [VMEM] * 6,
    )(
        place, send_index, pair_dest, pair_count, current_coef,
        fields, face_interp, current_history, group_weight, projection, kernels,
    )
    devices = 128
    across = [(d, (d + 1 if d % 2 else d - 1) % devices) for d in range(devices)]
    off_chip = lax.ppermute(off_chip, AXES, across)
    on_chip = lax.ppermute(on_chip, "c", [(0, 1), (1, 0)])
    mine = lax.all_to_all(message, ("z", "xh"), 0, 0, tiled=True)
    other = lax.ppermute(mine, "c", [(0, 1), (1, 0)])
    rate = call(
        element_kernel, shaped((6, 64, 256), F32), [SMEM] * 2 + [VMEM] * 8
    )(
        place, flux_couple, fields, inv_jacobian.reshape(1, -1), diff_matrix, face_interp,
        lift_matrix, neighbours, on_chip, off_chip,
    )
    partial = call(
        rays_kernel,
        shaped((8, 320, 128), BF16),
        [SMEM, VMEM, VMEM],
        (pltpu.VMEM((64, 2048), F32), pltpu.VMEM((32, 2048), F32), pltpu.VMEM((2048, 128), BF16)),
    )(place, mine, other)
    partial = lax.all_to_all(partial, ("y", "xl"), 0, 0, tiled=True)
    incoming = call(
        translate_kernel,
        shaped((8, 256, 128), BF16),
        [VMEM],
        (pltpu.VMEM((2, 256, 128), F32), pltpu.VMEM((256, 128), F32)),
    )(partial)
    incoming = lax.all_to_all(incoming, ("y", "xl"), 0, 0, tiled=True)
    own, partner = call(
        image_kernel,
        (shaped((8, 64, 128), F32), shaped((8, 64, 128), F32)),
        [SMEM, VMEM, VMEM, VMEM],
        (pltpu.VMEM((2048, 128), BF16),),
    )(place, incoming, mine, other)
    parts = own + lax.ppermute(partner, "c", [(0, 1), (1, 0)])
    parts = lax.all_to_all(parts, ("z", "xh"), 0, 0, tiled=True)
    return call(
        finish_kernel,
        (shaped((6, 64, 256), F32), shaped((64, 128), F32)),
        [SMEM] * 2 + [VMEM] * 4,
    )(bound_coef, flux_couple, parts, rate, lift_matrix, time_interp.reshape(1, -1))


def solution(mesh):
    mesh = Mesh(np.asarray(mesh.devices).reshape(4, 4, 2, 2, 2), AXES)
    patch, level = ("y", "z", "xl"), ("xh", "c")
    placed = (
        P(None, None, AXES), P(AXES), P(), P(), P(), P(), P(None, AXES), P(None, AXES), P(), P(),
        P(), P(None, AXES), P(None, AXES), P(AXES, None), P(level, patch, None, None),
        P(level, patch, None), P(level, patch),
    )
    return jax.shard_map(
        per_device,
        mesh=mesh,
        in_specs=placed,
        out_specs=(P(None, None, AXES), P(None, AXES)),
        check_vma=False,
    )
```

time: 636 us -> 101 us (0.16)
  waiting for transfers between devices: 429 us -> 6.46 us
  local copies, waits for them, and re-layouts: 86.5 us -> 2.9 us
  matrix products: 29.1 us -> 0 us
  Pallas kernels: 0 us -> 27.9 us
  between operations: 15.1 us -> 1.32 us
  other arithmetic: 10.5 us -> 2.36 us
  blocking collectives: 57.8 us -> 49.7 us
    all_gather x2 -> x0, waiting for transfers between devices: 429 us -> none  [the longest x1 247 us: side_by_side(): filled = lax.all_gather(both, axis, axis=dim, tiled=True)]
    unnamed x39 -> x17, local copies, waits for them, and re-layouts: 57.1 us -> 2.9 us
    dot_general x9 -> x0, matrix products: 29.1 us -> none  [the longest x1 9.72 us: per_device(): jnp.einsum('dts,sk->dtk', toeplitz(table), rays, preferred_element_type=j...]
    pallas_call x0 -> x6, Pallas kernels: none -> 27.9 us  [the longest x1 7.54 us: per_device(): call(rays_kernel, shaped((8, 320, 128), BF16), [SMEM, VMEM, VMEM], (pltpu...]
    gather x5 -> x0, local copies, waits for them, and re-layouts: 20 us -> none  [the longest x2 13.1 us: toeplitz(): picked = jnp.take(rows, jnp.clip(lagged, 0, count - 1), axis=-1)]
    all_to_all x1 -> x3, blocking collectives: 57.8 us -> 49.7 us  [the longest x1 20 us: per_device(): mine = lax.all_to_all(message, ('z', 'xh'), 0, 0, tiled=True)]
    split x1 -> x0, local copies, waits for them, and re-layouts: 7.97 us -> none  [side_by_side(): jnp.split(filled, [sum(widths[:k]) for k in range(1, len(widths))], axis=...]
    ppermute x2 -> x4, waiting for transfers between devices: 0.01 us -> 6.46 us  [the longest x1 2.76 us: per_device(): off_chip = lax.ppermute(off_chip, AXES, across)]
  transfers between devices with their start and end apart: 4 -> 5, of which waited for: 2 -> 3; matrix products, arithmetic and copies ran while one was open for 4% -> 1% of each run, Pallas kernels for 0% -> 7%
where the time goes in v1:
time: 101 us
  blocking collectives  49.7 us (49%)
  Pallas kernels  27.9 us (28%)
  starting transfers between devices  9.82 us (10%)
  waiting for transfers between devices  6.46 us (6%)
  local copies, waits for them, and re-layouts  2.9 us (3%)
  other arithmetic  2.36 us (2%)
  between operations  1.32 us (1%)
    all_to_all x1, blocking collectives, per_device(): mine = lax.all_to_all(message, ('z', 'xh'), 0, 0, tiled=True)  20 us
    all_to_all x1, blocking collectives, per_device(): partial = lax.all_to_all(partial, ('y', 'xl'), 0, 0, tiled=True)  16.5 us
    all_to_all x1, blocking collectives, per_device(): incoming = lax.all_to_all(incoming, ('y', 'xl'), 0, 0, tiled=True)  13.2 us
    pallas_call x1, Pallas kernels, per_device(): call(rays_kernel, shaped((8, 320, 128), BF16), [SMEM, VMEM, VMEM], (pltpu...  7.54 us
    pallas_call x1, Pallas kernels, per_device(): call(element_kernel, shaped((6, 64, 256), F32), [SMEM] * 2 + [VMEM] * 8)  6.91 us
    pallas_call x1, Pallas kernels, per_device(): call(image_kernel, (shaped((8, 64, 128), F32), shaped((8, 64, 128), F32))...  6.18 us
    ppermute x1, starting transfers between devices, per_device(): off_chip = lax.ppermute(off_chip, AXES, across)  6.06 us
    all_to_all x1, starting transfers between devices, per_device(): parts = lax.all_to_all(parts, ('z', 'xh'), 0, 0, tiled=True)  3.54 us
  transfers between devices with their start and end apart: 5, of which 3 were waited for; matrix products, arithmetic and copies ran while one was open for 1% of the time, Pallas kernels for 7%

profile of v1, /device:TPU:0, one launch (start us, length us, event | category | flops | bytes accessed | tf_op | source)
XLA Modules:
  0.0 100.5 jit_solution(16844284896995902439)
XLA Ops:
  1.3 0.7 pad_add_fusion.core_ref
  1.9 2.2 %shard_map.176 = (bf16[8,272,128]{2,1,0:T(8,128)(2,1)}, bf16[16,384]{1,0:T(8,128)(2,1)}, bf16[16,384]{1,0:T(8,128)(2,1)}) custom-call(s32[2]{0:T(128)} %pad_add_fusion.core_ref, s32[2,16]{1,0:T(2,128)} %send_ref.1, s32[1,1,16]{2,1,0:T(1,128)} %dest_ref.1, s32[1,1]{1,0:T(1,128)S(6)} %copy.21.count_ref, f32[6]{0:T(128)} %coef_ref.1, f32[6,64,256]{2,1,0:T(8,128)} %fields_ref.3, ...), custom_call_target="tpu_custom_call" | custom-call | tf_op jit(solution)/shard_map/pallas_call | solution.py:295
  4.2 20.0 %all_to_all.20.mine_ref = bf16[8,272,128]{2,1,0:T(8,128)(2,1)S(1)} all-to-all(bf16[8,272,128]{2,1,0:T(8,128)(2,1)} %get-tuple-element.7), channel_id=1, replica_groups=mesh['y'=4,'z'=4,'xl'=2,'xh'=2,'c'=2] {'z','xh'}, dimensions={0} | all-to-all | bytes 1114112 | tf_op jit(solution)/shard_map/all_to_all | solution.py:307
  24.2 0.0 copy-start
  24.2 0.0 collective-permute-start
  24.2 2.0 %collective-permute-done.other_ref = bf16[8,272,128]{2,1,0:T(8,128)(2,1)S(1)} collective-permute-done((bf16[8,272,128]{2,1,0:T(8,128)(2,1)S(1)}, bf16[8,272,128]{2,1,0:T(8,128)(2,1)S(1)}, u32[]{:S(2)}, u32[]{:S(2)}) %collective-permute-start) | collective-permute-done | bytes 557088 | tf_op jit(solution)/shard_map/ppermute | solution.py:308
  26.2 0.0 copy-done
  26.2 0.0 copy-start.1
  26.2 0.8 copy-done.1
  27.0 7.5 %shard_map.177 = bf16[8,320,128]{2,1,0:T(8,128)(2,1)} custom-call(s32[2]{0:T(128)} %pad_add_fusion.core_ref, bf16[8,272,128]{2,1,0:T(8,128)(2,1)} %copy-done, bf16[8,272,128]{2,1,0:T(8,128)(2,1)} %copy-done.1), custom_call_target="tpu_custom_call" | custom-call | tf_op jit(solution)/shard_map/pallas_call | solution.py:315
  34.5 16.5 %all_to_all.21.got_ref = bf16[8,320,128]{2,1,0:T(8,128)(2,1)} all-to-all(bf16[8,320,128]{2,1,0:T(8,128)(2,1)} %shard_map.177), channel_id=1, replica_groups=mesh['y'=4,'z'=4,'xl'=2,'xh'=2,'c'=2] {'y','xl'}, dimensions={0} | all-to-all | bytes 1310720 | tf_op jit(solution)/shard_map/all_to_all | solution.py:321
  51.0 2.5 %shard_map.178 = bf16[8,256,128]{2,1,0:T(8,128)(2,1)} custom-call(bf16[8,320,128]{2,1,0:T(8,128)(2,1)} %all_to_all.21.got_ref), custom_call_target="tpu_custom_call" | custom-call | tf_op jit(solution)/shard_map/pallas_call | solution.py:322
  53.5 13.2 %all_to_all.22.got_ref = bf16[8,256,128]{2,1,0:T(8,128)(2,1)} all-to-all(bf16[8,256,128]{2,1,0:T(8,128)(2,1)} %shard_map.178), channel_id=1, replica_groups=mesh['y'=4,'z'=4,'xl'=2,'xh'=2,'c'=2] {'y','xl'}, dimensions={0} | all-to-all | bytes 1048576 | tf_op jit(solution)/shard_map/all_to_all | solution.py:328
  66.8 6.2 %shard_map.179 = (f32[8,64,128]{2,1,0:T(8,128)}, f32[8,64,128]{2,1,0:T(8,128)}) custom-call(s32[2]{0:T(128)} %pad_add_fusion.core_ref, bf16[8,256,128]{2,1,0:T(8,128)(2,1)} %all_to_all.22.got_ref, bf16[8,272,128]{2,1,0:T(8,128)(2,1)} %copy-done, bf16[8,272,128]{2,1,0:T(8,128)(2,1)} %copy-done.1), custom_call_target="tpu_custom_call" | custom-call | tf_op jit(solution)/shard_map/pallas_call | solution.py:329
  73.0 0.0 collective-permute-start.1
  73.0 1.7 %collective-permute-done.1 = f32[8,64,128]{2,1,0:T(8,128)S(1)} collective-permute-done((f32[8,64,128]{2,1,0:T(8,128)}, f32[8,64,128]{2,1,0:T(8,128)S(1)}, u32[]{:S(2)}, u32[]{:S(2)}) %collective-permute-start.1) | collective-permute-done | bytes 262176 | tf_op jit(solution)/shard_map/ppermute | solution.py:335
  74.7 1.7 %add.3 = f32[8,64,128]{2,1,0:T(8,128)} add(f32[8,64,128]{2,1,0:T(8,128)} %get-tuple-element.8, f32[8,64,128]{2,1,0:T(8,128)S(1)} %collective-permute-done.1) | non-fusion elementwise | flops 65536 | bytes 786432 | tf_op jit(solution)/shard_map/add | solution.py:335
  76.4 0.0 copy-start.7
  76.4 0.0 copy-start.6
  76.4 0.0 copy-start.3
  76.4 3.5 %all-to-all-start.3 = ((f32[8,64,128]{2,1,0:T(8,128)}), f32[8,64,128]{2,1,0:T(8,128)S(1)}, u32[]{:S(2)}, u32[]{:S(2)}) async-start(f32[8,64,128]{2,1,0:T(8,128)} %add.3), calls=%async_computation.3 | async-start | bytes 524288 | tf_op jit(solution)/shard_map/all_to_all | solution.py:336
  80.0 0.0 copy-done.7
  80.0 0.2 collective-permute-start.2
  80.2 0.0 copy-done.6
  80.2 6.1 %collective-permute-start.3 = (bf16[16,384]{1,0:T(8,128)(2,1)S(1)}, bf16[16,384]{1,0:T(8,128)(2,1)S(1)}, u32[]{:S(2)}, u32[]{:S(2)}) collective-permute-start(bf16[16,384]{1,0:T(8,128)(2,1)S(1)} %copy-done.6), channel_id=1, source_target_pairs={{0,127},{1,2},{2,1},{3,4},{4,3},{5,6},{6,5},{7,8},{8,7},{9,10},{10... | collective-permute-start | bytes 36872 | tf_op jit(solution)/shard_map/ppermute | solution.py:305
  86.3 0.0 copy-done.3
  86.3 0.8 copy.19.lift_ref
  87.0 0.0 collective-permute-done.2.on_ref
  87.0 0.0 copy-start.4
  87.1 2.8 %collective-permute-done.3.off_ref = bf16[16,384]{1,0:T(8,128)(2,1)S(1)} collective-permute-done((bf16[16,384]{1,0:T(8,128)(2,1)S(1)}, bf16[16,384]{1,0:T(8,128)(2,1)S(1)}, u32[]{:S(2)}, u32[]{:S(2)}) %collective-permute-start.3) | collective-permute-done | bytes 12320 | tf_op jit(solution)/shard_map/ppermute | solution.py:305
  89.8 0.0 copy-start.5
  89.8 0.0 copy-done.4
  89.8 0.6 copy-done.5
  90.4 6.9 %shard_map.180.rate_ref = f32[6,64,256]{2,1,0:T(8,128)} custom-call(s32[2]{0:T(128)} %pad_add_fusion.core_ref, f32[6,6,6]{2,1,0:T(8,128)} %couple_ref.3, f32[6,64,256]{2,1,0:T(8,128)} %fields_ref.3, f32[1,256]{1,0:T(1,128)} %bitcast.4, f32[3,64,64]{2,1,0:T(8,128)} %diff_ref.1, f32[6,16,64]{2,1,0:T(8,128)} %interp_ref.3, f32[6,64,16]{2,1,0:T(8,128)} %copy.19.lift_ref, ...), custom_call_target="tpu_custom_call" | custom-call | tf_op jit(solution)/shard_map/pallas_call | solution.py:309
  97.3 0.0 all-to-all-done.3.parts_ref
  97.3 0.0 copy-start.2
  97.3 0.7 copy-done.2
  98.0 2.5 %shard_map.181 = (f32[6,64,256]{2,1,0:T(8,128)}, f32[64,128]{1,0:T(8,128)}) custom-call(f32[6]{0:T(128)} %bound_ref.1, f32[6,6,6]{2,1,0:T(8,128)} %couple_ref.3, f32[8,64,128]{2,1,0:T(8,128)} %copy-done.2, f32[6,64,256]{2,1,0:T(8,128)} %shard_map.180.rate_ref, f32[6,64,16]{2,1,0:T(8,128)} %copy.19.lift_ref, f32[1,64]{1,0:T(1,128)} %bitcast.5), custom_call_target="tpu_custom_call" | custom-call | tf_op jit(solution)/shard_map/pallas_call | solution.py:337
Async XLA Ops:
  24.2 2.0 %copy-start = (bf16[8,272,128]{2,1,0:T(8,128)(2,1)}, bf16[8,272,128]{2,1,0:T(8,128)(2,1)S(1)}, u32[]{:S(2)}) copy-start(bf16[8,272,128]{2,1,0:T(8,128)(2,1)S(1)} %all_to_all.20.mine_ref) | copy-start | bytes 1671172
  24.2 2.0 %collective-permute-start = (bf16[8,272,128]{2,1,0:T(8,128)(2,1)S(1)}, bf16[8,272,128]{2,1,0:T(8,128)(2,1)S(1)}, u32[]{:S(2)}, u32[]{:S(2)}) collective-permute-start(bf16[8,272,128]{2,1,0:T(8,128)(2,1)S(1)} %all_to_all.20.mine_ref), channel_id=1, source_target_pairs={{0,1},{1,0},{2,3},{3,2},{4,5},{5,4},{6,7},{7,6},{8,9},{9,8},{10,11... | collective-permute-start | bytes 1671176 | tf_op jit(solution)/shard_map/ppermute | solution.py:308
  26.2 0.8 copy-start.1
  73.0 1.7 %collective-permute-start.1 = (f32[8,64,128]{2,1,0:T(8,128)}, f32[8,64,128]{2,1,0:T(8,128)S(1)}, u32[]{:S(2)}, u32[]{:S(2)}) collective-permute-start(f32[8,64,128]{2,1,0:T(8,128)} %get-tuple-element.9), channel_id=1, source_target_pairs={{0,1},{1,0},{2,3},{3,2},{4,5},{5,4},{6,7},{7,6},{8,9},{9,8},{10,11... | collective-permute-start | bytes 786440 | tf_op jit(solution)/shard_map/ppermute | solution.py:335
  76.4 3.6 %copy-start.7 = (bf16[16,384]{1,0:T(8,128)(2,1)S(1)}, bf16[16,384]{1,0:T(8,128)(2,1)}, u32[]{:S(2)}) copy-start(bf16[16,384]{1,0:T(8,128)(2,1)} %get-tuple-element.10) | copy-start | bytes 36868
  76.4 3.8 %copy-start.6 = (bf16[16,384]{1,0:T(8,128)(2,1)S(1)}, bf16[16,384]{1,0:T(8,128)(2,1)}, u32[]{:S(2)}) copy-start(bf16[16,384]{1,0:T(8,128)(2,1)} %get-tuple-element.11) | copy-start | bytes 36868
  76.4 9.8 %copy-start.3 = (f32[6,64,16]{1,2,0:T(8,128)S(1)}, f32[6,64,16]{1,2,0:T(8,128)}, u32[]{:S(2)}) copy-start(f32[6,64,16]{1,2,0:T(8,128)} %param.21) | copy-start | bytes 73732
  76.4 20.9 %all-to-all-start.3 = ((f32[8,64,128]{2,1,0:T(8,128)}), f32[8,64,128]{2,1,0:T(8,128)S(1)}, u32[]{:S(2)}, u32[]{:S(2)}) async-start(f32[8,64,128]{2,1,0:T(8,128)} %add.3), calls=%async_computation.3 | async-start | bytes 524288 | tf_op jit(solution)/shard_map/all_to_all | solution.py:336
  80.0 7.1 %collective-permute-start.2 = (bf16[16,384]{1,0:T(8,128)(2,1)S(1)}, bf16[16,384]{1,0:T(8,128)(2,1)S(1)}, u32[]{:S(2)}, u32[]{:S(2)}) collective-permute-start(bf16[16,384]{1,0:T(8,128)(2,1)S(1)} %copy-done.7), channel_id=1, source_target_pairs={{0,1},{1,0},{2,3},{3,2},{4,5},{5,4},{6,7},{7,6},{8,9},{9,8},{10,11... | collective-permute-start | bytes 36872 | tf_op jit(solution)/shard_map/ppermute | solution.py:306
  80.2 9.6 %collective-permute-start.3 = (bf16[16,384]{1,0:T(8,128)(2,1)S(1)}, bf16[16,384]{1,0:T(8,128)(2,1)S(1)}, u32[]{:S(2)}, u32[]{:S(2)}) collective-permute-start(bf16[16,384]{1,0:T(8,128)(2,1)S(1)} %copy-done.6), channel_id=1, source_target_pairs={{0,127},{1,2},{2,1},{3,4},{4,3},{5,6},{6,5},{7,8},{8,7},{9,10},{10... | collective-permute-start | bytes 36872 | tf_op jit(solution)/shard_map/ppermute | solution.py:305
  87.0 2.8 %copy-start.4 = (bf16[16,384]{1,0:T(8,128)(2,1)}, bf16[16,384]{1,0:T(8,128)(2,1)S(1)}, u32[]{:S(2)}) copy-start(bf16[16,384]{1,0:T(8,128)(2,1)S(1)} %collective-permute-done.2.on_ref) | copy-start | bytes 36868
  89.8 0.6 copy-start.5
  97.3 0.7 copy-start.2

commit v2 on v1

--- a/solution.py
+++ b/solution.py
@@ -14,7 +14,7 @@
 AXES = ("y", "z", "xl", "xh", "c")
 VMEM = pl.BlockSpec(memory_space=pltpu.VMEM)
 SMEM = pl.BlockSpec(memory_space=pltpu.SMEM)
-ROW_C, ROW_W, ROW_T, ROWS = 128, 192, 256, 272
+ROW_C, ROW_W, ROW_T, ROWS = 256, 320, 352, 368
 NN = (((1,), (0,)), ((), ()))
 NT = (((1,), (1,)), ((), ()))
 TN = (((0,), (0,)), ((), ()))
@@ -53,11 +53,11 @@
 
 
 def pack_kernel(
-    core_ref, send_ref, dest_ref, count_ref, coef_ref,
+    place_ref, send_ref, dest_ref, count_ref, coef_ref,
     fields_ref, interp_ref, history_ref, weight_ref, projection_ref, kernels_ref,
     message_ref, on_ref, off_ref,
 ):
-    core = core_ref[0]
+    core = place_ref[0]
     elements = fields_ref.shape[2]
     flat = fields_ref[...].reshape(384, elements).astype(BF16)
 
@@ -101,41 +101,53 @@
         weights.append(mm(pick, weight_ref[...]).astype(BF16))
     for i in range(8):
         z, xh = i // 2, i % 2
-        message_ref[i, 0:128, :] = projection_ref[:, 128 * z : 128 * z + 128]
+        at = 256 * (z // 2)
+        message_ref[i, 0:128, :] = projection_ref[:, at : at + 128]
+        message_ref[i, 128:256, :] = projection_ref[:, at + 128 : at + 256]
         message_ref[i, ROW_C : ROW_C + 64, :] = currents
-        message_ref[i, ROW_W : ROW_W + 32, :] = weights[2 * xh]
-        message_ref[i, ROW_W + 32 : ROW_W + 64, :] = weights[2 * xh + 1]
+        message_ref[i, ROW_W : ROW_W + 32, :] = weights[2 * xh + z % 2]
         message_ref[i, ROW_T:ROWS, :] = table
 
 
-def own_weights(ref, i, core):
-    return ref[i, pl.ds(pl.multiple_of(ROW_W + 32 * core, 32), 32), :]
-
-
-def rays_kernel(core_ref, mine_ref, other_ref, out_ref, c_ref, w_ref, p_ref):
-    core = core_ref[0]
+def rays_kernel(place_ref, got_ref, keep_ref, send_ref, c_ref, w_ref, p_ref):
+    core, half = place_ref[0], place_ref[1]
+    mine = pl.multiple_of(128 * core, 128)
+    theirs = pl.multiple_of(128 * (1 - core), 128)
     for i in range(8):
-        for s, ref in ((0, mine_ref), (1, other_ref)):
-            at = 256 * i + 128 * s
-            c_ref[:, at : at + 128] = ref[i, ROW_C : ROW_C + 64, :].astype(F32)
-            w_ref[:, at : at + 128] = own_weights(ref, i, core).astype(F32)
-            p_ref[at : at + 128, :] = ref[i, 0:128, :]
+        at = 128 * i
+        c_ref[:, at : at + 128] = got_ref[i, ROW_C : ROW_C + 64, :].astype(F32)
+        w_ref[:, at : at + 128] = got_ref[i, ROW_W : ROW_W + 32, :].astype(F32)
+        p_ref[at : at + 128, 0:128] = got_ref[i, pl.ds(mine, 128), :]
+        p_ref[at : at + 128, 128:256] = got_ref[i, pl.ds(theirs, 128), :]
 
     def step(high, carry):
         c = c_ref[pl.ds(pl.multiple_of(8 * high, 8), 8), :]
         w = w_ref[...]
         rows = [(c[t : t + 1] * w).astype(BF16) for t in range(8)]
         product = mm(jnp.concatenate(rows, axis=0), p_ref[...])
-        parts = lane_blocks_swapped([product[32 * t : 32 * t + 32] for t in range(8)])
+        at = pl.multiple_of(32 * high, 32)
+        kept = lane_blocks_swapped([product[32 * t : 32 * t + 32, 0:128] for t in range(8)])
+        sent = lane_blocks_swapped([product[32 * t : 32 * t + 32, 128:256] for t in range(8)])
         for r in range(8):
-            out_ref[r, pl.ds(pl.multiple_of(32 * high, 32), 32), :] = parts[r].astype(BF16)
+            keep_ref[r, pl.ds(at, 32), :] = kept[r]
+            send_ref[r, pl.ds(at, 32), :] = sent[r].astype(BF16)
         return carry
 
     lax.fori_loop(0, 8, step, 0)
-    half = core_ref[1]
+    for z in range(4):
+        send_ref[z, 256:272, :] = got_ref[2 * z + half, ROW_T:ROWS, :]
+
+
+def joined_kernel(place_ref, keep_ref, send_ref, came_ref, out_ref):
+    has_tables = place_ref[0] == place_ref[2]
+    tables = []
+    for z in range(4):
+        here, there = send_ref[z, 256:272, :], came_ref[z, 256:272, :]
+        tables.append(jnp.where(has_tables, here.astype(F32), there.astype(F32)).astype(BF16))
+    tables = jnp.concatenate(tables, axis=0)
     for r in range(8):
-        for z in range(4):
-            out_ref[r, 256 + 16 * z : 272 + 16 * z, :] = mine_ref[2 * z + half, ROW_T:ROWS, :]
+        out_ref[r, 0:256, :] = (keep_ref[r] + came_ref[r, 0:256, :].astype(F32)).astype(BF16)
+        out_ref[r, 256:320, :] = tables
 
 
 def translate_kernel(got_ref, out_ref, h_ref, s_ref):
@@ -172,30 +184,37 @@
         out_ref[r] = incoming
 
 
-def image_kernel(core_ref, got_ref, mine_ref, other_ref, own_ref, partner_ref, rows_ref):
-    core = core_ref[0]
-    parts = lane_blocks_swapped([got_ref[r].astype(F32) for r in range(8)])
-    for t in range(8):
-        rows_ref[256 * t : 256 * t + 256, :] = parts[t].astype(BF16)
+def image_kernel(place_ref, here_ref, there_ref, got_ref, out_ref, rows_ref, p_ref):
+    core = place_ref[0]
+    mine = pl.multiple_of(128 * core, 128)
+    theirs = pl.multiple_of(128 * (1 - core), 128)
+    for h, ref in ((0, here_ref), (1, there_ref)):
+        parts = lane_blocks_swapped([ref[r].astype(F32) for r in range(8)])
+        for t in range(8):
+            rows_ref[256 * t : 256 * t + 256, 128 * h : 128 * h + 128] = parts[t].astype(BF16)
 
     def step(i, carry):
-        for ref, out in ((mine_ref, own_ref), (other_ref, partner_ref)):
-            image = mm(rows_ref[...], ref[i, 0:128, :], NT)
-            weight = own_weights(ref, i, core).astype(F32)
+        for s in range(2):
+            p_ref[128 * s : 128 * s + 128, 0:128] = got_ref[2 * i + s, pl.ds(mine, 128), :]
+            p_ref[128 * s : 128 * s + 128, 128:256] = got_ref[2 * i + s, pl.ds(theirs, 128), :]
+        image = mm(rows_ref[...], p_ref[...], NT)
+        for s in range(2):
+            weight = got_ref[2 * i + s, ROW_W : ROW_W + 32, :].astype(F32)
             weight = jnp.broadcast_to(weight[:, None, :], (32, 8, 128))
             for t in range(8):
-                block = image[256 * t : 256 * t + 256].reshape(32, 8, 128)
-                out[i, 8 * t : 8 * t + 8, :] = jnp.sum(block * weight, axis=0)
+                block = image[256 * t : 256 * t + 256, 128 * s : 128 * s + 128]
+                block = block.reshape(32, 8, 128) * weight
+                out_ref[2 * i + s, 8 * t : 8 * t + 8, :] = jnp.sum(block, axis=0)
         return carry
 
-    lax.fori_loop(0, 8, step, 0)
+    lax.fori_loop(0, 4, step, 0)
 
 
 def element_kernel(
-    core_ref, couple_ref, fields_ref, scale_ref, diff_ref, interp_ref, lift_ref, links_ref,
+    place_ref, couple_ref, fields_ref, scale_ref, diff_ref, interp_ref, lift_ref, links_ref,
     on_ref, off_ref, out_ref,
 ):
-    core = core_ref[0]
+    core = place_ref[0]
     elements = fields_ref.shape[2]
     interp = interp_ref[...].reshape(96, 64)
     diff = diff_ref[...].reshape(192, 64)
@@ -286,53 +305,63 @@
     return jax.ShapeDtypeStruct(shape, dtype)
 
 
+def vmem(shape, dtype):
+    return pltpu.VMEM(shape, dtype)
+
+
 def per_device(
     fields, inv_jacobian, diff_matrix, face_interp, lift_matrix, flux_couple, neighbours,
     send_index, bound_coef, current_coef, time_interp, current_history, group_weight, projection,
     kernels, pair_dest, pair_count,
 ):
-    place = jnp.stack([lax.axis_index("c"), lax.axis_index("xh")]).astype(jnp.int32)
+    place = jnp.stack([lax.axis_index("c"), lax.axis_index("xh"), lax.axis_index("z") % 2])
+    place = place.astype(jnp.int32)
     message, on_chip, off_chip = call(
         pack_kernel,
-        (shaped((8, ROWS, 128), BF16), shaped((16, 384), BF16), shaped((16, 384), BF16)),
+        (vmem((8, ROWS, 128), BF16), vmem((16, 384), BF16), vmem((16, 384), BF16)),
         [SMEM] * 5 + [VMEM] * 6,
     )(
         place, send_index, pair_dest, pair_count, current_coef,
         fields, face_interp, current_history, group_weight, projection, kernels,
     )
     devices = 128
+    beside = [(0, 1), (1, 0)]
     across = [(d, (d + 1 if d % 2 else d - 1) % devices) for d in range(devices)]
     off_chip = lax.ppermute(off_chip, AXES, across)
-    on_chip = lax.ppermute(on_chip, "c", [(0, 1), (1, 0)])
-    mine = lax.all_to_all(message, ("z", "xh"), 0, 0, tiled=True)
-    other = lax.ppermute(mine, "c", [(0, 1), (1, 0)])
+    on_chip = lax.ppermute(on_chip, "c", beside)
+    got = lax.all_to_all(message, ("z", "xh"), 0, 0, tiled=True)
+    got, off_chip, on_chip = lax.optimization_barrier((got, off_chip, on_chip))
     rate = call(
         element_kernel, shaped((6, 64, 256), F32), [SMEM] * 2 + [VMEM] * 8
     )(
         place, flux_couple, fields, inv_jacobian.reshape(1, -1), diff_matrix, face_interp,
         lift_matrix, neighbours, on_chip, off_chip,
     )
+    keep, send = call(
+        rays_kernel,
+        (vmem((8, 256, 128), F32), vmem((8, 272, 128), BF16)),
+        [SMEM, VMEM],
+        (pltpu.VMEM((64, 1024), F32), pltpu.VMEM((32, 1024), F32), pltpu.VMEM((1024, 256), BF16)),
+    )(place, got)
+    came = lax.ppermute(send, "c", beside)
     partial = call(
-        rays_kernel,
-        shaped((8, 320, 128), BF16),
-        [SMEM, VMEM, VMEM],
-        (pltpu.VMEM((64, 2048), F32), pltpu.VMEM((32, 2048), F32), pltpu.VMEM((2048, 128), BF16)),
-    )(place, mine, other)
+        joined_kernel, vmem((8, 320, 128), BF16), [SMEM, VMEM, VMEM, VMEM]
+    )(place, keep, send, came)
     partial = lax.all_to_all(partial, ("y", "xl"), 0, 0, tiled=True)
     incoming = call(
         translate_kernel,
-        shaped((8, 256, 128), BF16),
+        vmem((8, 256, 128), BF16),
         [VMEM],
         (pltpu.VMEM((2, 256, 128), F32), pltpu.VMEM((256, 128), F32)),
     )(partial)
     incoming = lax.all_to_all(incoming, ("y", "xl"), 0, 0, tiled=True)
-    own, partner = call(
+    beyond = lax.ppermute(incoming, "c", beside)
+    parts = call(
         image_kernel,
-        (shaped((8, 64, 128), F32), shaped((8, 64, 128), F32)),
+        vmem((8, 64, 128), F32),
         [SMEM, VMEM, VMEM, VMEM],
-        (pltpu.VMEM((2048, 128), BF16),),
-    )(place, incoming, mine, other)
-    parts = own + lax.ppermute(partner, "c", [(0, 1), (1, 0)])
+        (pltpu.VMEM((2048, 256), BF16), pltpu.VMEM((256, 256), BF16)),
+    )(place, incoming, beyond, got)
     parts = lax.all_to_all(parts, ("z", "xh"), 0, 0, tiled=True)
     return call(
         finish_kernel,

time: 101 us -> 94.3 us (0.934)
  blocking collectives: 49.7 us -> 27.4 us
  waiting for transfers between devices: 6.46 us -> 15.5 us
  starting transfers between devices: 9.82 us -> 18.1 us
  Pallas kernels: 27.9 us -> 25.6 us
  local copies, waits for them, and re-layouts: 2.9 us -> 4.99 us
  other arithmetic: 2.36 us -> 0.59 us
    all_to_all x1 -> x0, blocking collectives: 20 us -> none  [per_device(): mine = lax.all_to_all(message, ('z', 'xh'), 0, 0, tiled=True)]
    all_to_all x0 -> x1, starting transfers between devices: none -> 7.89 us  [per_device(): got = lax.all_to_all(message, ('z', 'xh'), 0, 0, tiled=True)]
    ppermute x1, waiting for transfers between devices: 2.76 us -> 10.1 us  [per_device(): off_chip = lax.ppermute(off_chip, AXES, across)]
    pallas_call x4 -> x5, Pallas kernels: 18.5 us -> 16.1 us  [the longest x1 5.42 us: per_device(): call(rays_kernel, (vmem((8, 256, 128), F32), vmem((8, 272, 128), BF16)),...]
    unnamed x17 -> x21, local copies, waits for them, and re-layouts: 2.9 us -> 4.99 us
    add x1 -> x0, other arithmetic: 1.69 us -> none  [per_device(): parts = own + lax.ppermute(partner, 'c', [(0, 1), (1, 0)])]
    all_to_all x1, waiting for transfers between devices: 0.01 us -> 1.59 us  [per_device(): parts = lax.all_to_all(parts, ('z', 'xh'), 0, 0, tiled=True)]
    all_to_all x1, blocking collectives: 16.5 us -> 15.3 us  [per_device(): partial = lax.all_to_all(partial, ('y', 'xl'), 0, 0, tiled=True)]
  transfers between devices with their start and end apart: 5 -> 6, of which waited for: 3 -> 4; matrix products, arithmetic and copies ran while one was open for 1% -> 1% of each run, Pallas kernels for 7% -> 7%
where the time goes in v2:
time: 94.3 us; the launch traced here: 93.5 us
  blocking collectives  27.4 us (29%)
  Pallas kernels  25.6 us (27%)
  starting transfers between devices  18.1 us (19%)
  waiting for transfers between devices  15.5 us (16%)
  local copies, waits for them, and re-layouts  4.99 us (5%)
  between operations  1.38 us (1%)
    all_to_all x1, blocking collectives, per_device(): partial = lax.all_to_all(partial, ('y', 'xl'), 0, 0, tiled=True)  15.3 us
    all_to_all x1, blocking collectives, per_device(): incoming = lax.all_to_all(incoming, ('y', 'xl'), 0, 0, tiled=True)  12.1 us
    ppermute x1, waiting for transfers between devices, per_device(): off_chip = lax.ppermute(off_chip, AXES, across)  10.1 us
    all_to_all x1, starting transfers between devices, per_device(): got = lax.all_to_all(message, ('z', 'xh'), 0, 0, tiled=True)  7.89 us
    pallas_call x1, Pallas kernels, per_device(): call(element_kernel, shaped((6, 64, 256), F32), [SMEM] * 2 + [VMEM] * 8)  6.91 us
    ppermute x1, starting transfers between devices, per_device(): off_chip = lax.ppermute(off_chip, AXES, across)  6.7 us
    pallas_call x1, Pallas kernels, per_device(): call(rays_kernel, (vmem((8, 256, 128), F32), vmem((8, 272, 128), BF16)),...  5.42 us
    pallas_call x1, Pallas kernels, per_device(): call(image_kernel, vmem((8, 64, 128), F32), [SMEM, VMEM, VMEM, VMEM], (pl...  5 us
  transfers between devices with their start and end apart: 6, of which 4 were waited for; matrix products, arithmetic and copies ran while one was open for 1% of the time, Pallas kernels for 7%

profile of v2, /device:TPU:0, one launch (start us, length us, event | category | flops | bytes accessed | tf_op | source)
XLA Modules:
  0.0 93.5 jit_solution(7636654254893278233)
XLA Ops:
  1.3 0.6 pad_add_fusion.place_ref
  1.9 2.3 %shard_map.176 = (bf16[8,368,128]{2,1,0:T(8,128)(2,1)}, bf16[16,384]{1,0:T(8,128)(2,1)S(1)}, bf16[16,384]{1,0:T(8,128)(2,1)S(1)}) custom-call(s32[3]{0:T(128)} %pad_add_fusion.place_ref, s32[2,16]{1,0:T(2,128)} %send_ref.1, s32[1,1,16]{2,1,0:T(1,128)} %dest_ref.1, s32[1,1]{1,0:T(1,128)S(6)} %copy.21.count_ref, f32[6]{0:T(128)} %coef_ref.1, ...), custom_call_target="tpu_custom_call" | custom-call | tf_op jit(solution)/shard_map/pallas_call | solution.py:319
  4.2 7.9 %all-to-all-start = ((bf16[8,368,128]{2,1,0:T(8,128)(2,1)}), bf16[8,368,128]{2,1,0:T(8,128)(2,1)S(1)}, u32[]{:S(2)}, u32[]{:S(2)}) async-start(bf16[8,368,128]{2,1,0:T(8,128)(2,1)} %get-tuple-element.10), calls=%async_computation | async-start | bytes 1507328 | tf_op jit(solution)/shard_map/all_to_all | solution.py:332
  12.1 6.7 %collective-permute-start = (bf16[16,384]{1,0:T(8,128)(2,1)S(1)}, bf16[16,384]{1,0:T(8,128)(2,1)S(1)}, u32[]{:S(2)}, u32[]{:S(2)}) collective-permute-start(bf16[16,384]{1,0:T(8,128)(2,1)S(1)} %get-tuple-element.11), channel_id=1, source_target_pairs={{0,127},{1,2},{2,1},{3,4},{4,3},{5,6},{6,5},{7,8},{8,7},{9,10},{10... | collective-permute-start | bytes 36872 | tf_op jit(solution)/shard_map/ppermute | solution.py:330
  18.8 0.0 collective-permute-start.1
  18.8 10.1 %collective-permute-done.off_ref = bf16[16,384]{1,0:T(8,128)(2,1)S(1)} collective-permute-done((bf16[16,384]{1,0:T(8,128)(2,1)S(1)}, bf16[16,384]{1,0:T(8,128)(2,1)S(1)}, u32[]{:S(2)}, u32[]{:S(2)}) %collective-permute-start) | collective-permute-done | bytes 12320 | tf_op jit(solution)/shard_map/ppermute | solution.py:330
  28.9 0.0 copy-start.8
  28.9 0.0 collective-permute-done.1.on_ref
  28.9 0.0 copy-start.9
  28.9 0.0 all-to-all-done.got_ref
  28.9 0.0 copy-start.2
  28.9 0.9 copy-done.2
  29.8 5.4 %shard_map.177 = (f32[8,256,128]{2,1,0:T(8,128)S(1)}, bf16[8,272,128]{2,1,0:T(8,128)(2,1)S(1)}) custom-call(s32[3]{0:T(128)} %pad_add_fusion.place_ref, bf16[8,368,128]{2,1,0:T(8,128)(2,1)} %copy-done.2), custom_call_target="tpu_custom_call" | custom-call | tf_op jit(solution)/shard_map/pallas_call | solution.py:340
  35.2 0.0 copy-done.8
  35.2 0.0 copy-done.9
  35.2 0.0 copy-start
  35.2 1.0 %copy-done = f32[8,256,128]{2,1,0:T(8,128)} copy-done((f32[8,256,128]{2,1,0:T(8,128)}, f32[8,256,128]{2,1,0:T(8,128)S(1)}, u32[]{:S(2)}) %copy-start) | copy-done | bytes 1048600
  36.2 0.0 copy-start.1
  36.2 0.0 collective-permute-start.2
  36.2 2.0 %collective-permute-done.2.came_ref = bf16[8,272,128]{2,1,0:T(8,128)(2,1)S(1)} collective-permute-done((bf16[8,272,128]{2,1,0:T(8,128)(2,1)S(1)}, bf16[8,272,128]{2,1,0:T(8,128)(2,1)S(1)}, u32[]{:S(2)}, u32[]{:S(2)}) %collective-permute-start.2) | collective-permute-done | bytes 557088 | tf_op jit(solution)/shard_map/ppermute | solution.py:346
  38.2 0.0 copy-start.5
  38.2 0.0 copy-done.1
  38.2 0.8 copy-done.5
  39.0 1.6 %shard_map.178 = bf16[8,320,128]{2,1,0:T(8,128)(2,1)S(1)} custom-call(s32[3]{0:T(128)} %pad_add_fusion.place_ref, f32[8,256,128]{2,1,0:T(8,128)} %copy-done, bf16[8,272,128]{2,1,0:T(8,128)(2,1)} %copy-done.1, bf16[8,272,128]{2,1,0:T(8,128)(2,1)} %copy-done.5), custom_call_target="tpu_custom_call" | custom-call | tf_op jit(solution)/shard_map/pallas_call | solution.py:347
  40.6 15.3 %all_to_all.20.got_ref = bf16[8,320,128]{2,1,0:T(8,128)(2,1)} all-to-all(bf16[8,320,128]{2,1,0:T(8,128)(2,1)S(1)} %shard_map.178), channel_id=1, replica_groups=mesh['y'=4,'z'=4,'xl'=2,'xh'=2,'c'=2] {'y','xl'}, dimensions={0} | all-to-all | bytes 1310720 | tf_op jit(solution)/shard_map/all_to_all | solution.py:350
  55.9 1.7 %shard_map.179 = bf16[8,256,128]{2,1,0:T(8,128)(2,1)S(1)} custom-call(bf16[8,320,128]{2,1,0:T(8,128)(2,1)} %all_to_all.20.got_ref), custom_call_target="tpu_custom_call" | custom-call | tf_op jit(solution)/shard_map/pallas_call | solution.py:351
  57.6 12.1 %all_to_all.21.here_ref = bf16[8,256,128]{2,1,0:T(8,128)(2,1)S(1)} all-to-all(bf16[8,256,128]{2,1,0:T(8,128)(2,1)S(1)} %shard_map.179), channel_id=1, replica_groups=mesh['y'=4,'z'=4,'xl'=2,'xh'=2,'c'=2] {'y','xl'}, dimensions={0} | all-to-all | bytes 1048576 | tf_op jit(solution)/shard_map/all_to_all | solution.py:357
  69.8 0.0 copy-start.3
  69.8 0.0 collective-permute-start.3
  69.8 1.9 %collective-permute-done.3.there_ref = bf16[8,256,128]{2,1,0:T(8,128)(2,1)S(1)} collective-permute-done((bf16[8,256,128]{2,1,0:T(8,128)(2,1)S(1)}, bf16[8,256,128]{2,1,0:T(8,128)(2,1)S(1)}, u32[]{:S(2)}, u32[]{:S(2)}) %collective-permute-start.3) | collective-permute-done | bytes 524320 | tf_op jit(solution)/shard_map/ppermute | solution.py:358
  71.7 0.0 copy-done.3
  71.7 0.0 copy-start.6
  71.7 0.8 copy-done.6
  72.5 5.0 %shard_map.180 = f32[8,64,128]{2,1,0:T(8,128)} custom-call(s32[3]{0:T(128)} %pad_add_fusion.place_ref, bf16[8,256,128]{2,1,0:T(8,128)(2,1)} %copy-done.3, bf16[8,256,128]{2,1,0:T(8,128)(2,1)} %copy-done.6, bf16[8,368,128]{2,1,0:T(8,128)(2,1)} %copy-done.2), custom_call_target="tpu_custom_call" | custom-call | tf_op jit(solution)/shard_map/pallas_call | solution.py:359
  77.5 0.0 copy-start.7
  77.5 3.5 %all-to-all-start.3 = ((f32[8,64,128]{2,1,0:T(8,128)}), f32[8,64,128]{2,1,0:T(8,128)S(1)}, u32[]{:S(2)}, u32[]{:S(2)}) async-start(f32[8,64,128]{2,1,0:T(8,128)} %shard_map.180), calls=%async_computation.3 | async-start | bytes 524288 | tf_op jit(solution)/shard_map/all_to_all | solution.py:365
  81.0 0.0 copy-done.7
  81.0 0.8 copy.19.lift_ref
  81.8 6.9 %shard_map.181.rate_ref = f32[6,64,256]{2,1,0:T(8,128)} custom-call(s32[3]{0:T(128)} %pad_add_fusion.place_ref, f32[6,6,6]{2,1,0:T(8,128)} %couple_ref.3, f32[6,64,256]{2,1,0:T(8,128)} %fields_ref.3, f32[1,256]{1,0:T(1,128)} %bitcast.5, f32[3,64,64]{2,1,0:T(8,128)} %diff_ref.1, f32[6,16,64]{2,1,0:T(8,128)} %interp_ref.3, f32[6,64,16]{2,1,0:T(8,128)} %copy.19.lift_ref, ...), custom_call_target="tpu_custom_call" | custom-call | tf_op jit(solution)/shard_map/pallas_call | solution.py:334
  88.7 1.6 %all-to-all-done.3.parts_ref = f32[8,64,128]{2,1,0:T(8,128)S(1)} async-done(((f32[8,64,128]{2,1,0:T(8,128)}), f32[8,64,128]{2,1,0:T(8,128)S(1)}, u32[]{:S(2)}, u32[]{:S(2)}) %all-to-all-start.3) | async-done | bytes 262176 | tf_op jit(solution)/shard_map/all_to_all | solution.py:365
  90.3 0.0 copy-start.4
  90.3 0.7 copy-done.4
  91.0 2.5 %shard_map.182 = (f32[6,64,256]{2,1,0:T(8,128)}, f32[64,128]{1,0:T(8,128)}) custom-call(f32[6]{0:T(128)} %bound_ref.1, f32[6,6,6]{2,1,0:T(8,128)} %couple_ref.3, f32[8,64,128]{2,1,0:T(8,128)} %copy-done.4, f32[6,64,256]{2,1,0:T(8,128)} %shard_map.181.rate_ref, f32[6,64,16]{2,1,0:T(8,128)} %copy.19.lift_ref, f32[1,64]{1,0:T(1,128)} %bitcast.6), custom_call_target="tpu_custom_call" | custom-call | tf_op jit(solution)/shard_map/pallas_call | solution.py:366
Async XLA Ops:
  4.2 24.7 %all-to-all-start = ((bf16[8,368,128]{2,1,0:T(8,128)(2,1)}), bf16[8,368,128]{2,1,0:T(8,128)(2,1)S(1)}, u32[]{:S(2)}, u32[]{:S(2)}) async-start(bf16[8,368,128]{2,1,0:T(8,128)(2,1)} %get-tuple-element.10), calls=%async_computation | async-start | bytes 1507328 | tf_op jit(solution)/shard_map/all_to_all | solution.py:332
  12.1 16.8 %collective-permute-start = (bf16[16,384]{1,0:T(8,128)(2,1)S(1)}, bf16[16,384]{1,0:T(8,128)(2,1)S(1)}, u32[]{:S(2)}, u32[]{:S(2)}) collective-permute-start(bf16[16,384]{1,0:T(8,128)(2,1)S(1)} %get-tuple-element.11), channel_id=1, source_target_pairs={{0,127},{1,2},{2,1},{3,4},{4,3},{5,6},{6,5},{7,8},{8,7},{9,10},{10... | collective-permute-start | bytes 36872 | tf_op jit(solution)/shard_map/ppermute | solution.py:330
  18.8 10.1 %collective-permute-start.1 = (bf16[16,384]{1,0:T(8,128)(2,1)S(1)}, bf16[16,384]{1,0:T(8,128)(2,1)S(1)}, u32[]{:S(2)}, u32[]{:S(2)}) collective-permute-start(bf16[16,384]{1,0:T(8,128)(2,1)S(1)} %get-tuple-element.12), channel_id=1, source_target_pairs={{0,1},{1,0},{2,3},{3,2},{4,5},{5,4},{6,7},{7,6},{8,9},{9,8},{10,11... | collective-permute-start | bytes 36872 | tf_op jit(solution)/shard_map/ppermute | solution.py:331
  28.9 6.4 %copy-start.8 = (bf16[16,384]{1,0:T(8,128)(2,1)}, bf16[16,384]{1,0:T(8,128)(2,1)S(1)}, u32[]{:S(2)}) copy-start(bf16[16,384]{1,0:T(8,128)(2,1)S(1)} %collective-permute-done.off_ref) | copy-start | bytes 36868
  28.9 6.4 %copy-start.9 = (bf16[16,384]{1,0:T(8,128)(2,1)}, bf16[16,384]{1,0:T(8,128)(2,1)S(1)}, u32[]{:S(2)}) copy-start(bf16[16,384]{1,0:T(8,128)(2,1)S(1)} %collective-permute-done.1.on_ref) | copy-start | bytes 36868
  28.9 0.9 copy-start.2
  35.2 1.0 %copy-start = (f32[8,256,128]{2,1,0:T(8,128)}, f32[8,256,128]{2,1,0:T(8,128)S(1)}, u32[]{:S(2)}) copy-start(f32[8,256,128]{2,1,0:T(8,128)S(1)} %get-tuple-element.14.keep_ref) | copy-start | bytes 3145732
  36.2 2.0 %copy-start.1 = (bf16[8,272,128]{2,1,0:T(8,128)(2,1)}, bf16[8,272,128]{2,1,0:T(8,128)(2,1)S(1)}, u32[]{:S(2)}) copy-start(bf16[8,272,128]{2,1,0:T(8,128)(2,1)S(1)} %get-tuple-element.15.send_ref) | copy-start | bytes 1671172
  36.2 2.0 %collective-permute-start.2 = (bf16[8,272,128]{2,1,0:T(8,128)(2,1)S(1)}, bf16[8,272,128]{2,1,0:T(8,128)(2,1)S(1)}, u32[]{:S(2)}, u32[]{:S(2)}) collective-permute-start(bf16[8,272,128]{2,1,0:T(8,128)(2,1)S(1)} %get-tuple-element.15.send_ref), channel_id=1, source_target_pairs={{0,1},{1,0},{2,3},{3,2},{4,5},{5,4},{6,7},{7,6},{8,9},{9,8},{10,11... | collective-permute-start | bytes 1671176 | tf_op jit(solution)/shard_map/ppermute | solution.py:346
  38.2 0.8 copy-start.5
  69.8 1.9 %copy-start.3 = (bf16[8,256,128]{2,1,0:T(8,128)(2,1)}, bf16[8,256,128]{2,1,0:T(8,128)(2,1)S(1)}, u32[]{:S(2)}) copy-start(bf16[8,256,128]{2,1,0:T(8,128)(2,1)S(1)} %all_to_all.21.here_ref) | copy-start | bytes 1572868
  69.8 1.9 %collective-permute-start.3 = (bf16[8,256,128]{2,1,0:T(8,128)(2,1)S(1)}, bf16[8,256,128]{2,1,0:T(8,128)(2,1)S(1)}, u32[]{:S(2)}, u32[]{:S(2)}) collective-permute-start(bf16[8,256,128]{2,1,0:T(8,128)(2,1)S(1)} %all_to_all.21.here_ref), channel_id=1, source_target_pairs={{0,1},{1,0},{2,3},{3,2},{4,5},{5,4},{6,7},{7,6},{8,9},{9,8},{10,11... | collective-permute-start | bytes 1572872 | tf_op jit(solution)/shard_map/ppermute | solution.py:358
  71.7 0.8 copy-start.6
  77.5 3.6 %copy-start.7 = (f32[6,64,16]{1,2,0:T(8,128)S(1)}, f32[6,64,16]{1,2,0:T(8,128)}, u32[]{:S(2)}) copy-start(f32[6,64,16]{1,2,0:T(8,128)} %param.21) | copy-start | bytes 73732
  77.5 12.8 %all-to-all-start.3 = ((f32[8,64,128]{2,1,0:T(8,128)}), f32[8,64,128]{2,1,0:T(8,128)S(1)}, u32[]{:S(2)}, u32[]{:S(2)}) async-start(f32[8,64,128]{2,1,0:T(8,128)} %shard_map.180), calls=%async_computation.3 | async-start | bytes 524288 | tf_op jit(solution)/shard_map/all_to_all | solution.py:365
  90.3 0.7 copy-start.4

commit v3 on v2

--- a/solution.py
+++ b/solution.py
@@ -212,7 +212,7 @@
 
 def element_kernel(
     place_ref, couple_ref, fields_ref, scale_ref, diff_ref, interp_ref, lift_ref, links_ref,
-    on_ref, off_ref, out_ref,
+    on_ref, off_ref, out_ref, first_ref,
 ):
     core = place_ref[0]
     elements = fields_ref.shape[2]
@@ -250,7 +250,7 @@
             flux = couple_ref[f, c, 0] * jumps[0]
             for k in range(1, 6):
                 flux = flux + couple_ref[f, c, k] * jumps[k]
-            surface[c] = surface[c] + mm(lift_ref[f], flux, NN, HIGH)
+            surface[c] = surface[c] + mm(lift_ref[f], flux, TN, HIGH)
 
     def grad(r, c):
         return grads[c][64 * r : 64 * r + 64]
@@ -265,12 +265,16 @@
     )
     scale = scale_ref[...]
     for c in range(6):
-        out_ref[c] = curls[c] * scale + surface[c]
+        value = curls[c] * scale + surface[c]
+        out_ref[c] = value
+        first_ref[c] = value[:, 0:128]
 
 
 def finish_kernel(
-    bound_ref, couple_ref, parts_ref, rate_ref, lift_ref, time_ref, rate_out, field_out,
+    bound_ref, couple_ref, parts_ref, first_ref, lift_ref, time_ref, rate_ref, rate_out,
+    field_out, tile_ref, sem,
 ):
+    del rate_ref
     total = parts_ref[0]
     for i in range(1, 8):
         total = total + parts_ref[i]
@@ -281,24 +285,31 @@
     node = iota((16, 128), 1) % 16 == iota((16, 128), 0)
     by_node = jnp.where(node, now, 0.0)
     collect = one_hot(iota((128, 128), 0) // 16 == iota((128, 128), 1))
-    lifted = mm(lift_ref[5], mm(by_node, collect, NN, HIGH), NN, HIGH)
+    lifted = mm(lift_ref[5], mm(by_node, collect, NN, HIGH), TN, HIGH)
     for c in range(6):
         factor = couple_ref[5, c, 0] * bound_ref[0]
         for k in range(1, 6):
             factor = factor + couple_ref[5, c, k] * bound_ref[k]
-        rate_out[c, :, 0:128] = rate_ref[c, :, 0:128] + factor * lifted
-        rate_out[c, :, 128:256] = rate_ref[c, :, 128:256]
-
-
-def call(kernel, out, in_specs, scratch=(), **options):
-    return pl.pallas_call(
+        tile_ref[c] = first_ref[c] + factor * lifted
+    copy = pltpu.make_async_copy(tile_ref, rate_out.at[:, :, pl.ds(0, 128)], sem)
+    copy.start()
+    copy.wait()
+
+
+def call(kernel, out, in_specs, scratch=(), out_specs=None, **options):
+    run = pl.pallas_call(
         kernel,
         out_shape=out,
         in_specs=in_specs,
-        out_specs=jax.tree.map(lambda _: VMEM, out),
+        out_specs=jax.tree.map(lambda _: VMEM, out) if out_specs is None else out_specs,
         scratch_shapes=list(scratch),
         **options,
     )
+    return run
+
+
+def held(x):
+    return pltpu.with_memory_space_constraint(x, pltpu.VMEM)
 
 
 def shaped(shape, dtype):
@@ -331,12 +342,7 @@
     on_chip = lax.ppermute(on_chip, "c", beside)
     got = lax.all_to_all(message, ("z", "xh"), 0, 0, tiled=True)
     got, off_chip, on_chip = lax.optimization_barrier((got, off_chip, on_chip))
-    rate = call(
-        element_kernel, shaped((6, 64, 256), F32), [SMEM] * 2 + [VMEM] * 8
-    )(
-        place, flux_couple, fields, inv_jacobian.reshape(1, -1), diff_matrix, face_interp,
-        lift_matrix, neighbours, on_chip, off_chip,
-    )
+    got = held(got)
     keep, send = call(
         rays_kernel,
         (vmem((8, 256, 128), F32), vmem((8, 272, 128), BF16)),
@@ -346,14 +352,25 @@
     came = lax.ppermute(send, "c", beside)
     partial = call(
         joined_kernel, vmem((8, 320, 128), BF16), [SMEM, VMEM, VMEM, VMEM]
-    )(place, keep, send, came)
+    )(place, held(keep), held(send), held(came))
+    partial, on_chip, off_chip = lax.optimization_barrier((partial, on_chip, off_chip))
+    lift = lift_matrix.transpose(0, 2, 1)
+    rate, first = call(
+        element_kernel,
+        (shaped((6, 64, 256), F32), vmem((6, 64, 128), F32)),
+        [SMEM] * 2 + [VMEM] * 8,
+    )(
+        place, flux_couple, fields, inv_jacobian.reshape(1, -1), diff_matrix, face_interp,
+        lift, neighbours, held(on_chip), held(off_chip),
+    )
     partial = lax.all_to_all(partial, ("y", "xl"), 0, 0, tiled=True)
+    partial, rate, first = lax.optimization_barrier((partial, rate, first))
     incoming = call(
         translate_kernel,
         vmem((8, 256, 128), BF16),
         [VMEM],
         (pltpu.VMEM((2, 256, 128), F32), pltpu.VMEM((256, 128), F32)),
-    )(partial)
+    )(held(partial))
     incoming = lax.all_to_all(incoming, ("y", "xl"), 0, 0, tiled=True)
     beyond = lax.ppermute(incoming, "c", beside)
     parts = call(
@@ -361,13 +378,17 @@
         vmem((8, 64, 128), F32),
         [SMEM, VMEM, VMEM, VMEM],
         (pltpu.VMEM((2048, 256), BF16), pltpu.VMEM((256, 256), BF16)),
-    )(place, incoming, beyond, got)
+    )(place, held(incoming), held(beyond), got)
     parts = lax.all_to_all(parts, ("z", "xh"), 0, 0, tiled=True)
+    anywhere = pl.BlockSpec(memory_space=pl.ANY)
     return call(
         finish_kernel,
         (shaped((6, 64, 256), F32), shaped((64, 128), F32)),
-        [SMEM] * 2 + [VMEM] * 4,
-    )(bound_coef, flux_couple, parts, rate, lift_matrix, time_interp.reshape(1, -1))
+        [SMEM] * 2 + [VMEM] * 4 + [anywhere],
+        (pltpu.VMEM((6, 64, 128), F32), pltpu.SemaphoreType.DMA),
+        out_specs=(anywhere, VMEM),
+        input_output_aliases={6: 0},
+    )(bound_coef, flux_couple, held(parts), held(first), lift, time_interp.reshape(1, -1), rate)
 
 
 def solution(mesh):

time: 94.3 us -> 88.3 us (0.936)
  local copies, waits for them, and re-layouts: 4.99 us -> 0.86 us
  waiting for transfers between devices: 15.5 us -> 19 us
  Pallas kernels: 25.6 us -> 22.9 us
  blocking collectives: 27.4 us -> 24.7 us
    unnamed x21 -> x4, local copies, waits for them, and re-layouts: 4.99 us -> 0.86 us
    all_to_all x1, waiting for transfers between devices: 1.59 us -> 5.12 us  [per_device(): partial = lax.all_to_all(partial, ('y', 'xl'), 0, 0, tiled=True)]
    all_to_all x1, blocking collectives: 15.3 us -> 11.8 us  [per_device(): parts = lax.all_to_all(parts, ('z', 'xh'), 0, 0, tiled=True)]
    pallas_call x1, Pallas kernels: 5 us -> 3.51 us  [per_device(): call(image_kernel, vmem((8, 64, 128), F32), [SMEM, VMEM, VMEM, VMEM], (pl...]
    pallas_call x1, Pallas kernels: 1.74 us -> 0.66 us  [per_device(): call(translate_kernel, vmem((8, 256, 128), BF16), [VMEM], (pltpu.VMEM((2,...]
  transfers between devices with their start and end apart: 6 -> 6, of which waited for: 4 -> 4; matrix products, arithmetic and copies ran while one was open for 1% -> 0% of each run, Pallas kernels for 7% -> 8%
where the time goes in v3:
time: 88.3 us; the launch traced here: 87.6 us
  blocking collectives  24.7 us (28%)
  Pallas kernels  22.9 us (26%)
  waiting for transfers between devices  19 us (22%)
  starting transfers between devices  18.1 us (20%)
  between operations  1.34 us (2%)
    all_to_all x1, blocking collectives, per_device(): incoming = lax.all_to_all(incoming, ('y', 'xl'), 0, 0, tiled=True)  12.9 us
    all_to_all x1, blocking collectives, per_device(): parts = lax.all_to_all(parts, ('z', 'xh'), 0, 0, tiled=True)  11.8 us
    ppermute x1, waiting for transfers between devices, per_device(): off_chip = lax.ppermute(off_chip, AXES, across)  10.1 us
    all_to_all x1, starting transfers between devices, per_device(): got = lax.all_to_all(message, ('z', 'xh'), 0, 0, tiled=True)  7.89 us
    pallas_call x1, Pallas kernels, per_device(): call(element_kernel, (shaped((6, 64, 256), F32), vmem((6, 64, 128), F32))...  6.92 us
    ppermute x1, starting transfers between devices, per_device(): off_chip = lax.ppermute(off_chip, AXES, across)  6.7 us
    all_to_all x1, waiting for transfers between devices, per_device(): partial = lax.all_to_all(partial, ('y', 'xl'), 0, 0, tiled=True)  5.12 us
    pallas_call x1, Pallas kernels, per_device(): call(rays_kernel, (vmem((8, 256, 128), F32), vmem((8, 272, 128), BF16)),...  4.95 us
  transfers between devices with their start and end apart: 6, of which 4 were waited for; matrix products, arithmetic and copies ran while one was open for 0% of the time, Pallas kernels for 8%

profile of v3, /device:TPU:0, one launch (start us, length us, event | category | flops | bytes accessed | tf_op | source)
XLA Modules:
  0.0 87.6 jit_solution(5513788333032660649)
XLA Ops:
  1.3 0.7 pad_add_fusion.place_ref
  1.9 2.3 %shard_map.176 = (bf16[8,368,128]{2,1,0:T(8,128)(2,1)}, bf16[16,384]{1,0:T(8,128)(2,1)S(1)}, bf16[16,384]{1,0:T(8,128)(2,1)S(1)}) custom-call(s32[3]{0:T(128)} %pad_add_fusion.place_ref, s32[2,16]{1,0:T(2,128)} %send_ref.1, s32[1,1,16]{2,1,0:T(1,128)} %dest_ref.1, s32[1,1]{1,0:T(1,128)S(6)} %copy.21.count_ref, f32[6]{0:T(128)} %coef_ref.1, ...), custom_call_target="tpu_custom_call" | custom-call | tf_op jit(solution)/shard_map/pallas_call | solution.py:330
  4.3 7.9 %all-to-all-start = ((bf16[8,368,128]{2,1,0:T(8,128)(2,1)}), bf16[8,368,128]{2,1,0:T(8,128)(2,1)S(1)}, u32[]{:S(2)}, u32[]{:S(2)}) async-start(bf16[8,368,128]{2,1,0:T(8,128)(2,1)} %get-tuple-element.18), calls=%async_computation | async-start | bytes 1507328 | tf_op jit(solution)/shard_map/all_to_all | solution.py:343
  12.1 6.7 %collective-permute-start = (bf16[16,384]{1,0:T(8,128)(2,1)S(1)}, bf16[16,384]{1,0:T(8,128)(2,1)S(1)}, u32[]{:S(2)}, u32[]{:S(2)}) collective-permute-start(bf16[16,384]{1,0:T(8,128)(2,1)S(1)} %get-tuple-element.19), channel_id=1, source_target_pairs={{0,127},{1,2},{2,1},{3,4},{4,3},{5,6},{6,5},{7,8},{8,7},{9,10},{10... | collective-permute-start | bytes 36872 | tf_op jit(solution)/shard_map/ppermute | solution.py:341
  18.8 0.0 collective-permute-start.1
  18.8 10.1 %collective-permute-done.off_ref = bf16[16,384]{1,0:T(8,128)(2,1)S(1)} collective-permute-done((bf16[16,384]{1,0:T(8,128)(2,1)S(1)}, bf16[16,384]{1,0:T(8,128)(2,1)S(1)}, u32[]{:S(2)}, u32[]{:S(2)}) %collective-permute-start) | collective-permute-done | bytes 12320 | tf_op jit(solution)/shard_map/ppermute | solution.py:341
  28.9 0.0 collective-permute-done.1.on_ref
  28.9 0.0 all-to-all-done.got_ref
  28.9 4.9 %shard_map.177 = (f32[8,256,128]{2,1,0:T(8,128)S(1)}, bf16[8,272,128]{2,1,0:T(8,128)(2,1)S(1)}) custom-call(s32[3]{0:T(128)} %pad_add_fusion.place_ref, bf16[8,368,128]{2,1,0:T(8,128)(2,1)S(1)} %all-to-all-done.got_ref), custom_call_target="tpu_custom_call" | custom-call | tf_op jit(solution)/shard_map/pallas_call | solution.py:346
  33.9 0.0 copy-start
  33.9 0.9 copy-done
  34.7 0.0 collective-permute-start.2
  34.7 2.0 %collective-permute-done.2.came_ref = bf16[8,272,128]{2,1,0:T(8,128)(2,1)S(1)} collective-permute-done((bf16[8,272,128]{2,1,0:T(8,128)(2,1)S(1)}, bf16[8,272,128]{2,1,0:T(8,128)(2,1)S(1)}, u32[]{:S(2)}, u32[]{:S(2)}) %collective-permute-start.2) | collective-permute-done | bytes 557088 | tf_op jit(solution)/shard_map/ppermute | solution.py:352
  36.7 1.6 %shard_map.178 = bf16[8,320,128]{2,1,0:T(8,128)(2,1)} custom-call(s32[3]{0:T(128)} %pad_add_fusion.place_ref, f32[8,256,128]{2,1,0:T(8,128)S(1)} %get-tuple-element.22.keep_ref, bf16[8,272,128]{2,1,0:T(8,128)(2,1)S(1)} %get-tuple-element.23.send_ref, bf16[8,272,128]{2,1,0:T(8,128)(2,1)S(1)} %collective-permute-done.2.came_ref), custom_call_target="tpu_custom_call" | custom-call | tf_op jit(solution)/shard_map/pallas_call | solution.py:353
  38.3 3.5 %all-to-all-start.1 = ((bf16[8,320,128]{2,1,0:T(8,128)(2,1)}), bf16[8,320,128]{2,1,0:T(8,128)(2,1)S(1)}, u32[]{:S(2)}, u32[]{:S(2)}) async-start(bf16[8,320,128]{2,1,0:T(8,128)(2,1)} %shard_map.178), calls=%async_computation.1 | async-start | bytes 1310720 | tf_op jit(solution)/shard_map/all_to_all | solution.py:366
  41.8 6.9 %shard_map.179 = (f32[6,64,256]{2,1,0:T(8,128)}, f32[6,64,128]{2,1,0:T(8,128)S(1)}) custom-call(s32[3]{0:T(128)} %pad_add_fusion.place_ref, f32[6,6,6]{2,1,0:T(8,128)} %couple_ref.3, f32[6,64,256]{2,1,0:T(8,128)} %fields_ref.3, f32[1,256]{1,0:T(1,128)} %bitcast.8, f32[3,64,64]{2,1,0:T(8,128)} %diff_ref.1, f32[6,16,64]{2,1,0:T(8,128)} %interp_ref.3, ...), custom_call_target="tpu_custom_call" | custom-call | tf_op jit(solution)/shard_map/pallas_call | solution.py:358
  48.8 5.1 %all-to-all-done.1.got_ref = bf16[8,320,128]{2,1,0:T(8,128)(2,1)S(1)} async-done(((bf16[8,320,128]{2,1,0:T(8,128)(2,1)}), bf16[8,320,128]{2,1,0:T(8,128)(2,1)S(1)}, u32[]{:S(2)}, u32[]{:S(2)}) %all-to-all-start.1) | async-done | bytes 655392 | tf_op jit(solution)/shard_map/all_to_all | solution.py:366
  53.9 0.7 shard_map.180
  54.6 0.0 copy-start.1
  54.6 12.9 %all_to_all.20.here_ref = bf16[8,256,128]{2,1,0:T(8,128)(2,1)S(1)} all-to-all(bf16[8,256,128]{2,1,0:T(8,128)(2,1)S(1)} %shard_map.180), channel_id=1, replica_groups=mesh['y'=4,'z'=4,'xl'=2,'xh'=2,'c'=2] {'y','xl'}, dimensions={0} | all-to-all | bytes 1048576 | tf_op jit(solution)/shard_map/all_to_all | solution.py:374
  67.5 0.0 collective-permute-start.3
  67.5 1.9 %collective-permute-done.3.there_ref = bf16[8,256,128]{2,1,0:T(8,128)(2,1)S(1)} collective-permute-done((bf16[8,256,128]{2,1,0:T(8,128)(2,1)S(1)}, bf16[8,256,128]{2,1,0:T(8,128)(2,1)S(1)}, u32[]{:S(2)}, u32[]{:S(2)}) %collective-permute-start.3) | collective-permute-done | bytes 524320 | tf_op jit(solution)/shard_map/ppermute | solution.py:375
  69.4 0.0 copy-done.1
  69.4 3.5 %shard_map.181 = f32[8,64,128]{2,1,0:T(8,128)S(1)} custom-call(s32[3]{0:T(128)} %pad_add_fusion.place_ref, bf16[8,256,128]{2,1,0:T(8,128)(2,1)S(1)} %all_to_all.20.here_ref, bf16[8,256,128]{2,1,0:T(8,128)(2,1)S(1)} %collective-permute-done.3.there_ref, bf16[8,368,128]{2,1,0:T(8,128)(2,1)S(1)} %copy-done.1), custom_call_target="tpu_custom_call" | custom-call | tf_op jit(solution)/shard_map/pallas_call | solution.py:376
  72.9 11.8 %all_to_all.21.parts_ref = f32[8,64,128]{2,1,0:T(8,128)S(1)} all-to-all(f32[8,64,128]{2,1,0:T(8,128)S(1)} %shard_map.181), channel_id=1, replica_groups=mesh['y'=4,'z'=4,'xl'=2,'xh'=2,'c'=2] {'z','xh'}, dimensions={0} | all-to-all | bytes 524288 | tf_op jit(solution)/shard_map/all_to_all | solution.py:382
  84.7 2.9 %shard_map.182 = (f32[6,64,256]{2,1,0:T(8,128)}, f32[64,128]{1,0:T(8,128)}) custom-call(f32[6]{0:T(128)} %bound_ref.1, f32[6,6,6]{2,1,0:T(8,128)} %couple_ref.3, f32[8,64,128]{2,1,0:T(8,128)S(1)} %all_to_all.21.parts_ref, f32[6,64,128]{2,1,0:T(8,128)S(1)} %get-tuple-element.32.first_ref, f32[6,16,64]{2,1,0:T(8,128)} %bitcast.7, ...), custom_call_target="tpu_custom_call", output_to_operand_aliasing={{0}: (6, {})} | custom-call | tf_op jit(solution)/shard_map/pallas_call | solution.py:384
Async XLA Ops:
  4.3 24.6 %all-to-all-start = ((bf16[8,368,128]{2,1,0:T(8,128)(2,1)}), bf16[8,368,128]{2,1,0:T(8,128)(2,1)S(1)}, u32[]{:S(2)}, u32[]{:S(2)}) async-start(bf16[8,368,128]{2,1,0:T(8,128)(2,1)} %get-tuple-element.18), calls=%async_computation | async-start | bytes 1507328 | tf_op jit(solution)/shard_map/all_to_all | solution.py:343
  12.1 16.8 %collective-permute-start = (bf16[16,384]{1,0:T(8,128)(2,1)S(1)}, bf16[16,384]{1,0:T(8,128)(2,1)S(1)}, u32[]{:S(2)}, u32[]{:S(2)}) collective-permute-start(bf16[16,384]{1,0:T(8,128)(2,1)S(1)} %get-tuple-element.19), channel_id=1, source_target_pairs={{0,127},{1,2},{2,1},{3,4},{4,3},{5,6},{6,5},{7,8},{8,7},{9,10},{10... | collective-permute-start | bytes 36872 | tf_op jit(solution)/shard_map/ppermute | solution.py:341
  18.8 10.1 %collective-permute-start.1 = (bf16[16,384]{1,0:T(8,128)(2,1)S(1)}, bf16[16,384]{1,0:T(8,128)(2,1)S(1)}, u32[]{:S(2)}, u32[]{:S(2)}) collective-permute-start(bf16[16,384]{1,0:T(8,128)(2,1)S(1)} %get-tuple-element.20), channel_id=1, source_target_pairs={{0,1},{1,0},{2,3},{3,2},{4,5},{5,4},{6,7},{7,6},{8,9},{9,8},{10,11... | collective-permute-start | bytes 36872 | tf_op jit(solution)/shard_map/ppermute | solution.py:342
  33.9 0.9 copy-start
  34.7 2.0 %collective-permute-start.2 = (bf16[8,272,128]{2,1,0:T(8,128)(2,1)S(1)}, bf16[8,272,128]{2,1,0:T(8,128)(2,1)S(1)}, u32[]{:S(2)}, u32[]{:S(2)}) collective-permute-start(bf16[8,272,128]{2,1,0:T(8,128)(2,1)S(1)} %get-tuple-element.23.send_ref), channel_id=1, source_target_pairs={{0,1},{1,0},{2,3},{3,2},{4,5},{5,4},{6,7},{7,6},{8,9},{9,8},{10,11... | collective-permute-start | bytes 1671176 | tf_op jit(solution)/shard_map/ppermute | solution.py:352
  38.3 15.6 %all-to-all-start.1 = ((bf16[8,320,128]{2,1,0:T(8,128)(2,1)}), bf16[8,320,128]{2,1,0:T(8,128)(2,1)S(1)}, u32[]{:S(2)}, u32[]{:S(2)}) async-start(bf16[8,320,128]{2,1,0:T(8,128)(2,1)} %shard_map.178), calls=%async_computation.1 | async-start | bytes 1310720 | tf_op jit(solution)/shard_map/all_to_all | solution.py:366
  54.6 14.8 %copy-start.1 = (bf16[8,368,128]{2,1,0:T(8,128)(2,1)S(1)}, bf16[8,368,128]{2,1,0:T(8,128)(2,1)}, u32[]{:S(2)}) copy-start(bf16[8,368,128]{2,1,0:T(8,128)(2,1)} %copy-done) | copy-start | bytes 2260996
  67.5 1.9 %collective-permute-start.3 = (bf16[8,256,128]{2,1,0:T(8,128)(2,1)S(1)}, bf16[8,256,128]{2,1,0:T(8,128)(2,1)S(1)}, u32[]{:S(2)}, u32[]{:S(2)}) collective-permute-start(bf16[8,256,128]{2,1,0:T(8,128)(2,1)S(1)} %all_to_all.20.here_ref), channel_id=1, source_target_pairs={{0,1},{1,0},{2,3},{3,2},{4,5},{5,4},{6,7},{7,6},{8,9},{9,8},{10,11... | collective-permute-start | bytes 1572872 | tf_op jit(solution)/shard_map/ppermute | solution.py:375

commit v4 on v3

--- a/solution.py
+++ b/solution.py
@@ -109,7 +109,11 @@
         message_ref[i, ROW_T:ROWS, :] = table
 
 
-def rays_kernel(place_ref, got_ref, keep_ref, send_ref, c_ref, w_ref, p_ref):
+def rays_kernel(
+    place_ref, got_ref, on_ref, keep_ref, send_ref, saved_ref, c_ref, w_ref, p_ref, sem,
+):
+    save = pltpu.make_async_copy(got_ref, saved_ref, sem)
+    save.start()
     core, half = place_ref[0], place_ref[1]
     mine = pl.multiple_of(128 * core, 128)
     theirs = pl.multiple_of(128 * (1 - core), 128)
@@ -120,25 +124,30 @@
         p_ref[at : at + 128, 0:128] = got_ref[i, pl.ds(mine, 128), :]
         p_ref[at : at + 128, 128:256] = got_ref[i, pl.ds(theirs, 128), :]
 
-    def step(high, carry):
-        c = c_ref[pl.ds(pl.multiple_of(8 * high, 8), 8), :]
+    def step(pair, carry):
+        c = c_ref[pl.ds(pl.multiple_of(16 * pair, 16), 16), :]
         w = w_ref[...]
-        rows = [(c[t : t + 1] * w).astype(BF16) for t in range(8)]
+        rows = [(c[t : t + 1] * w).astype(BF16) for t in range(16)]
         product = mm(jnp.concatenate(rows, axis=0), p_ref[...])
-        at = pl.multiple_of(32 * high, 32)
-        kept = lane_blocks_swapped([product[32 * t : 32 * t + 32, 0:128] for t in range(8)])
-        sent = lane_blocks_swapped([product[32 * t : 32 * t + 32, 128:256] for t in range(8)])
-        for r in range(8):
-            keep_ref[r, pl.ds(at, 32), :] = kept[r]
-            send_ref[r, pl.ds(at, 32), :] = sent[r].astype(BF16)
+        for s in range(2):
+            at = pl.multiple_of(64 * pair + 32 * s, 32)
+            part = [product[256 * s + 32 * t : 256 * s + 32 * t + 32] for t in range(8)]
+            kept = lane_blocks_swapped([x[:, 0:128] for x in part])
+            sent = lane_blocks_swapped([x[:, 128:256] for x in part])
+            for r in range(8):
+                keep_ref[r, pl.ds(at, 32), :] = kept[r]
+                send_ref[r, pl.ds(at, 32), :] = sent[r].astype(BF16)
         return carry
 
-    lax.fori_loop(0, 8, step, 0)
+    lax.fori_loop(0, 4, step, 0)
     for z in range(4):
         send_ref[z, 256:272, :] = got_ref[2 * z + half, ROW_T:ROWS, :]
-
-
-def joined_kernel(place_ref, keep_ref, send_ref, came_ref, out_ref):
+    for i in range(3):
+        send_ref[4 + i, 256:272, :] = on_ref[:, 128 * i : 128 * i + 128]
+    save.wait()
+
+
+def joined_kernel(place_ref, keep_ref, send_ref, came_ref, out_ref, on_ref):
     has_tables = place_ref[0] == place_ref[2]
     tables = []
     for z in range(4):
@@ -148,6 +157,8 @@
     for r in range(8):
         out_ref[r, 0:256, :] = (keep_ref[r] + came_ref[r, 0:256, :].astype(F32)).astype(BF16)
         out_ref[r, 256:320, :] = tables
+    for i in range(3):
+        on_ref[:, 128 * i : 128 * i + 128] = came_ref[4 + i, 256:272, :]
 
 
 def translate_kernel(got_ref, out_ref, h_ref, s_ref):
@@ -184,7 +195,11 @@
         out_ref[r] = incoming
 
 
-def image_kernel(place_ref, here_ref, there_ref, got_ref, out_ref, rows_ref, p_ref):
+def image_kernel(
+    place_ref, here_ref, there_ref, saved_ref, out_ref, rows_ref, p_ref, got_ref, sem,
+):
+    load = pltpu.make_async_copy(saved_ref, got_ref, sem)
+    load.start()
     core = place_ref[0]
     mine = pl.multiple_of(128 * core, 128)
     theirs = pl.multiple_of(128 * (1 - core), 128)
@@ -192,6 +207,7 @@
         parts = lane_blocks_swapped([ref[r].astype(F32) for r in range(8)])
         for t in range(8):
             rows_ref[256 * t : 256 * t + 256, 128 * h : 128 * h + 128] = parts[t].astype(BF16)
+    load.wait()
 
     def step(i, carry):
         for s in range(2):
@@ -211,22 +227,24 @@
 
 
 def element_kernel(
-    place_ref, couple_ref, fields_ref, scale_ref, diff_ref, interp_ref, lift_ref, links_ref,
-    on_ref, off_ref, out_ref, first_ref,
+    place_ref, couple_ref, bound_ref, fields_ref, scale_ref, diff_ref, interp_ref, lift_ref,
+    links_ref, time_ref, on_ref, off_ref, out_ref, first_ref, nodes_ref, times_ref, factor_ref,
 ):
     core = place_ref[0]
     elements = fields_ref.shape[2]
-    interp = interp_ref[...].reshape(96, 64)
-    diff = diff_ref[...].reshape(192, 64)
-    ghosts = jnp.concatenate([on_ref[...], off_ref[...]], axis=0).astype(F32)
-    own, ghost = [], []
-    grads = []
+    both = jnp.concatenate([interp_ref[...].reshape(96, 64), diff_ref[...].reshape(192, 64)], axis=0)
+    both_high, both_low = halves(both)
+    both = jnp.concatenate([both_high, both_high, both_low], axis=1)
+    ghosts = jnp.concatenate([on_ref[...], off_ref[...]], axis=0)
+    own, ghost, grads = [], [], []
     for c in range(6):
-        local = fields_ref[c]
-        own.append(mm(interp, local, NN, HIGH))
-        ghost.append(mm(interp, ghosts[:, 64 * c : 64 * c + 64], NT, HIGH))
-        grads.append(mm(diff, local, NN, HIGH))
-    surface = [jnp.zeros((64, elements), F32) for _ in range(6)]
+        high, low = halves(fields_ref[c])
+        product = mm(both, jnp.concatenate([high, low, high], axis=0))
+        own.append(product[0:96])
+        grads.append(product[96:288])
+        beyond = ghosts[:, 64 * c : 64 * c + 64]
+        ghost.append(mm(both_high[0:96], beyond, NT) + mm(both_low[0:96], beyond, NT))
+    fluxes = [[] for _ in range(6)]
     bound = iota((16, elements), 1) < 8
     for f in range(6):
         at, to = 16 * f, 16 * (f ^ 1)
@@ -237,9 +255,9 @@
         outer = links - elements
         outer = jnp.where(core == 0, outer ^ 16, outer)
         outside = one_hot(iota((32, elements), 0) == outer, BF16)
-        high, low = halves(pool)
-        ghost_high, ghost_low = halves(beyond)
-        across = mm(high, inside) + mm(low, inside) + mm(ghost_high, outside) + mm(ghost_low, outside)
+        across = mm(jnp.concatenate(halves(pool), axis=0), inside)
+        across = across + mm(jnp.concatenate(halves(beyond), axis=0), outside)
+        across = across[0:96] + across[96:192]
         jumps = []
         for c in range(6):
             there = across[16 * c : 16 * c + 16]
@@ -250,7 +268,9 @@
             flux = couple_ref[f, c, 0] * jumps[0]
             for k in range(1, 6):
                 flux = flux + couple_ref[f, c, k] * jumps[k]
-            surface[c] = surface[c] + mm(lift_ref[f], flux, TN, HIGH)
+            fluxes[c].append(flux)
+    lift = lift_ref[...].reshape(96, 64)
+    lift_high, lift_low = halves(lift)
 
     def grad(r, c):
         return grads[c][64 * r : 64 * r + 64]
@@ -265,14 +285,26 @@
     )
     scale = scale_ref[...]
     for c in range(6):
-        value = curls[c] * scale + surface[c]
+        high, low = halves(jnp.concatenate(fluxes[c], axis=0))
+        surface = mm(lift_high, high, TN) + mm(lift_high, low, TN) + mm(lift_low, high, TN)
+        value = curls[c] * scale + surface
         out_ref[c] = value
         first_ref[c] = value[:, 0:128]
+    chosen = one_hot(iota((16, 128), 1) % 16 == iota((16, 128), 0))
+    nodes_ref[...] = mm(lift_ref[5], chosen, TN, HIGH)
+    row, sample = iota((64, 64), 0), iota((64, 64), 1)
+    times = jnp.where(row % 8 * 8 + row // 8 == sample, time_ref[...], 0.0)
+    times_ref[...] = jnp.broadcast_to(jnp.sum(times, axis=1, keepdims=True), (64, 128))
+    for c in range(6):
+        factor = couple_ref[5, c, 0] * bound_ref[0]
+        for k in range(1, 6):
+            factor = factor + couple_ref[5, c, k] * bound_ref[k]
+        factor_ref[c] = jnp.full((8, 128), factor, F32)
 
 
 def finish_kernel(
-    bound_ref, couple_ref, parts_ref, first_ref, lift_ref, time_ref, rate_ref, rate_out,
-    field_out, tile_ref, sem,
+    parts_ref, first_ref, nodes_ref, times_ref, factor_ref, rate_ref, rate_out, field_out,
+    tile_ref, sem,
 ):
     del rate_ref
     total = parts_ref[0]
@@ -281,16 +313,11 @@
     total = total * jnp.float32(1.0 / np.sqrt(np.float32(512)))
     for t in range(8):
         field_out[pl.ds(t, 8, stride=8), :] = total[8 * t : 8 * t + 8]
-    now = mm(time_ref[...], field_out[...], NN, HIGH)
-    node = iota((16, 128), 1) % 16 == iota((16, 128), 0)
-    by_node = jnp.where(node, now, 0.0)
-    collect = one_hot(iota((128, 128), 0) // 16 == iota((128, 128), 1))
-    lifted = mm(lift_ref[5], mm(by_node, collect, NN, HIGH), TN, HIGH)
+    now = jnp.sum(times_ref[...] * total, axis=0, keepdims=True)
+    collect = one_hot(iota((256, 128), 0) % 128 // 16 == iota((256, 128), 1), BF16)
+    lifted = mm(jnp.concatenate(halves(nodes_ref[...] * now), axis=1), collect)
     for c in range(6):
-        factor = couple_ref[5, c, 0] * bound_ref[0]
-        for k in range(1, 6):
-            factor = factor + couple_ref[5, c, k] * bound_ref[k]
-        tile_ref[c] = first_ref[c] + factor * lifted
+        tile_ref[c] = first_ref[c] + factor_ref[c, 0:1, :] * lifted
     copy = pltpu.make_async_copy(tile_ref, rate_out.at[:, :, pl.ds(0, 128)], sem)
     copy.start()
     copy.wait()
@@ -303,6 +330,7 @@
         in_specs=in_specs,
         out_specs=jax.tree.map(lambda _: VMEM, out) if out_specs is None else out_specs,
         scratch_shapes=list(scratch),
+        compiler_params=pltpu.CompilerParams(vmem_limit_bytes=24 << 20),
         **options,
     )
     return run
@@ -338,33 +366,30 @@
     devices = 128
     beside = [(0, 1), (1, 0)]
     across = [(d, (d + 1 if d % 2 else d - 1) % devices) for d in range(devices)]
+    anywhere = pl.BlockSpec(memory_space=pl.ANY)
+    got = lax.all_to_all(message, ("z", "xh"), 0, 0, tiled=True)
+    keep, send, saved = call(
+        rays_kernel,
+        (
+            vmem((8, 256, 128), F32), vmem((8, 272, 128), BF16),
+            pltpu.HBM((8, ROWS, 128), BF16),
+        ),
+        [SMEM, VMEM, VMEM],
+        (
+            pltpu.VMEM((64, 1024), F32), pltpu.VMEM((32, 1024), F32),
+            pltpu.VMEM((1024, 256), BF16), pltpu.SemaphoreType.DMA,
+        ),
+        out_specs=(VMEM, VMEM, pl.BlockSpec(memory_space=pltpu.HBM)),
+    )(place, held(got), held(on_chip))
+    send, off_chip = lax.optimization_barrier((send, off_chip))
+    came = lax.ppermute(send, "c", beside)
     off_chip = lax.ppermute(off_chip, AXES, across)
-    on_chip = lax.ppermute(on_chip, "c", beside)
-    got = lax.all_to_all(message, ("z", "xh"), 0, 0, tiled=True)
-    got, off_chip, on_chip = lax.optimization_barrier((got, off_chip, on_chip))
-    got = held(got)
-    keep, send = call(
-        rays_kernel,
-        (vmem((8, 256, 128), F32), vmem((8, 272, 128), BF16)),
-        [SMEM, VMEM],
-        (pltpu.VMEM((64, 1024), F32), pltpu.VMEM((32, 1024), F32), pltpu.VMEM((1024, 256), BF16)),
-    )(place, got)
-    came = lax.ppermute(send, "c", beside)
-    partial = call(
-        joined_kernel, vmem((8, 320, 128), BF16), [SMEM, VMEM, VMEM, VMEM]
+    partial, on_chip = call(
+        joined_kernel,
+        (vmem((8, 320, 128), BF16), vmem((16, 384), BF16)),
+        [SMEM, VMEM, VMEM, VMEM],
     )(place, held(keep), held(send), held(came))
-    partial, on_chip, off_chip = lax.optimization_barrier((partial, on_chip, off_chip))
-    lift = lift_matrix.transpose(0, 2, 1)
-    rate, first = call(
-        element_kernel,
-        (shaped((6, 64, 256), F32), vmem((6, 64, 128), F32)),
-        [SMEM] * 2 + [VMEM] * 8,
-    )(
-        place, flux_couple, fields, inv_jacobian.reshape(1, -1), diff_matrix, face_interp,
-        lift, neighbours, held(on_chip), held(off_chip),
-    )
     partial = lax.all_to_all(partial, ("y", "xl"), 0, 0, tiled=True)
-    partial, rate, first = lax.optimization_barrier((partial, rate, first))
     incoming = call(
         translate_kernel,
         vmem((8, 256, 128), BF16),
@@ -376,19 +401,34 @@
     parts = call(
         image_kernel,
         vmem((8, 64, 128), F32),
-        [SMEM, VMEM, VMEM, VMEM],
-        (pltpu.VMEM((2048, 256), BF16), pltpu.VMEM((256, 256), BF16)),
-    )(place, held(incoming), held(beyond), got)
+        [SMEM, VMEM, VMEM, pl.BlockSpec(memory_space=pltpu.HBM)],
+        (
+            pltpu.VMEM((2048, 256), BF16), pltpu.VMEM((256, 256), BF16),
+            pltpu.VMEM((8, ROWS, 128), BF16), pltpu.SemaphoreType.DMA,
+        ),
+    )(place, held(incoming), held(beyond), saved)
+    parts, on_chip, off_chip = lax.optimization_barrier((parts, on_chip, off_chip))
+    rate, first, nodes, times, factor = call(
+        element_kernel,
+        (
+            shaped((6, 64, 256), F32), vmem((6, 64, 128), F32), vmem((64, 128), F32),
+            vmem((64, 128), F32), vmem((6, 8, 128), F32),
+        ),
+        [SMEM] * 3 + [VMEM] * 9,
+    )(
+        place, flux_couple, bound_coef, fields, inv_jacobian.reshape(1, -1), diff_matrix,
+        face_interp, lift_matrix.transpose(0, 2, 1), neighbours, time_interp.reshape(1, -1),
+        held(on_chip), held(off_chip),
+    )
     parts = lax.all_to_all(parts, ("z", "xh"), 0, 0, tiled=True)
-    anywhere = pl.BlockSpec(memory_space=pl.ANY)
     return call(
         finish_kernel,
         (shaped((6, 64, 256), F32), shaped((64, 128), F32)),
-        [SMEM] * 2 + [VMEM] * 4 + [anywhere],
+        [VMEM] * 5 + [anywhere],
         (pltpu.VMEM((6, 64, 128), F32), pltpu.SemaphoreType.DMA),
         out_specs=(anywhere, VMEM),
-        input_output_aliases={6: 0},
-    )(bound_coef, flux_couple, held(parts), held(first), lift, time_interp.reshape(1, -1), rate)
+        input_output_aliases={5: 0},
+    )(held(parts), held(first), held(nodes), held(times), held(factor), rate)
 
 
 def solution(mesh):

time: 88.3 us -> 86.4 us (0.978)
  blocking collectives: 24.7 us -> 50.1 us
  starting transfers between devices: 18.1 us -> 5.87 us
  waiting for transfers between devices: 19 us -> 8.84 us
  Pallas kernels: 22.9 us -> 14.7 us
  local copies, waits for them, and re-layouts: 0.86 us -> 4.65 us
    all_to_all x1 -> x2, blocking collectives: 11.8 us -> 38 us  [the longest x1 21.7 us: per_device(): got = lax.all_to_all(message, ('z', 'xh'), 0, 0, tiled=True)]
    ppermute x1, waiting for transfers between devices: 10.1 us -> 1.82 us  [per_device(): off_chip = lax.ppermute(off_chip, AXES, across)]
    all_to_all x2 -> x1, starting transfers between devices: 11.4 us -> 3.55 us  [per_device(): parts = lax.all_to_all(parts, ('z', 'xh'), 0, 0, tiled=True)]
    pallas_call x4, Pallas kernels: 17 us -> 11.6 us  [the longest x1 4.47 us: per_device(): call(image_kernel, vmem((8, 64, 128), F32), [SMEM, VMEM, VMEM, pl.BlockSp...]
    ppermute x1, starting transfers between devices: 6.7 us -> 2.23 us  [per_device(): off_chip = lax.ppermute(off_chip, AXES, across)]
    unnamed x4 -> x38, local copies, waits for them, and re-layouts: 0.86 us -> 4.65 us
    ppermute x1, waiting for transfers between devices: 1.91 us -> 0.01 us  [per_device(): beyond = lax.ppermute(incoming, 'c', beside)]
    pallas_call x1, Pallas kernels: 2.94 us -> 1.48 us  [per_device(): call(finish_kernel, (shaped((6, 64, 256), F32), shaped((64, 128), F32)),...]
  transfers between devices with their start and end apart: 6 -> 4, of which waited for: 4 -> 3; matrix products, arithmetic and copies ran while one was open for 0% -> 0% of each run, Pallas kernels for 8% -> 9%
where the time goes in v4:
time: 86.4 us; the launch traced here: 85.7 us
  blocking collectives  50.1 us (58%)
  Pallas kernels  14.7 us (17%)
  waiting for transfers between devices  8.84 us (10%)
  starting transfers between devices  5.87 us (7%)
  local copies, waits for them, and re-layouts  4.65 us (5%)
  between operations  1.5 us (2%)
    all_to_all x1, blocking collectives, per_device(): got = lax.all_to_all(message, ('z', 'xh'), 0, 0, tiled=True)  21.7 us
    all_to_all x1, blocking collectives, per_device(): partial = lax.all_to_all(partial, ('y', 'xl'), 0, 0, tiled=True)  16.2 us
    all_to_all x1, blocking collectives, per_device(): incoming = lax.all_to_all(incoming, ('y', 'xl'), 0, 0, tiled=True)  12.1 us
    all_to_all x1, waiting for transfers between devices, per_device(): parts = lax.all_to_all(parts, ('z', 'xh'), 0, 0, tiled=True)  5.08 us
    unnamed x38, local copies, waits for them, and re-layouts  4.65 us
    pallas_call x1, Pallas kernels, per_device(): call(image_kernel, vmem((8, 64, 128), F32), [SMEM, VMEM, VMEM, pl.BlockSp...  4.47 us
    all_to_all x1, starting transfers between devices, per_device(): parts = lax.all_to_all(parts, ('z', 'xh'), 0, 0, tiled=True)  3.55 us
    pallas_call x1, Pallas kernels, per_device(): call(rays_kernel, (vmem((8, 256, 128), F32), vmem((8, 272, 128), BF16), p...  3.53 us
  transfers between devices with their start and end apart: 4, of which 3 were waited for; matrix products, arithmetic and copies ran while one was open for 0% of the time, Pallas kernels for 9%

profile of v4, /device:TPU:0, one launch (start us, length us, event | category | flops | bytes accessed | tf_op | source)
XLA Modules:
  0.0 85.7 jit_solution(875128621488600565)
XLA Ops:
  0.6 0.0 copy-start.8
  1.3 0.0 copy-start.12
  1.3 0.0 copy-start.13
  1.3 0.0 copy-start.15
  1.3 0.0 copy-start.16
  1.3 0.1 pad_add_fusion.place_ref
  1.4 0.0 copy-done.8
  1.4 0.6 copy-done.12
  2.0 0.0 copy-done.13
  2.0 0.0 copy-done.15
  2.0 0.0 copy-done.16
  2.0 1.0 %copy-done = f32[6,64,256]{2,1,0:T(8,128)S(1)} copy-done((f32[6,64,256]{2,1,0:T(8,128)S(1)}, f32[6,64,256]{2,1,0:T(8,128)}, u32[]{:S(2)}) %copy-start) | copy-done | bytes 393240
  3.0 0.8 copy-done.3
  3.8 0.9 %copy-done.5 = bf16[128,512]{1,0:T(8,128)(2,1)S(1)} copy-done((bf16[128,512]{1,0:T(8,128)(2,1)S(1)}, bf16[128,512]{1,0:T(8,128)(2,1)}, u32[]{:S(2)}) %copy-start.5) | copy-done | bytes 131096
  4.7 0.7 copy-done.10
  5.4 0.9 %shard_map.176 = (bf16[8,368,128]{2,1,0:T(8,128)(2,1)S(1)}, bf16[16,384]{1,0:T(8,128)(2,1)S(1)}, bf16[16,384]{1,0:T(8,128)(2,1)S(1)}) custom-call(s32[3]{0:T(128)S(1)} %pad_add_fusion.place_ref, s32[2,16]{1,0:T(2,128)S(1)} %copy-done.13, s32[1,1,16]{2,1,0:T(1,128)S(1)} %copy-done.15, s32[1,1]{1,0:T(1,128)S(6)} %copy.21.count_ref, f32[6]{0:T(128)S(1)} %copy-done.16, ...), custom_call_target="tpu_custom_call" | custom-call | tf_op jit(solution)/shard_map/pallas_call | solution.py:358
  6.3 21.7 %all_to_all.20.got_ref = bf16[8,368,128]{2,1,0:T(8,128)(2,1)S(1)} all-to-all(bf16[8,368,128]{2,1,0:T(8,128)(2,1)S(1)} %get-tuple-element.20), channel_id=1, replica_groups=mesh['y'=4,'z'=4,'xl'=2,'xh'=2,'c'=2] {'z','xh'}, dimensions={0} | all-to-all | bytes 1507328 | tf_op jit(solution)/shard_map/all_to_all | solution.py:370
  28.1 3.5 %shard_map.177 = (f32[8,256,128]{2,1,0:T(8,128)S(1)}, bf16[8,272,128]{2,1,0:T(8,128)(2,1)S(1)}, bf16[8,368,128]{2,1,0:T(8,128)(2,1)}) custom-call(s32[3]{0:T(128)S(1)} %pad_add_fusion.place_ref, bf16[8,368,128]{2,1,0:T(8,128)(2,1)S(1)} %all_to_all.20.got_ref, bf16[16,384]{1,0:T(8,128)(2,1)S(1)} %get-tuple-element.21.on_ref), custom_call_target="tpu_custom_call" | custom-call | tf_op jit(solution)/shard_map/pallas_call | solution.py:371
  31.6 0.1 collective-permute-start
  31.7 1.9 %collective-permute-done.came_ref = bf16[8,272,128]{2,1,0:T(8,128)(2,1)S(1)} collective-permute-done((bf16[8,272,128]{2,1,0:T(8,128)(2,1)S(1)}, bf16[8,272,128]{2,1,0:T(8,128)(2,1)S(1)}, u32[]{:S(2)}, u32[]{:S(2)}) %collective-permute-start) | collective-permute-done | bytes 557088 | tf_op jit(solution)/shard_map/ppermute | solution.py:385
  33.6 0.7 shard_map.178
  34.3 16.2 %all_to_all.21.got_ref = bf16[8,320,128]{2,1,0:T(8,128)(2,1)S(1)} all-to-all(bf16[8,320,128]{2,1,0:T(8,128)(2,1)S(1)} %get-tuple-element.26), channel_id=1, replica_groups=mesh['y'=4,'z'=4,'xl'=2,'xh'=2,'c'=2] {'y','xl'}, dimensions={0} | all-to-all | bytes 1310720 | tf_op jit(solution)/shard_map/all_to_all | solution.py:392
  50.5 0.7 shard_map.179
  51.2 0.0 copy-start.2
  51.2 12.1 %all_to_all.22.here_ref = bf16[8,256,128]{2,1,0:T(8,128)(2,1)S(1)} all-to-all(bf16[8,256,128]{2,1,0:T(8,128)(2,1)S(1)} %shard_map.179), channel_id=1, replica_groups=mesh['y'=4,'z'=4,'xl'=2,'xh'=2,'c'=2] {'y','xl'}, dimensions={0} | all-to-all | bytes 1048576 | tf_op jit(solution)/shard_map/all_to_all | solution.py:399
  63.4 0.0 collective-permute-start.1
  63.4 2.2 %collective-permute-start.2 = (bf16[16,384]{1,0:T(8,128)(2,1)S(1)}, bf16[16,384]{1,0:T(8,128)(2,1)S(1)}, u32[]{:S(2)}, u32[]{:S(2)}) collective-permute-start(bf16[16,384]{1,0:T(8,128)(2,1)S(1)} %get-tuple-element.29), channel_id=1, source_target_pairs={{0,127},{1,2},{2,1},{3,4},{4,3},{5,6},{6,5},{7,8},{8,7},{9,10},{10... | collective-permute-start | bytes 36872 | tf_op jit(solution)/shard_map/ppermute | solution.py:386
  65.6 0.0 collective-permute-done.1.there_ref
  65.6 0.0 copy-done.2
  65.6 4.5 %shard_map.180 = f32[8,64,128]{2,1,0:T(8,128)} custom-call(s32[3]{0:T(128)S(1)} %pad_add_fusion.place_ref, bf16[8,256,128]{2,1,0:T(8,128)(2,1)S(1)} %all_to_all.22.here_ref, bf16[8,256,128]{2,1,0:T(8,128)(2,1)S(1)} %collective-permute-done.1.there_ref, bf16[8,368,128]{2,1,0:T(8,128)(2,1)S(1)} %copy-done.2), custom_call_target="tpu_custom_call" | custom-call | tf_op jit(solution)/shard_map/pallas_call | solution.py:401
  70.1 0.0 copy-start.1
  70.1 1.8 %collective-permute-done.2.off_ref = bf16[16,384]{1,0:T(8,128)(2,1)S(1)} collective-permute-done((bf16[16,384]{1,0:T(8,128)(2,1)S(1)}, bf16[16,384]{1,0:T(8,128)(2,1)S(1)}, u32[]{:S(2)}, u32[]{:S(2)}) %collective-permute-start.2) | collective-permute-done | bytes 12320 | tf_op jit(solution)/shard_map/ppermute | solution.py:386
  71.9 0.0 copy-start.18
  71.9 3.6 %all-to-all-start.3 = ((f32[8,64,128]{2,1,0:T(8,128)}), f32[8,64,128]{2,1,0:T(8,128)S(1)}, u32[]{:S(2)}, u32[]{:S(2)}) async-start(f32[8,64,128]{2,1,0:T(8,128)} %shard_map.180), calls=%async_computation.3 | async-start | bytes 524288 | tf_op jit(solution)/shard_map/all_to_all | solution.py:423
  75.5 0.0 copy-start.14
  75.5 0.0 copy-start.17
  75.5 0.0 copy-done.6
  75.5 0.0 copy-done.1
  75.5 0.0 copy-done.4
  75.5 0.0 copy-done.7
  75.6 0.0 copy-done.9
  75.6 0.0 copy-done.11
  75.6 0.0 copy-done.18
  75.6 0.6 copy-done.14
  76.2 0.0 copy-done.17
  76.2 3.0 %shard_map.181 = (f32[6,64,256]{2,1,0:T(8,128)}, f32[6,64,128]{2,1,0:T(8,128)S(1)}, f32[64,128]{1,0:T(8,128)S(1)}, f32[64,128]{1,0:T(8,128)S(1)}, f32[6,8,128]{2,1,0:T(8,128)S(1)}) custom-call(s32[3]{0:T(128)S(1)} %pad_add_fusion.place_ref, f32[6,6,6]{2,1,0:T(8,128)S(1)} %copy-done.9, f32[6]{0:T(128)S(1)} %copy-done.17, f32[6,64,256]{2,1,0:T(8,128)S(1)} %copy-done.1, ...), custom_call_target="tpu_custom_call" | custom-call | tf_op jit(solution)/shard_map/pallas_call | solution.py:411
  79.1 5.1 %all-to-all-done.3.parts_ref = f32[8,64,128]{2,1,0:T(8,128)S(1)} async-done(((f32[8,64,128]{2,1,0:T(8,128)}), f32[8,64,128]{2,1,0:T(8,128)S(1)}, u32[]{:S(2)}, u32[]{:S(2)}) %all-to-all-start.3) | async-done | bytes 262176 | tf_op jit(solution)/shard_map/all_to_all | solution.py:423
  84.2 1.5 %shard_map.182 = (f32[6,64,256]{2,1,0:T(8,128)}, f32[64,128]{1,0:T(8,128)}) custom-call(f32[8,64,128]{2,1,0:T(8,128)S(1)} %all-to-all-done.3.parts_ref, f32[6,64,128]{2,1,0:T(8,128)S(1)} %get-tuple-element.33.first_ref, f32[64,128]{1,0:T(8,128)S(1)} %get-tuple-element.34.nodes_ref, ...), custom_call_target="tpu_custom_call", output_to_operand_aliasing={{0}: (5, {})} | custom-call | tf_op jit(solution)/shard_map/pallas_call | solution.py:424
  (9 shorter events, 0.0 us)
Async XLA Ops:
  0.6 0.8 copy-start.8
  1.3 0.7 copy-start.12
  1.3 0.7 copy-start.13
  1.3 0.7 copy-start.15
  1.3 0.7 copy-start.16
  2.0 1.0 %copy-start = (f32[6,64,256]{2,1,0:T(8,128)S(1)}, f32[6,64,256]{2,1,0:T(8,128)}, u32[]{:S(2)}) copy-start(f32[6,64,256]{2,1,0:T(8,128)} %fields_ref.3) | copy-start | bytes 1179652
  3.0 0.8 copy-start.3
  3.8 0.9 %copy-start.5 = (bf16[128,512]{1,0:T(8,128)(2,1)S(1)}, bf16[128,512]{1,0:T(8,128)(2,1)}, u32[]{:S(2)}) copy-start(bf16[128,512]{1,0:T(8,128)(2,1)} %projection_ref.1) | copy-start | bytes 393220
  4.7 0.7 copy-start.10
  31.6 2.0 %collective-permute-start = (bf16[8,272,128]{2,1,0:T(8,128)(2,1)S(1)}, bf16[8,272,128]{2,1,0:T(8,128)(2,1)S(1)}, u32[]{:S(2)}, u32[]{:S(2)}) collective-permute-start(bf16[8,272,128]{2,1,0:T(8,128)(2,1)S(1)} %get-tuple-element.25.send_ref), channel_id=1, source_target_pairs={{0,1},{1,0},{2,3},{3,2},{4,5},{5,4},{6,7},{7,6},{8,9},{9,8},{10,11... | collective-permute-start | bytes 1671176 | tf_op jit(solution)/shard_map/ppermute | solution.py:385
  51.2 14.4 %copy-start.2 = (bf16[8,368,128]{2,1,0:T(8,128)(2,1)S(1)}, bf16[8,368,128]{2,1,0:T(8,128)(2,1)}, u32[]{:S(2)}) copy-start(bf16[8,368,128]{2,1,0:T(8,128)(2,1)} %get-tuple-element.27.saved_ref) | copy-start | bytes 2260996
  63.4 2.2 %collective-permute-start.1 = (bf16[8,256,128]{2,1,0:T(8,128)(2,1)S(1)}, bf16[8,256,128]{2,1,0:T(8,128)(2,1)S(1)}, u32[]{:S(2)}, u32[]{:S(2)}) collective-permute-start(bf16[8,256,128]{2,1,0:T(8,128)(2,1)S(1)} %all_to_all.22.here_ref), channel_id=1, source_target_pairs={{0,1},{1,0},{2,3},{3,2},{4,5},{5,4},{6,7},{7,6},{8,9},{9,8},{10,11... | collective-permute-start | bytes 1572872 | tf_op jit(solution)/shard_map/ppermute | solution.py:400
  63.4 8.6 %collective-permute-start.2 = (bf16[16,384]{1,0:T(8,128)(2,1)S(1)}, bf16[16,384]{1,0:T(8,128)(2,1)S(1)}, u32[]{:S(2)}, u32[]{:S(2)}) collective-permute-start(bf16[16,384]{1,0:T(8,128)(2,1)S(1)} %get-tuple-element.29), channel_id=1, source_target_pairs={{0,127},{1,2},{2,1},{3,4},{4,3},{5,6},{6,5},{7,8},{8,7},{9,10},{10... | collective-permute-start | bytes 36872 | tf_op jit(solution)/shard_map/ppermute | solution.py:386
  65.6 9.9 %copy-start.6 = (f32[3,64,64]{2,1,0:T(8,128)S(1)}, f32[3,64,64]{2,1,0:T(8,128)}, u32[]{:S(2)}) copy-start(f32[3,64,64]{2,1,0:T(8,128)} %diff_ref.1) | copy-start | bytes 147460
  70.1 5.5 %copy-start.1 = (f32[6,64,256]{2,1,0:T(8,128)S(1)}, f32[6,64,256]{2,1,0:T(8,128)}, u32[]{:S(2)}) copy-start(f32[6,64,256]{2,1,0:T(8,128)} %fields_ref.3) | copy-start | bytes 1179652
  71.9 3.6 %copy-start.4 = (f32[6,16,64]{2,1,0:T(8,128)S(1)}, f32[6,16,64]{2,1,0:T(8,128)}, u32[]{:S(2)}) copy-start(f32[6,16,64]{2,1,0:T(8,128)} %interp_ref.3) | copy-start | bytes 73732
  71.9 3.6 %copy-start.7 = (f32[6,64,16]{1,2,0:T(8,128)S(1)}, f32[6,64,16]{1,2,0:T(8,128)}, u32[]{:S(2)}) copy-start(f32[6,64,16]{1,2,0:T(8,128)} %param.21) | copy-start | bytes 73732
  71.9 3.6 %copy-start.9 = (f32[6,6,6]{2,1,0:T(8,128)S(1)}, f32[6,6,6]{2,1,0:T(8,128)}, u32[]{:S(2)}) copy-start(f32[6,6,6]{2,1,0:T(8,128)} %couple_ref.1) | copy-start | bytes 2596
  71.9 3.7 %copy-start.11 = (s32[6,256]{1,0:T(8,128)S(1)}, s32[6,256]{1,0:T(8,128)}, u32[]{:S(2)}) copy-start(s32[6,256]{1,0:T(8,128)} %links_ref.1) | copy-start | bytes 18436
  71.9 3.7 %copy-start.18 = (f32[64]{0:T(128)S(1)}, f32[64]{0:T(128)}, u32[]{:S(2)}) copy-start(f32[64]{0:T(128)} %param.27) | copy-start | bytes 772
  71.9 12.3 %all-to-all-start.3 = ((f32[8,64,128]{2,1,0:T(8,128)}), f32[8,64,128]{2,1,0:T(8,128)S(1)}, u32[]{:S(2)}, u32[]{:S(2)}) async-start(f32[8,64,128]{2,1,0:T(8,128)} %shard_map.180), calls=%async_computation.3 | async-start | bytes 524288 | tf_op jit(solution)/shard_map/all_to_all | solution.py:423
  75.5 0.7 copy-start.14
  75.5 0.7 copy-start.17

commit v5 on v4

--- a/solution.py
+++ b/solution.py
@@ -1,5 +1,3 @@
-import functools
-
 import jax
 import jax.numpy as jnp
 import numpy as np
@@ -7,6 +5,7 @@
 from jax.experimental import pallas as pl
 from jax.experimental.pallas import tpu as pltpu
 from jax.sharding import Mesh, PartitionSpec as P
+
 
 F32 = jnp.float32
 BF16 = jnp.bfloat16
@@ -53,11 +52,11 @@
 
 
 def pack_kernel(
-    place_ref, send_ref, dest_ref, count_ref, coef_ref,
+    send_ref, dest_ref, count_ref, coef_ref,
     fields_ref, interp_ref, history_ref, weight_ref, projection_ref, kernels_ref,
     message_ref, on_ref, off_ref,
 ):
-    core = place_ref[0]
+    core = lax.axis_index("c")
     elements = fields_ref.shape[2]
     flat = fields_ref[...].reshape(384, elements).astype(BF16)
 
@@ -109,12 +108,8 @@
         message_ref[i, ROW_T:ROWS, :] = table
 
 
-def rays_kernel(
-    place_ref, got_ref, on_ref, keep_ref, send_ref, saved_ref, c_ref, w_ref, p_ref, sem,
-):
-    save = pltpu.make_async_copy(got_ref, saved_ref, sem)
-    save.start()
-    core, half = place_ref[0], place_ref[1]
+def rays_kernel(got_ref, on_ref, keep_ref, send_ref, c_ref, w_ref, p_ref):
+    core, half = lax.axis_index("c"), lax.axis_index("xh")
     mine = pl.multiple_of(128 * core, 128)
     theirs = pl.multiple_of(128 * (1 - core), 128)
     for i in range(8):
@@ -144,11 +139,10 @@
         send_ref[z, 256:272, :] = got_ref[2 * z + half, ROW_T:ROWS, :]
     for i in range(3):
         send_ref[4 + i, 256:272, :] = on_ref[:, 128 * i : 128 * i + 128]
-    save.wait()
-
-
-def joined_kernel(place_ref, keep_ref, send_ref, came_ref, out_ref, on_ref):
-    has_tables = place_ref[0] == place_ref[2]
+
+
+def joined_kernel(keep_ref, send_ref, came_ref, out_ref, on_ref):
+    has_tables = lax.axis_index("c") == lax.axis_index("z") % 2
     tables = []
     for z in range(4):
         here, there = send_ref[z, 256:272, :], came_ref[z, 256:272, :]
@@ -195,19 +189,14 @@
         out_ref[r] = incoming
 
 
-def image_kernel(
-    place_ref, here_ref, there_ref, saved_ref, out_ref, rows_ref, p_ref, got_ref, sem,
-):
-    load = pltpu.make_async_copy(saved_ref, got_ref, sem)
-    load.start()
-    core = place_ref[0]
+def image_kernel(here_ref, there_ref, got_ref, out_ref, rows_ref, p_ref):
+    core = lax.axis_index("c")
     mine = pl.multiple_of(128 * core, 128)
     theirs = pl.multiple_of(128 * (1 - core), 128)
     for h, ref in ((0, here_ref), (1, there_ref)):
         parts = lane_blocks_swapped([ref[r].astype(F32) for r in range(8)])
         for t in range(8):
             rows_ref[256 * t : 256 * t + 256, 128 * h : 128 * h + 128] = parts[t].astype(BF16)
-    load.wait()
 
     def step(i, carry):
         for s in range(2):
@@ -227,10 +216,10 @@
 
 
 def element_kernel(
-    place_ref, couple_ref, bound_ref, fields_ref, scale_ref, diff_ref, interp_ref, lift_ref,
+    couple_ref, bound_ref, fields_ref, scale_ref, diff_ref, interp_ref, lift_ref,
     links_ref, time_ref, on_ref, off_ref, out_ref, first_ref, nodes_ref, times_ref, factor_ref,
 ):
-    core = place_ref[0]
+    core = lax.axis_index("c")
     elements = fields_ref.shape[2]
     both = jnp.concatenate([interp_ref[...].reshape(96, 64), diff_ref[...].reshape(192, 64)], axis=0)
     both_high, both_low = halves(both)
@@ -323,14 +312,14 @@
     copy.wait()
 
 
-def call(kernel, out, in_specs, scratch=(), out_specs=None, **options):
+def call(kernel, out, in_specs, scratch=(), out_specs=None, grant=24, **options):
     run = pl.pallas_call(
         kernel,
         out_shape=out,
         in_specs=in_specs,
         out_specs=jax.tree.map(lambda _: VMEM, out) if out_specs is None else out_specs,
         scratch_shapes=list(scratch),
-        compiler_params=pltpu.CompilerParams(vmem_limit_bytes=24 << 20),
+        compiler_params=pltpu.CompilerParams(vmem_limit_bytes=grant << 20),
         **options,
     )
     return run
@@ -353,42 +342,33 @@
     send_index, bound_coef, current_coef, time_interp, current_history, group_weight, projection,
     kernels, pair_dest, pair_count,
 ):
-    place = jnp.stack([lax.axis_index("c"), lax.axis_index("xh"), lax.axis_index("z") % 2])
-    place = place.astype(jnp.int32)
     message, on_chip, off_chip = call(
         pack_kernel,
         (vmem((8, ROWS, 128), BF16), vmem((16, 384), BF16), vmem((16, 384), BF16)),
-        [SMEM] * 5 + [VMEM] * 6,
+        [SMEM] * 4 + [VMEM] * 6,
+        grant=60,
     )(
-        place, send_index, pair_dest, pair_count, current_coef,
+        send_index, pair_dest, pair_count, current_coef,
         fields, face_interp, current_history, group_weight, projection, kernels,
     )
     devices = 128
     beside = [(0, 1), (1, 0)]
     across = [(d, (d + 1 if d % 2 else d - 1) % devices) for d in range(devices)]
     anywhere = pl.BlockSpec(memory_space=pl.ANY)
+    off_chip = lax.ppermute(off_chip, AXES, across)
     got = lax.all_to_all(message, ("z", "xh"), 0, 0, tiled=True)
-    keep, send, saved = call(
+    keep, send = call(
         rays_kernel,
-        (
-            vmem((8, 256, 128), F32), vmem((8, 272, 128), BF16),
-            pltpu.HBM((8, ROWS, 128), BF16),
-        ),
-        [SMEM, VMEM, VMEM],
-        (
-            pltpu.VMEM((64, 1024), F32), pltpu.VMEM((32, 1024), F32),
-            pltpu.VMEM((1024, 256), BF16), pltpu.SemaphoreType.DMA,
-        ),
-        out_specs=(VMEM, VMEM, pl.BlockSpec(memory_space=pltpu.HBM)),
-    )(place, held(got), held(on_chip))
-    send, off_chip = lax.optimization_barrier((send, off_chip))
+        (vmem((8, 256, 128), F32), vmem((8, 272, 128), BF16)),
+        [VMEM] * 2,
+        (pltpu.VMEM((64, 1024), F32), pltpu.VMEM((32, 1024), F32), pltpu.VMEM((1024, 256), BF16)),
+    )(held(got), held(on_chip))
     came = lax.ppermute(send, "c", beside)
-    off_chip = lax.ppermute(off_chip, AXES, across)
     partial, on_chip = call(
         joined_kernel,
         (vmem((8, 320, 128), BF16), vmem((16, 384), BF16)),
-        [SMEM, VMEM, VMEM, VMEM],
-    )(place, held(keep), held(send), held(came))
+        [VMEM] * 3,
+    )(held(keep), held(send), held(came))
     partial = lax.all_to_all(partial, ("y", "xl"), 0, 0, tiled=True)
     incoming = call(
         translate_kernel,
@@ -401,12 +381,9 @@
     parts = call(
         image_kernel,
         vmem((8, 64, 128), F32),
-        [SMEM, VMEM, VMEM, pl.BlockSpec(memory_space=pltpu.HBM)],
-        (
-            pltpu.VMEM((2048, 256), BF16), pltpu.VMEM((256, 256), BF16),
-            pltpu.VMEM((8, ROWS, 128), BF16), pltpu.SemaphoreType.DMA,
-        ),
-    )(place, held(incoming), held(beyond), saved)
+        [VMEM] * 3,
+        (pltpu.VMEM((2048, 256), BF16), pltpu.VMEM((256, 256), BF16)),
+    )(held(incoming), held(beyond), held(got))
     parts, on_chip, off_chip = lax.optimization_barrier((parts, on_chip, off_chip))
     rate, first, nodes, times, factor = call(
         element_kernel,
@@ -414,9 +391,9 @@
             shaped((6, 64, 256), F32), vmem((6, 64, 128), F32), vmem((64, 128), F32),
             vmem((64, 128), F32), vmem((6, 8, 128), F32),
         ),
-        [SMEM] * 3 + [VMEM] * 9,
+        [SMEM] * 2 + [VMEM] * 9,
     )(
-        place, flux_couple, bound_coef, fields, inv_jacobian.reshape(1, -1), diff_matrix,
+        flux_couple, bound_coef, fields, inv_jacobian.reshape(1, -1), diff_matrix,
         face_interp, lift_matrix.transpose(0, 2, 1), neighbours, time_interp.reshape(1, -1),
         held(on_chip), held(off_chip),
     )

time: 86.4 us -> 81.2 us (0.940)
  local copies, waits for them, and re-layouts: 4.65 us -> 0.63 us
  Pallas kernels: 14.7 us -> 13.1 us
  waiting for transfers between devices: 8.84 us -> 9.79 us
    unnamed x38 -> x18, local copies, waits for them, and re-layouts: 4.65 us -> 0.63 us
    pallas_call x2, Pallas kernels: 8 us -> 6.51 us  [the longest x1 3.55 us: per_device(): call(image_kernel, vmem((8, 64, 128), F32), [VMEM] * 3, (pltpu.VMEM((2048...]
    ppermute x1, waiting for transfers between devices: 1.82 us -> 2.76 us  [per_device(): off_chip = lax.ppermute(off_chip, AXES, across)]
  transfers between devices with their start and end apart: 4 -> 4, of which waited for: 3 -> 3; matrix products, arithmetic and copies ran while one was open for 0% -> 0% of each run, Pallas kernels for 9% -> 8%
where the time goes in v5:
time: 81.2 us; the launch traced here: 80.8 us
  blocking collectives  50 us (62%)
  Pallas kernels  13.1 us (16%)
  waiting for transfers between devices  9.79 us (12%)
  starting transfers between devices  5.88 us (7%)
  between operations  1.41 us (2%)
    all_to_all x1, blocking collectives, per_device(): got = lax.all_to_all(message, ('z', 'xh'), 0, 0, tiled=True)  21.7 us
    all_to_all x1, blocking collectives, per_device(): partial = lax.all_to_all(partial, ('y', 'xl'), 0, 0, tiled=True)  16.2 us
    all_to_all x1, blocking collectives, per_device(): incoming = lax.all_to_all(incoming, ('y', 'xl'), 0, 0, tiled=True)  12 us
    all_to_all x1, waiting for transfers between devices, per_device(): parts = lax.all_to_all(parts, ('z', 'xh'), 0, 0, tiled=True)  5.09 us
    all_to_all x1, starting transfers between devices, per_device(): parts = lax.all_to_all(parts, ('z', 'xh'), 0, 0, tiled=True)  3.55 us
    pallas_call x1, Pallas kernels, per_device(): call(image_kernel, vmem((8, 64, 128), F32), [VMEM] * 3, (pltpu.VMEM((2048...  3.55 us
    pallas_call x1, Pallas kernels, per_device(): call(rays_kernel, (vmem((8, 256, 128), F32), vmem((8, 272, 128), BF16)),...  2.96 us
    pallas_call x1, Pallas kernels, per_device(): call(element_kernel, (shaped((6, 64, 256), F32), vmem((6, 64, 128), F32),...  2.95 us
  transfers between devices with their start and end apart: 4, of which 3 were waited for; matrix products, arithmetic and copies ran while one was open for 0% of the time, Pallas kernels for 8%

profile of v5, /device:TPU:0, one launch (start us, length us, event | category | flops | bytes accessed | tf_op | source)
XLA Modules:
  0.0 80.8 jit_solution(18126376337026705474)
XLA Ops:
  1.3 1.4 %shard_map.176 = (bf16[8,368,128]{2,1,0:T(8,128)(2,1)S(1)}, bf16[16,384]{1,0:T(8,128)(2,1)S(1)}, bf16[16,384]{1,0:T(8,128)(2,1)S(1)}) custom-call(s32[2,16]{1,0:T(2,128)} %send_ref.1, s32[1,1,16]{2,1,0:T(1,128)} %dest_ref.1, s32[1,1]{1,0:T(1,128)S(6)} %copy.21.count_ref, f32[6]{0:T(128)} %coef_ref.1, f32[6,64,256]{2,1,0:T(8,128)} %fields_ref.3, ...), custom_call_target="tpu_custom_call" | custom-call | tf_op jit(solution)/shard_map/pallas_call | solution.py:345
  2.7 21.7 %all_to_all.20.got_ref = bf16[8,368,128]{2,1,0:T(8,128)(2,1)S(1)} all-to-all(bf16[8,368,128]{2,1,0:T(8,128)(2,1)S(1)} %get-tuple-element.17), channel_id=1, replica_groups=mesh['y'=4,'z'=4,'xl'=2,'xh'=2,'c'=2] {'z','xh'}, dimensions={0} | all-to-all | bytes 1507328 | tf_op jit(solution)/shard_map/all_to_all | solution.py:359
  24.5 3.0 %shard_map.177 = (f32[8,256,128]{2,1,0:T(8,128)S(1)}, bf16[8,272,128]{2,1,0:T(8,128)(2,1)S(1)}) custom-call(bf16[8,368,128]{2,1,0:T(8,128)(2,1)S(1)} %all_to_all.20.got_ref, bf16[16,384]{1,0:T(8,128)(2,1)S(1)} %get-tuple-element.18.on_ref), custom_call_target="tpu_custom_call" | custom-call | tf_op jit(solution)/shard_map/pallas_call | solution.py:360
  27.4 0.1 collective-permute-start
  27.5 1.9 %collective-permute-done.came_ref = bf16[8,272,128]{2,1,0:T(8,128)(2,1)S(1)} collective-permute-done((bf16[8,272,128]{2,1,0:T(8,128)(2,1)S(1)}, bf16[8,272,128]{2,1,0:T(8,128)(2,1)S(1)}, u32[]{:S(2)}, u32[]{:S(2)}) %collective-permute-start) | collective-permute-done | bytes 557088 | tf_op jit(solution)/shard_map/ppermute | solution.py:366
  29.5 0.1 shard_map.178
  29.6 16.2 %all_to_all.21.got_ref = bf16[8,320,128]{2,1,0:T(8,128)(2,1)S(1)} all-to-all(bf16[8,320,128]{2,1,0:T(8,128)(2,1)S(1)} %get-tuple-element.21), channel_id=1, replica_groups=mesh['y'=4,'z'=4,'xl'=2,'xh'=2,'c'=2] {'y','xl'}, dimensions={0} | all-to-all | bytes 1310720 | tf_op jit(solution)/shard_map/all_to_all | solution.py:372
  45.8 0.7 shard_map.179
  46.5 12.0 %all_to_all.22.here_ref = bf16[8,256,128]{2,1,0:T(8,128)(2,1)S(1)} all-to-all(bf16[8,256,128]{2,1,0:T(8,128)(2,1)S(1)} %shard_map.179), channel_id=1, replica_groups=mesh['y'=4,'z'=4,'xl'=2,'xh'=2,'c'=2] {'y','xl'}, dimensions={0} | all-to-all | bytes 1048576 | tf_op jit(solution)/shard_map/all_to_all | solution.py:379
  58.5 0.0 collective-permute-start.1
  58.5 2.2 %collective-permute-start.2 = (bf16[16,384]{1,0:T(8,128)(2,1)S(1)}, bf16[16,384]{1,0:T(8,128)(2,1)S(1)}, u32[]{:S(2)}, u32[]{:S(2)}) collective-permute-start(bf16[16,384]{1,0:T(8,128)(2,1)S(1)} %get-tuple-element.23), channel_id=1, source_target_pairs={{0,127},{1,2},{2,1},{3,4},{4,3},{5,6},{6,5},{7,8},{8,7},{9,10},{10... | collective-permute-start | bytes 36872 | tf_op jit(solution)/shard_map/ppermute | solution.py:358
  60.7 0.0 collective-permute-done.1.there_ref
  60.7 0.0 copy-start.2
  60.7 3.5 %shard_map.180 = f32[8,64,128]{2,1,0:T(8,128)} custom-call(bf16[8,256,128]{2,1,0:T(8,128)(2,1)S(1)} %all_to_all.22.here_ref, bf16[8,256,128]{2,1,0:T(8,128)(2,1)S(1)} %collective-permute-done.1.there_ref, bf16[8,368,128]{2,1,0:T(8,128)(2,1)S(1)} %all_to_all.20.got_ref), custom_call_target="tpu_custom_call" | custom-call | tf_op jit(solution)/shard_map/pallas_call | solution.py:381
  64.3 0.0 copy-start
  64.3 2.8 %collective-permute-done.2.off_ref = bf16[16,384]{1,0:T(8,128)(2,1)S(1)} collective-permute-done((bf16[16,384]{1,0:T(8,128)(2,1)S(1)}, bf16[16,384]{1,0:T(8,128)(2,1)S(1)}, u32[]{:S(2)}, u32[]{:S(2)}) %collective-permute-start.2) | collective-permute-done | bytes 12320 | tf_op jit(solution)/shard_map/ppermute | solution.py:358
  67.0 0.0 copy-start.1
  67.0 0.0 copy-start.3
  67.0 0.0 copy-start.4
  67.0 0.0 copy-start.5
  67.0 0.0 copy-start.8
  67.1 3.6 %all-to-all-start.3 = ((f32[8,64,128]{2,1,0:T(8,128)}), f32[8,64,128]{2,1,0:T(8,128)S(1)}, u32[]{:S(2)}, u32[]{:S(2)}) async-start(f32[8,64,128]{2,1,0:T(8,128)} %shard_map.180), calls=%async_computation.3 | async-start | bytes 524288 | tf_op jit(solution)/shard_map/all_to_all | solution.py:400
  70.6 0.0 copy-start.6
  70.6 0.0 copy-start.7
  70.6 0.0 copy-done.2
  70.7 0.0 copy-done
  70.7 0.0 copy-done.1
  70.7 0.0 copy-done.3
  70.7 0.0 copy-done.4
  70.7 0.0 copy-done.5
  70.7 0.0 copy-done.8
  70.7 0.6 copy-done.6
  71.3 0.0 copy-done.7
  71.3 2.9 %shard_map.181 = (f32[6,64,256]{2,1,0:T(8,128)}, f32[6,64,128]{2,1,0:T(8,128)S(1)}, f32[64,128]{1,0:T(8,128)S(1)}, f32[64,128]{1,0:T(8,128)S(1)}, f32[6,8,128]{2,1,0:T(8,128)S(1)}) custom-call(f32[6,6,6]{2,1,0:T(8,128)S(1)} %copy-done.4, f32[6]{0:T(128)S(1)} %copy-done.7, f32[6,64,256]{2,1,0:T(8,128)S(1)} %copy-done, f32[1,256]{1,0:T(1,128)S(1)} %bitcast.4, ...), custom_call_target="tpu_custom_call" | custom-call | tf_op jit(solution)/shard_map/pallas_call | solution.py:388
  74.3 5.1 %all-to-all-done.3.parts_ref = f32[8,64,128]{2,1,0:T(8,128)S(1)} async-done(((f32[8,64,128]{2,1,0:T(8,128)}), f32[8,64,128]{2,1,0:T(8,128)S(1)}, u32[]{:S(2)}, u32[]{:S(2)}) %all-to-all-start.3) | async-done | bytes 262176 | tf_op jit(solution)/shard_map/all_to_all | solution.py:400
  79.3 1.5 %shard_map.182 = (f32[6,64,256]{2,1,0:T(8,128)}, f32[64,128]{1,0:T(8,128)}) custom-call(f32[8,64,128]{2,1,0:T(8,128)S(1)} %all-to-all-done.3.parts_ref, f32[6,64,128]{2,1,0:T(8,128)S(1)} %get-tuple-element.27.first_ref, f32[64,128]{1,0:T(8,128)S(1)} %get-tuple-element.28.nodes_ref, ...), custom_call_target="tpu_custom_call", output_to_operand_aliasing={{0}: (5, {})} | custom-call | tf_op jit(solution)/shard_map/pallas_call | solution.py:401
Async XLA Ops:
  27.4 2.0 %collective-permute-start = (bf16[8,272,128]{2,1,0:T(8,128)(2,1)S(1)}, bf16[8,272,128]{2,1,0:T(8,128)(2,1)S(1)}, u32[]{:S(2)}, u32[]{:S(2)}) collective-permute-start(bf16[8,272,128]{2,1,0:T(8,128)(2,1)S(1)} %get-tuple-element.20.send_ref), channel_id=1, source_target_pairs={{0,1},{1,0},{2,3},{3,2},{4,5},{5,4},{6,7},{7,6},{8,9},{9,8},{10,11... | collective-permute-start | bytes 1671176 | tf_op jit(solution)/shard_map/ppermute | solution.py:366
  58.5 2.2 %collective-permute-start.1 = (bf16[8,256,128]{2,1,0:T(8,128)(2,1)S(1)}, bf16[8,256,128]{2,1,0:T(8,128)(2,1)S(1)}, u32[]{:S(2)}, u32[]{:S(2)}) collective-permute-start(bf16[8,256,128]{2,1,0:T(8,128)(2,1)S(1)} %all_to_all.22.here_ref), channel_id=1, source_target_pairs={{0,1},{1,0},{2,3},{3,2},{4,5},{5,4},{6,7},{7,6},{8,9},{9,8},{10,11... | collective-permute-start | bytes 1572872 | tf_op jit(solution)/shard_map/ppermute | solution.py:380
  58.5 8.6 %collective-permute-start.2 = (bf16[16,384]{1,0:T(8,128)(2,1)S(1)}, bf16[16,384]{1,0:T(8,128)(2,1)S(1)}, u32[]{:S(2)}, u32[]{:S(2)}) collective-permute-start(bf16[16,384]{1,0:T(8,128)(2,1)S(1)} %get-tuple-element.23), channel_id=1, source_target_pairs={{0,127},{1,2},{2,1},{3,4},{4,3},{5,6},{6,5},{7,8},{8,7},{9,10},{10... | collective-permute-start | bytes 36872 | tf_op jit(solution)/shard_map/ppermute | solution.py:358
  60.7 9.9 %copy-start.2 = (f32[3,64,64]{2,1,0:T(8,128)S(1)}, f32[3,64,64]{2,1,0:T(8,128)}, u32[]{:S(2)}) copy-start(f32[3,64,64]{2,1,0:T(8,128)} %diff_ref.1) | copy-start | bytes 147460
  64.3 6.4 %copy-start = (f32[6,64,256]{2,1,0:T(8,128)S(1)}, f32[6,64,256]{2,1,0:T(8,128)}, u32[]{:S(2)}) copy-start(f32[6,64,256]{2,1,0:T(8,128)} %fields_ref.3) | copy-start | bytes 1179652
  67.0 3.6 %copy-start.1 = (f32[6,16,64]{2,1,0:T(8,128)S(1)}, f32[6,16,64]{2,1,0:T(8,128)}, u32[]{:S(2)}) copy-start(f32[6,16,64]{2,1,0:T(8,128)} %interp_ref.3) | copy-start | bytes 73732
  67.0 3.6 %copy-start.3 = (f32[6,64,16]{1,2,0:T(8,128)S(1)}, f32[6,64,16]{1,2,0:T(8,128)}, u32[]{:S(2)}) copy-start(f32[6,64,16]{1,2,0:T(8,128)} %param.21) | copy-start | bytes 73732
  67.0 3.6 %copy-start.4 = (f32[6,6,6]{2,1,0:T(8,128)S(1)}, f32[6,6,6]{2,1,0:T(8,128)}, u32[]{:S(2)}) copy-start(f32[6,6,6]{2,1,0:T(8,128)} %couple_ref.1) | copy-start | bytes 2596
  67.0 3.7 %copy-start.5 = (s32[6,256]{1,0:T(8,128)S(1)}, s32[6,256]{1,0:T(8,128)}, u32[]{:S(2)}) copy-start(s32[6,256]{1,0:T(8,128)} %links_ref.1) | copy-start | bytes 18436
  67.0 3.7 %copy-start.8 = (f32[64]{0:T(128)S(1)}, f32[64]{0:T(128)}, u32[]{:S(2)}) copy-start(f32[64]{0:T(128)} %param.27) | copy-start | bytes 772
  67.1 12.3 %all-to-all-start.3 = ((f32[8,64,128]{2,1,0:T(8,128)}), f32[8,64,128]{2,1,0:T(8,128)S(1)}, u32[]{:S(2)}, u32[]{:S(2)}) async-start(f32[8,64,128]{2,1,0:T(8,128)} %shard_map.180), calls=%async_computation.3 | async-start | bytes 524288 | tf_op jit(solution)/shard_map/all_to_all | solution.py:400
  70.6 0.7 copy-start.6
  70.6 0.7 copy-start.7

commit v6 on v5

--- a/solution.py
+++ b/solution.py
@@ -14,6 +14,12 @@
 VMEM = pl.BlockSpec(memory_space=pltpu.VMEM)
 SMEM = pl.BlockSpec(memory_space=pltpu.SMEM)
 ROW_C, ROW_W, ROW_T, ROWS = 256, 320, 352, 368
+SETS = [
+    [((((y * 4 + z) * 2 + (s ^ xh)) * 2 + xh) * 2) + c for z in range(4) for xh in range(2)]
+    for y in range(4)
+    for s in range(2)
+    for c in range(2)
+]
 NN = (((1,), (0,)), ((), ()))
 NT = (((1,), (1,)), ((), ()))
 TN = (((0,), (0,)), ((), ()))
@@ -356,7 +362,7 @@
     across = [(d, (d + 1 if d % 2 else d - 1) % devices) for d in range(devices)]
     anywhere = pl.BlockSpec(memory_space=pl.ANY)
     off_chip = lax.ppermute(off_chip, AXES, across)
-    got = lax.all_to_all(message, ("z", "xh"), 0, 0, tiled=True)
+    got = lax.all_to_all(message, AXES, 0, 0, axis_index_groups=SETS, tiled=True)
     keep, send = call(
         rays_kernel,
         (vmem((8, 256, 128), F32), vmem((8, 272, 128), BF16)),
@@ -397,7 +403,7 @@
         face_interp, lift_matrix.transpose(0, 2, 1), neighbours, time_interp.reshape(1, -1),
         held(on_chip), held(off_chip),
     )
-    parts = lax.all_to_all(parts, ("z", "xh"), 0, 0, tiled=True)
+    parts = lax.all_to_all(parts, AXES, 0, 0, axis_index_groups=SETS, tiled=True)
     return call(
         finish_kernel,
         (shaped((6, 64, 256), F32), shaped((64, 128), F32)),

time: 81.2 us -> 80.3 us (0.989)
  no operation moved by 1% of the time
where the time goes in v6:
time: 80.3 us; the launch traced here: 79.9 us
  blocking collectives  49.3 us (61%)
  Pallas kernels  13.1 us (16%)
  waiting for transfers between devices  9.17 us (11%)
  starting transfers between devices  6.21 us (8%)
  between operations  1.41 us (2%)
    all_to_all x1, blocking collectives, per_device(): lax.all_to_all(message, AXES, 0, 0, axis_index_groups=SETS, tiled=True)  21.2 us
    all_to_all x1, blocking collectives, per_device(): partial = lax.all_to_all(partial, ('y', 'xl'), 0, 0, tiled=True)  16.2 us
    all_to_all x1, blocking collectives, per_device(): incoming = lax.all_to_all(incoming, ('y', 'xl'), 0, 0, tiled=True)  12 us
    all_to_all x1, waiting for transfers between devices, per_device(): lax.all_to_all(parts, AXES, 0, 0, axis_index_groups=SETS, tiled=True)  4.8 us
    all_to_all x1, starting transfers between devices, per_device(): lax.all_to_all(parts, AXES, 0, 0, axis_index_groups=SETS, tiled=True)  3.55 us
    pallas_call x1, Pallas kernels, per_device(): call(image_kernel, vmem((8, 64, 128), F32), [VMEM] * 3, (pltpu.VMEM((2048...  3.55 us
    pallas_call x1, Pallas kernels, per_device(): call(rays_kernel, (vmem((8, 256, 128), F32), vmem((8, 272, 128), BF16)),...  2.97 us
    pallas_call x1, Pallas kernels, per_device(): call(element_kernel, (shaped((6, 64, 256), F32), vmem((6, 64, 128), F32),...  2.95 us
  transfers between devices with their start and end apart: 4, of which 3 were waited for; matrix products, arithmetic and copies ran while one was open for 0% of the time, Pallas kernels for 8%

profile of v6, /device:TPU:0, one launch (start us, length us, event | category | flops | bytes accessed | tf_op | source)
XLA Modules:
  0.0 79.9 jit_solution(5751692622081724704)
XLA Ops:
  1.3 1.4 %shard_map.176 = (bf16[8,368,128]{2,1,0:T(8,128)(2,1)S(1)}, bf16[16,384]{1,0:T(8,128)(2,1)S(1)}, bf16[16,384]{1,0:T(8,128)(2,1)S(1)}) custom-call(s32[2,16]{1,0:T(2,128)} %send_ref.1, s32[1,1,16]{2,1,0:T(1,128)} %dest_ref.1, s32[1,1]{1,0:T(1,128)S(6)} %copy.21.count_ref, f32[6]{0:T(128)} %coef_ref.1, f32[6,64,256]{2,1,0:T(8,128)} %fields_ref.3, ...), custom_call_target="tpu_custom_call" | custom-call | tf_op jit(solution)/shard_map/pallas_call | solution.py:351
  2.7 21.2 %all_to_all.20.got_ref = bf16[8,368,128]{2,1,0:T(8,128)(2,1)S(1)} all-to-all(bf16[8,368,128]{2,1,0:T(8,128)(2,1)S(1)} %get-tuple-element.17), channel_id=1, replica_groups={{0,6,8,14,16,22,24,30},{1,7,9,15,17,23,25,31},{4,2,12,10,20,18,28,26},{..., dimensions={0} | all-to-all | bytes 1507328 | tf_op jit(solution)/shard_map/all_to_all | solution.py:365
  23.9 3.0 %shard_map.177 = (f32[8,256,128]{2,1,0:T(8,128)S(1)}, bf16[8,272,128]{2,1,0:T(8,128)(2,1)S(1)}) custom-call(bf16[8,368,128]{2,1,0:T(8,128)(2,1)S(1)} %all_to_all.20.got_ref, bf16[16,384]{1,0:T(8,128)(2,1)S(1)} %get-tuple-element.18.on_ref), custom_call_target="tpu_custom_call" | custom-call | tf_op jit(solution)/shard_map/pallas_call | solution.py:366
  26.9 0.1 collective-permute-start
  27.0 1.9 %collective-permute-done.came_ref = bf16[8,272,128]{2,1,0:T(8,128)(2,1)S(1)} collective-permute-done((bf16[8,272,128]{2,1,0:T(8,128)(2,1)S(1)}, bf16[8,272,128]{2,1,0:T(8,128)(2,1)S(1)}, u32[]{:S(2)}, u32[]{:S(2)}) %collective-permute-start) | collective-permute-done | bytes 557088 | tf_op jit(solution)/shard_map/ppermute | solution.py:372
  28.9 0.1 shard_map.178
  29.0 16.2 %all_to_all.21.got_ref = bf16[8,320,128]{2,1,0:T(8,128)(2,1)S(1)} all-to-all(bf16[8,320,128]{2,1,0:T(8,128)(2,1)S(1)} %get-tuple-element.21), channel_id=1, replica_groups=mesh['y'=4,'z'=4,'xl'=2,'xh'=2,'c'=2] {'y','xl'}, dimensions={0} | all-to-all | bytes 1310720 | tf_op jit(solution)/shard_map/all_to_all | solution.py:378
  45.2 0.7 shard_map.179
  45.8 12.0 %all_to_all.22.here_ref = bf16[8,256,128]{2,1,0:T(8,128)(2,1)S(1)} all-to-all(bf16[8,256,128]{2,1,0:T(8,128)(2,1)S(1)} %shard_map.179), channel_id=1, replica_groups=mesh['y'=4,'z'=4,'xl'=2,'xh'=2,'c'=2] {'y','xl'}, dimensions={0} | all-to-all | bytes 1048576 | tf_op jit(solution)/shard_map/all_to_all | solution.py:385
  57.9 0.0 collective-permute-start.1
  57.9 2.6 %collective-permute-start.2 = (bf16[16,384]{1,0:T(8,128)(2,1)S(1)}, bf16[16,384]{1,0:T(8,128)(2,1)S(1)}, u32[]{:S(2)}, u32[]{:S(2)}) collective-permute-start(bf16[16,384]{1,0:T(8,128)(2,1)S(1)} %get-tuple-element.23), channel_id=1, source_target_pairs={{0,127},{1,2},{2,1},{3,4},{4,3},{5,6},{6,5},{7,8},{8,7},{9,10},{10... | collective-permute-start | bytes 36872 | tf_op jit(solution)/shard_map/ppermute | solution.py:364
  60.4 0.0 collective-permute-done.1.there_ref
  60.4 0.0 copy-start.2
  60.4 3.5 %shard_map.180 = f32[8,64,128]{2,1,0:T(8,128)} custom-call(bf16[8,256,128]{2,1,0:T(8,128)(2,1)S(1)} %all_to_all.22.here_ref, bf16[8,256,128]{2,1,0:T(8,128)(2,1)S(1)} %collective-permute-done.1.there_ref, bf16[8,368,128]{2,1,0:T(8,128)(2,1)S(1)} %all_to_all.20.got_ref), custom_call_target="tpu_custom_call" | custom-call | tf_op jit(solution)/shard_map/pallas_call | solution.py:387
  64.0 0.0 copy-start
  64.0 2.4 %collective-permute-done.2.off_ref = bf16[16,384]{1,0:T(8,128)(2,1)S(1)} collective-permute-done((bf16[16,384]{1,0:T(8,128)(2,1)S(1)}, bf16[16,384]{1,0:T(8,128)(2,1)S(1)}, u32[]{:S(2)}, u32[]{:S(2)}) %collective-permute-start.2) | collective-permute-done | bytes 12320 | tf_op jit(solution)/shard_map/ppermute | solution.py:364
  66.4 0.0 copy-start.1
  66.4 0.0 copy-start.3
  66.4 0.0 copy-start.4
  66.4 0.0 copy-start.5
  66.4 0.0 copy-start.8
  66.4 3.6 %all-to-all-start.3 = ((f32[8,64,128]{2,1,0:T(8,128)}), f32[8,64,128]{2,1,0:T(8,128)S(1)}, u32[]{:S(2)}, u32[]{:S(2)}) async-start(f32[8,64,128]{2,1,0:T(8,128)} %shard_map.180), calls=%async_computation.3 | async-start | bytes 524288 | tf_op jit(solution)/shard_map/all_to_all | solution.py:406
  70.0 0.0 copy-start.6
  70.0 0.0 copy-start.7
  70.0 0.0 copy-done.2
  70.0 0.0 copy-done
  70.0 0.0 copy-done.1
  70.0 0.0 copy-done.3
  70.1 0.0 copy-done.4
  70.1 0.0 copy-done.5
  70.1 0.0 copy-done.8
  70.1 0.6 copy-done.6
  70.7 0.0 copy-done.7
  70.7 2.9 %shard_map.181 = (f32[6,64,256]{2,1,0:T(8,128)}, f32[6,64,128]{2,1,0:T(8,128)S(1)}, f32[64,128]{1,0:T(8,128)S(1)}, f32[64,128]{1,0:T(8,128)S(1)}, f32[6,8,128]{2,1,0:T(8,128)S(1)}) custom-call(f32[6,6,6]{2,1,0:T(8,128)S(1)} %copy-done.4, f32[6]{0:T(128)S(1)} %copy-done.7, f32[6,64,256]{2,1,0:T(8,128)S(1)} %copy-done, f32[1,256]{1,0:T(1,128)S(1)} %bitcast.4, ...), custom_call_target="tpu_custom_call" | custom-call | tf_op jit(solution)/shard_map/pallas_call | solution.py:394
  73.6 4.8 %all-to-all-done.3.parts_ref = f32[8,64,128]{2,1,0:T(8,128)S(1)} async-done(((f32[8,64,128]{2,1,0:T(8,128)}), f32[8,64,128]{2,1,0:T(8,128)S(1)}, u32[]{:S(2)}, u32[]{:S(2)}) %all-to-all-start.3) | async-done | bytes 262176 | tf_op jit(solution)/shard_map/all_to_all | solution.py:406
  78.4 1.5 %shard_map.182 = (f32[6,64,256]{2,1,0:T(8,128)}, f32[64,128]{1,0:T(8,128)}) custom-call(f32[8,64,128]{2,1,0:T(8,128)S(1)} %all-to-all-done.3.parts_ref, f32[6,64,128]{2,1,0:T(8,128)S(1)} %get-tuple-element.27.first_ref, f32[64,128]{1,0:T(8,128)S(1)} %get-tuple-element.28.nodes_ref, ...), custom_call_target="tpu_custom_call", output_to_operand_aliasing={{0}: (5, {})} | custom-call | tf_op jit(solution)/shard_map/pallas_call | solution.py:407
Async XLA Ops:
  26.9 2.0 %collective-permute-start = (bf16[8,272,128]{2,1,0:T(8,128)(2,1)S(1)}, bf16[8,272,128]{2,1,0:T(8,128)(2,1)S(1)}, u32[]{:S(2)}, u32[]{:S(2)}) collective-permute-start(bf16[8,272,128]{2,1,0:T(8,128)(2,1)S(1)} %get-tuple-element.20.send_ref), channel_id=1, source_target_pairs={{0,1},{1,0},{2,3},{3,2},{4,5},{5,4},{6,7},{7,6},{8,9},{9,8},{10,11... | collective-permute-start | bytes 1671176 | tf_op jit(solution)/shard_map/ppermute | solution.py:372
  57.9 2.6 %collective-permute-start.1 = (bf16[8,256,128]{2,1,0:T(8,128)(2,1)S(1)}, bf16[8,256,128]{2,1,0:T(8,128)(2,1)S(1)}, u32[]{:S(2)}, u32[]{:S(2)}) collective-permute-start(bf16[8,256,128]{2,1,0:T(8,128)(2,1)S(1)} %all_to_all.22.here_ref), channel_id=1, source_target_pairs={{0,1},{1,0},{2,3},{3,2},{4,5},{5,4},{6,7},{7,6},{8,9},{9,8},{10,11... | collective-permute-start | bytes 1572872 | tf_op jit(solution)/shard_map/ppermute | solution.py:386
  57.9 8.6 %collective-permute-start.2 = (bf16[16,384]{1,0:T(8,128)(2,1)S(1)}, bf16[16,384]{1,0:T(8,128)(2,1)S(1)}, u32[]{:S(2)}, u32[]{:S(2)}) collective-permute-start(bf16[16,384]{1,0:T(8,128)(2,1)S(1)} %get-tuple-element.23), channel_id=1, source_target_pairs={{0,127},{1,2},{2,1},{3,4},{4,3},{5,6},{6,5},{7,8},{8,7},{9,10},{10... | collective-permute-start | bytes 36872 | tf_op jit(solution)/shard_map/ppermute | solution.py:364
  60.4 9.6 %copy-start.2 = (f32[3,64,64]{2,1,0:T(8,128)S(1)}, f32[3,64,64]{2,1,0:T(8,128)}, u32[]{:S(2)}) copy-start(f32[3,64,64]{2,1,0:T(8,128)} %diff_ref.1) | copy-start | bytes 147460
  64.0 6.1 %copy-start = (f32[6,64,256]{2,1,0:T(8,128)S(1)}, f32[6,64,256]{2,1,0:T(8,128)}, u32[]{:S(2)}) copy-start(f32[6,64,256]{2,1,0:T(8,128)} %fields_ref.3) | copy-start | bytes 1179652
  66.4 3.6 %copy-start.1 = (f32[6,16,64]{2,1,0:T(8,128)S(1)}, f32[6,16,64]{2,1,0:T(8,128)}, u32[]{:S(2)}) copy-start(f32[6,16,64]{2,1,0:T(8,128)} %interp_ref.3) | copy-start | bytes 73732
  66.4 3.6 %copy-start.3 = (f32[6,64,16]{1,2,0:T(8,128)S(1)}, f32[6,64,16]{1,2,0:T(8,128)}, u32[]{:S(2)}) copy-start(f32[6,64,16]{1,2,0:T(8,128)} %param.21) | copy-start | bytes 73732
  66.4 3.6 %copy-start.4 = (f32[6,6,6]{2,1,0:T(8,128)S(1)}, f32[6,6,6]{2,1,0:T(8,128)}, u32[]{:S(2)}) copy-start(f32[6,6,6]{2,1,0:T(8,128)} %couple_ref.1) | copy-start | bytes 2596
  66.4 3.7 %copy-start.5 = (s32[6,256]{1,0:T(8,128)S(1)}, s32[6,256]{1,0:T(8,128)}, u32[]{:S(2)}) copy-start(s32[6,256]{1,0:T(8,128)} %links_ref.1) | copy-start | bytes 18436
  66.4 3.7 %copy-start.8 = (f32[64]{0:T(128)S(1)}, f32[64]{0:T(128)}, u32[]{:S(2)}) copy-start(f32[64]{0:T(128)} %param.27) | copy-start | bytes 772
  66.4 12.0 %all-to-all-start.3 = ((f32[8,64,128]{2,1,0:T(8,128)}), f32[8,64,128]{2,1,0:T(8,128)S(1)}, u32[]{:S(2)}, u32[]{:S(2)}) async-start(f32[8,64,128]{2,1,0:T(8,128)} %shard_map.180), calls=%async_computation.3 | async-start | bytes 524288 | tf_op jit(solution)/shard_map/all_to_all | solution.py:406
  70.0 0.7 copy-start.6
  70.0 0.7 copy-start.7

commit v7 on v6

--- a/solution.py
+++ b/solution.py
@@ -120,31 +120,29 @@
     theirs = pl.multiple_of(128 * (1 - core), 128)
     for i in range(8):
         at = 128 * i
-        c_ref[:, at : at + 128] = got_ref[i, ROW_C : ROW_C + 64, :].astype(F32)
-        w_ref[:, at : at + 128] = got_ref[i, ROW_W : ROW_W + 32, :].astype(F32)
+        c_ref[i] = got_ref[i, ROW_C : ROW_C + 64, :].astype(F32)
+        w_ref[i] = got_ref[i, ROW_W : ROW_W + 32, :].astype(F32)
         p_ref[at : at + 128, 0:128] = got_ref[i, pl.ds(mine, 128), :]
         p_ref[at : at + 128, 128:256] = got_ref[i, pl.ds(theirs, 128), :]
-
-    def step(pair, carry):
-        c = c_ref[pl.ds(pl.multiple_of(16 * pair, 16), 16), :]
-        w = w_ref[...]
-        rows = [(c[t : t + 1] * w).astype(BF16) for t in range(16)]
-        product = mm(jnp.concatenate(rows, axis=0), p_ref[...])
-        for s in range(2):
-            at = pl.multiple_of(64 * pair + 32 * s, 32)
-            part = [product[256 * s + 32 * t : 256 * s + 32 * t + 32] for t in range(8)]
-            kept = lane_blocks_swapped([x[:, 0:128] for x in part])
-            sent = lane_blocks_swapped([x[:, 128:256] for x in part])
-            for r in range(8):
-                keep_ref[r, pl.ds(at, 32), :] = kept[r]
-                send_ref[r, pl.ds(at, 32), :] = sent[r].astype(BF16)
-        return carry
-
-    lax.fori_loop(0, 4, step, 0)
     for z in range(4):
         send_ref[z, 256:272, :] = got_ref[2 * z + half, ROW_T:ROWS, :]
     for i in range(3):
         send_ref[4 + i, 256:272, :] = on_ref[:, 128 * i : 128 * i + 128]
+    for high in range(8):
+        rows = []
+        for t in range(8 * high, 8 * high + 8):
+            row = []
+            for i in range(8):
+                c = c_ref[i, pl.ds(t, 8, stride=0), :]
+                row.append((w_ref[i].reshape(4, 8, 128) * c[None]).reshape(32, 128))
+            rows.append(jnp.concatenate(row, axis=1).astype(BF16))
+        product = mm(jnp.concatenate(rows, axis=0), p_ref[...])
+        part = [product[32 * t : 32 * t + 32] for t in range(8)]
+        kept = lane_blocks_swapped([x[:, 0:128] for x in part])
+        sent = lane_blocks_swapped([x[:, 128:256].astype(BF16) for x in part])
+        for r in range(8):
+            keep_ref[r, 32 * high : 32 * high + 32, :] = kept[r]
+            send_ref[r, 32 * high : 32 * high + 32, :] = sent[r]
 
 
 def joined_kernel(keep_ref, send_ref, came_ref, out_ref, on_ref):
@@ -195,30 +193,38 @@
         out_ref[r] = incoming
 
 
-def image_kernel(here_ref, there_ref, got_ref, out_ref, rows_ref, p_ref):
+def image_kernel(here_ref, there_ref, got_ref, out_ref, p_ref, w_ref):
     core = lax.axis_index("c")
     mine = pl.multiple_of(128 * core, 128)
     theirs = pl.multiple_of(128 * (1 - core), 128)
-    for h, ref in ((0, here_ref), (1, there_ref)):
-        parts = lane_blocks_swapped([ref[r].astype(F32) for r in range(8)])
-        for t in range(8):
-            rows_ref[256 * t : 256 * t + 256, 128 * h : 128 * h + 128] = parts[t].astype(BF16)
-
-    def step(i, carry):
-        for s in range(2):
-            p_ref[128 * s : 128 * s + 128, 0:128] = got_ref[2 * i + s, pl.ds(mine, 128), :]
-            p_ref[128 * s : 128 * s + 128, 128:256] = got_ref[2 * i + s, pl.ds(theirs, 128), :]
-        image = mm(rows_ref[...], p_ref[...], NT)
-        for s in range(2):
-            weight = got_ref[2 * i + s, ROW_W : ROW_W + 32, :].astype(F32)
-            weight = jnp.broadcast_to(weight[:, None, :], (32, 8, 128))
+    for i in range(8):
+        at = 128 * i
+        p_ref[at : at + 128, 0:128] = got_ref[i, pl.ds(mine, 128), :]
+        p_ref[at : at + 128, 128:256] = got_ref[i, pl.ds(theirs, 128), :]
+        w_ref[i] = got_ref[i, ROW_W : ROW_W + 32, :].astype(F32)
+    for chunk in range(2):
+        at = 128 * chunk
+        rows = []
+        for ref in (here_ref, there_ref):
+            parts = [ref[r, at : at + 128, :] for r in range(8)]
+            rows.append(jnp.concatenate(lane_blocks_swapped(parts), axis=0))
+        rows = jnp.concatenate(rows, axis=1)
+        for i in range(4):
+            image = mm(rows, p_ref[256 * i : 256 * i + 256, :], NT)
+            weight = [
+                jnp.concatenate([w_ref[2 * i + s, pl.ds(q, 8, stride=0), :] for s in range(2)], axis=1)
+                for q in range(16 * chunk, 16 * chunk + 16)
+            ]
             for t in range(8):
-                block = image[256 * t : 256 * t + 256, 128 * s : 128 * s + 128]
-                block = block.reshape(32, 8, 128) * weight
-                out_ref[2 * i + s, 8 * t : 8 * t + 8, :] = jnp.sum(block, axis=0)
-        return carry
-
-    lax.fori_loop(0, 4, step, 0)
+                total = image[128 * t : 128 * t + 8] * weight[0]
+                for q in range(1, 16):
+                    at = 128 * t + 8 * q
+                    total = total + image[at : at + 8] * weight[q]
+                for s in range(2):
+                    part = total[:, 128 * s : 128 * s + 128]
+                    if chunk > 0:
+                        part = part + out_ref[2 * i + s, 8 * t : 8 * t + 8, :]
+                    out_ref[2 * i + s, 8 * t : 8 * t + 8, :] = part
 
 
 def element_kernel(
@@ -367,7 +373,7 @@
         rays_kernel,
         (vmem((8, 256, 128), F32), vmem((8, 272, 128), BF16)),
         [VMEM] * 2,
-        (pltpu.VMEM((64, 1024), F32), pltpu.VMEM((32, 1024), F32), pltpu.VMEM((1024, 256), BF16)),
+        (pltpu.VMEM((8, 64, 128), F32), pltpu.VMEM((8, 32, 128), F32), pltpu.VMEM((1024, 256), BF16)),
     )(held(got), held(on_chip))
     came = lax.ppermute(send, "c", beside)
     partial, on_chip = call(
@@ -388,7 +394,7 @@
         image_kernel,
         vmem((8, 64, 128), F32),
         [VMEM] * 3,
-        (pltpu.VMEM((2048, 256), BF16), pltpu.VMEM((256, 256), BF16)),
+        (pltpu.VMEM((1024, 256), BF16), pltpu.VMEM((8, 32, 128), F32)),
     )(held(incoming), held(beyond), held(got))
     parts, on_chip, off_chip = lax.optimization_barrier((parts, on_chip, off_chip))
     rate, first, nodes, times, factor = call(

time: 80.3 us -> 79.1 us (0.985)
  Pallas kernels: 13.1 us -> 10.8 us
  waiting for transfers between devices: 9.17 us -> 10.2 us
    pallas_call x1, Pallas kernels: 2.97 us -> 1.73 us  [per_device(): call(rays_kernel, (vmem((8, 256, 128), F32), vmem((8, 272, 128), BF16)),...]
    ppermute x1, waiting for transfers between devices: 2.43 us -> 3.49 us  [per_device(): off_chip = lax.ppermute(off_chip, AXES, across)]
    pallas_call x1, Pallas kernels: 3.55 us -> 2.49 us  [per_device(): call(image_kernel, vmem((8, 64, 128), F32), [VMEM] * 3, (pltpu.VMEM((1024...]
  transfers between devices with their start and end apart: 4 -> 4, of which waited for: 3 -> 3; matrix products, arithmetic and copies ran while one was open for 0% -> 0% of each run, Pallas kernels for 8% -> 7%
where the time goes in v7:
time: 79.1 us; the launch traced here: 78.6 us
  blocking collectives  49.3 us (62%)
  Pallas kernels  10.8 us (14%)
  waiting for transfers between devices  10.2 us (13%)
  starting transfers between devices  6.21 us (8%)
  between operations  1.42 us (2%)
    all_to_all x1, blocking collectives, per_device(): lax.all_to_all(message, AXES, 0, 0, axis_index_groups=SETS, tiled=True)  21.2 us
    all_to_all x1, blocking collectives, per_device(): partial = lax.all_to_all(partial, ('y', 'xl'), 0, 0, tiled=True)  16.2 us
    all_to_all x1, blocking collectives, per_device(): incoming = lax.all_to_all(incoming, ('y', 'xl'), 0, 0, tiled=True)  12 us
    all_to_all x1, waiting for transfers between devices, per_device(): lax.all_to_all(parts, AXES, 0, 0, axis_index_groups=SETS, tiled=True)  4.8 us
    all_to_all x1, starting transfers between devices, per_device(): lax.all_to_all(parts, AXES, 0, 0, axis_index_groups=SETS, tiled=True)  3.55 us
    ppermute x1, waiting for transfers between devices, per_device(): off_chip = lax.ppermute(off_chip, AXES, across)  3.49 us
    pallas_call x1, Pallas kernels, per_device(): call(element_kernel, (shaped((6, 64, 256), F32), vmem((6, 64, 128), F32),...  2.95 us
    ppermute x1, starting transfers between devices, per_device(): off_chip = lax.ppermute(off_chip, AXES, across)  2.57 us
  transfers between devices with their start and end apart: 4, of which 3 were waited for; matrix products, arithmetic and copies ran while one was open for 0% of the time, Pallas kernels for 7%

profile of v7, /device:TPU:0, one launch (start us, length us, event | category | flops | bytes accessed | tf_op | source)
XLA Modules:
  0.0 78.6 jit_solution(6652550685192343003)
XLA Ops:
  1.3 1.4 %shard_map.176 = (bf16[8,368,128]{2,1,0:T(8,128)(2,1)S(1)}, bf16[16,384]{1,0:T(8,128)(2,1)S(1)}, bf16[16,384]{1,0:T(8,128)(2,1)S(1)}) custom-call(s32[2,16]{1,0:T(2,128)} %send_ref.1, s32[1,1,16]{2,1,0:T(1,128)} %dest_ref.1, s32[1,1]{1,0:T(1,128)S(6)} %copy.21.count_ref, f32[6]{0:T(128)} %coef_ref.1, f32[6,64,256]{2,1,0:T(8,128)} %fields_ref.3, ...), custom_call_target="tpu_custom_call" | custom-call | tf_op jit(solution)/shard_map/pallas_call | solution.py:357
  2.7 21.2 %all_to_all.20.got_ref = bf16[8,368,128]{2,1,0:T(8,128)(2,1)S(1)} all-to-all(bf16[8,368,128]{2,1,0:T(8,128)(2,1)S(1)} %get-tuple-element.17), channel_id=1, replica_groups={{0,6,8,14,16,22,24,30},{1,7,9,15,17,23,25,31},{4,2,12,10,20,18,28,26},{..., dimensions={0} | all-to-all | bytes 1507328 | tf_op jit(solution)/shard_map/all_to_all | solution.py:371
  23.9 1.7 %shard_map.177 = (f32[8,256,128]{2,1,0:T(8,128)S(1)}, bf16[8,272,128]{2,1,0:T(8,128)(2,1)S(1)}) custom-call(bf16[8,368,128]{2,1,0:T(8,128)(2,1)S(1)} %all_to_all.20.got_ref, bf16[16,384]{1,0:T(8,128)(2,1)S(1)} %get-tuple-element.18.on_ref), custom_call_target="tpu_custom_call" | custom-call | tf_op jit(solution)/shard_map/pallas_call | solution.py:372
  25.6 0.1 collective-permute-start
  25.7 1.9 %collective-permute-done.came_ref = bf16[8,272,128]{2,1,0:T(8,128)(2,1)S(1)} collective-permute-done((bf16[8,272,128]{2,1,0:T(8,128)(2,1)S(1)}, bf16[8,272,128]{2,1,0:T(8,128)(2,1)S(1)}, u32[]{:S(2)}, u32[]{:S(2)}) %collective-permute-start) | collective-permute-done | bytes 557088 | tf_op jit(solution)/shard_map/ppermute | solution.py:378
  27.7 0.1 shard_map.178
  27.8 16.2 %all_to_all.21.got_ref = bf16[8,320,128]{2,1,0:T(8,128)(2,1)S(1)} all-to-all(bf16[8,320,128]{2,1,0:T(8,128)(2,1)S(1)} %get-tuple-element.21), channel_id=1, replica_groups=mesh['y'=4,'z'=4,'xl'=2,'xh'=2,'c'=2] {'y','xl'}, dimensions={0} | all-to-all | bytes 1310720 | tf_op jit(solution)/shard_map/all_to_all | solution.py:384
  43.9 0.7 shard_map.179
  44.6 12.0 %all_to_all.22.here_ref = bf16[8,256,128]{2,1,0:T(8,128)(2,1)S(1)} all-to-all(bf16[8,256,128]{2,1,0:T(8,128)(2,1)S(1)} %shard_map.179), channel_id=1, replica_groups=mesh['y'=4,'z'=4,'xl'=2,'xh'=2,'c'=2] {'y','xl'}, dimensions={0} | all-to-all | bytes 1048576 | tf_op jit(solution)/shard_map/all_to_all | solution.py:391
  56.6 0.0 collective-permute-start.1
  56.6 2.6 %collective-permute-start.2 = (bf16[16,384]{1,0:T(8,128)(2,1)S(1)}, bf16[16,384]{1,0:T(8,128)(2,1)S(1)}, u32[]{:S(2)}, u32[]{:S(2)}) collective-permute-start(bf16[16,384]{1,0:T(8,128)(2,1)S(1)} %get-tuple-element.23), channel_id=1, source_target_pairs={{0,127},{1,2},{2,1},{3,4},{4,3},{5,6},{6,5},{7,8},{8,7},{9,10},{10... | collective-permute-start | bytes 36872 | tf_op jit(solution)/shard_map/ppermute | solution.py:370
  59.2 0.0 collective-permute-done.1.there_ref
  59.2 0.0 copy-start.2
  59.2 2.5 %shard_map.180 = f32[8,64,128]{2,1,0:T(8,128)} custom-call(bf16[8,256,128]{2,1,0:T(8,128)(2,1)S(1)} %all_to_all.22.here_ref, bf16[8,256,128]{2,1,0:T(8,128)(2,1)S(1)} %collective-permute-done.1.there_ref, bf16[8,368,128]{2,1,0:T(8,128)(2,1)S(1)} %all_to_all.20.got_ref), custom_call_target="tpu_custom_call" | custom-call | tf_op jit(solution)/shard_map/pallas_call | solution.py:393
  61.7 0.0 copy-start
  61.7 3.5 %collective-permute-done.2.off_ref = bf16[16,384]{1,0:T(8,128)(2,1)S(1)} collective-permute-done((bf16[16,384]{1,0:T(8,128)(2,1)S(1)}, bf16[16,384]{1,0:T(8,128)(2,1)S(1)}, u32[]{:S(2)}, u32[]{:S(2)}) %collective-permute-start.2) | collective-permute-done | bytes 12320 | tf_op jit(solution)/shard_map/ppermute | solution.py:370
  65.1 0.0 copy-start.1
  65.2 0.0 copy-start.3
  65.2 0.0 copy-start.4
  65.2 0.0 copy-start.5
  65.2 0.0 copy-start.8
  65.2 3.6 %all-to-all-start.3 = ((f32[8,64,128]{2,1,0:T(8,128)}), f32[8,64,128]{2,1,0:T(8,128)S(1)}, u32[]{:S(2)}, u32[]{:S(2)}) async-start(f32[8,64,128]{2,1,0:T(8,128)} %shard_map.180), calls=%async_computation.3 | async-start | bytes 524288 | tf_op jit(solution)/shard_map/all_to_all | solution.py:412
  68.7 0.0 copy-start.6
  68.7 0.0 copy-start.7
  68.8 0.0 copy-done.2
  68.8 0.0 copy-done
  68.8 0.0 copy-done.1
  68.8 0.0 copy-done.3
  68.8 0.0 copy-done.4
  68.8 0.0 copy-done.5
  68.8 0.0 copy-done.8
  68.8 0.6 copy-done.6
  69.4 0.0 copy-done.7
  69.4 2.9 %shard_map.181 = (f32[6,64,256]{2,1,0:T(8,128)}, f32[6,64,128]{2,1,0:T(8,128)S(1)}, f32[64,128]{1,0:T(8,128)S(1)}, f32[64,128]{1,0:T(8,128)S(1)}, f32[6,8,128]{2,1,0:T(8,128)S(1)}) custom-call(f32[6,6,6]{2,1,0:T(8,128)S(1)} %copy-done.4, f32[6]{0:T(128)S(1)} %copy-done.7, f32[6,64,256]{2,1,0:T(8,128)S(1)} %copy-done, f32[1,256]{1,0:T(1,128)S(1)} %bitcast.4, ...), custom_call_target="tpu_custom_call" | custom-call | tf_op jit(solution)/shard_map/pallas_call | solution.py:400
  72.4 4.8 %all-to-all-done.3.parts_ref = f32[8,64,128]{2,1,0:T(8,128)S(1)} async-done(((f32[8,64,128]{2,1,0:T(8,128)}), f32[8,64,128]{2,1,0:T(8,128)S(1)}, u32[]{:S(2)}, u32[]{:S(2)}) %all-to-all-start.3) | async-done | bytes 262176 | tf_op jit(solution)/shard_map/all_to_all | solution.py:412
  77.2 1.5 %shard_map.182 = (f32[6,64,256]{2,1,0:T(8,128)}, f32[64,128]{1,0:T(8,128)}) custom-call(f32[8,64,128]{2,1,0:T(8,128)S(1)} %all-to-all-done.3.parts_ref, f32[6,64,128]{2,1,0:T(8,128)S(1)} %get-tuple-element.27.first_ref, f32[64,128]{1,0:T(8,128)S(1)} %get-tuple-element.28.nodes_ref, ...), custom_call_target="tpu_custom_call", output_to_operand_aliasing={{0}: (5, {})} | custom-call | tf_op jit(solution)/shard_map/pallas_call | solution.py:413
Async XLA Ops:
  25.6 2.0 %collective-permute-start = (bf16[8,272,128]{2,1,0:T(8,128)(2,1)S(1)}, bf16[8,272,128]{2,1,0:T(8,128)(2,1)S(1)}, u32[]{:S(2)}, u32[]{:S(2)}) collective-permute-start(bf16[8,272,128]{2,1,0:T(8,128)(2,1)S(1)} %get-tuple-element.20.send_ref), channel_id=1, source_target_pairs={{0,1},{1,0},{2,3},{3,2},{4,5},{5,4},{6,7},{7,6},{8,9},{9,8},{10,11... | collective-permute-start | bytes 1671176 | tf_op jit(solution)/shard_map/ppermute | solution.py:378
  56.6 2.6 %collective-permute-start.1 = (bf16[8,256,128]{2,1,0:T(8,128)(2,1)S(1)}, bf16[8,256,128]{2,1,0:T(8,128)(2,1)S(1)}, u32[]{:S(2)}, u32[]{:S(2)}) collective-permute-start(bf16[8,256,128]{2,1,0:T(8,128)(2,1)S(1)} %all_to_all.22.here_ref), channel_id=1, source_target_pairs={{0,1},{1,0},{2,3},{3,2},{4,5},{5,4},{6,7},{7,6},{8,9},{9,8},{10,11... | collective-permute-start | bytes 1572872 | tf_op jit(solution)/shard_map/ppermute | solution.py:392
  56.6 8.6 %collective-permute-start.2 = (bf16[16,384]{1,0:T(8,128)(2,1)S(1)}, bf16[16,384]{1,0:T(8,128)(2,1)S(1)}, u32[]{:S(2)}, u32[]{:S(2)}) collective-permute-start(bf16[16,384]{1,0:T(8,128)(2,1)S(1)} %get-tuple-element.23), channel_id=1, source_target_pairs={{0,127},{1,2},{2,1},{3,4},{4,3},{5,6},{6,5},{7,8},{8,7},{9,10},{10... | collective-permute-start | bytes 36872 | tf_op jit(solution)/shard_map/ppermute | solution.py:370
  59.2 9.6 %copy-start.2 = (f32[3,64,64]{2,1,0:T(8,128)S(1)}, f32[3,64,64]{2,1,0:T(8,128)}, u32[]{:S(2)}) copy-start(f32[3,64,64]{2,1,0:T(8,128)} %diff_ref.1) | copy-start | bytes 147460
  61.7 7.1 %copy-start = (f32[6,64,256]{2,1,0:T(8,128)S(1)}, f32[6,64,256]{2,1,0:T(8,128)}, u32[]{:S(2)}) copy-start(f32[6,64,256]{2,1,0:T(8,128)} %fields_ref.3) | copy-start | bytes 1179652
  65.1 3.6 %copy-start.1 = (f32[6,16,64]{2,1,0:T(8,128)S(1)}, f32[6,16,64]{2,1,0:T(8,128)}, u32[]{:S(2)}) copy-start(f32[6,16,64]{2,1,0:T(8,128)} %interp_ref.3) | copy-start | bytes 73732
  65.2 3.6 %copy-start.3 = (f32[6,64,16]{1,2,0:T(8,128)S(1)}, f32[6,64,16]{1,2,0:T(8,128)}, u32[]{:S(2)}) copy-start(f32[6,64,16]{1,2,0:T(8,128)} %param.21) | copy-start | bytes 73732
  65.2 3.6 %copy-start.4 = (f32[6,6,6]{2,1,0:T(8,128)S(1)}, f32[6,6,6]{2,1,0:T(8,128)}, u32[]{:S(2)}) copy-start(f32[6,6,6]{2,1,0:T(8,128)} %couple_ref.1) | copy-start | bytes 2596
  65.2 3.7 %copy-start.5 = (s32[6,256]{1,0:T(8,128)S(1)}, s32[6,256]{1,0:T(8,128)}, u32[]{:S(2)}) copy-start(s32[6,256]{1,0:T(8,128)} %links_ref.1) | copy-start | bytes 18436
  65.2 3.7 %copy-start.8 = (f32[64]{0:T(128)S(1)}, f32[64]{0:T(128)}, u32[]{:S(2)}) copy-start(f32[64]{0:T(128)} %param.27) | copy-start | bytes 772
  65.2 12.0 %all-to-all-start.3 = ((f32[8,64,128]{2,1,0:T(8,128)}), f32[8,64,128]{2,1,0:T(8,128)S(1)}, u32[]{:S(2)}, u32[]{:S(2)}) async-start(f32[8,64,128]{2,1,0:T(8,128)} %shard_map.180), calls=%async_computation.3 | async-start | bytes 524288 | tf_op jit(solution)/shard_map/all_to_all | solution.py:412
  68.7 0.7 copy-start.6
  68.7 0.7 copy-start.7

commit v8 on v7

--- a/solution.py
+++ b/solution.py
@@ -193,7 +193,7 @@
         out_ref[r] = incoming
 
 
-def image_kernel(here_ref, there_ref, got_ref, out_ref, p_ref, w_ref):
+def image_kernel(here_ref, there_ref, got_ref, out_ref, p_ref, w_ref, sum_ref):
     core = lax.axis_index("c")
     mine = pl.multiple_of(128 * core, 128)
     theirs = pl.multiple_of(128 * (1 - core), 128)
@@ -223,8 +223,10 @@
                 for s in range(2):
                     part = total[:, 128 * s : 128 * s + 128]
                     if chunk > 0:
-                        part = part + out_ref[2 * i + s, 8 * t : 8 * t + 8, :]
-                    out_ref[2 * i + s, 8 * t : 8 * t + 8, :] = part
+                        part = part + sum_ref[2 * i + s, 8 * t : 8 * t + 8, :]
+                    sum_ref[2 * i + s, 8 * t : 8 * t + 8, :] = part
+    for i in range(8):
+        out_ref[i] = sum_ref[i].astype(BF16)
 
 
 def element_kernel(
@@ -305,23 +307,27 @@
 
 def finish_kernel(
     parts_ref, first_ref, nodes_ref, times_ref, factor_ref, rate_ref, rate_out, field_out,
-    tile_ref, sem,
+    tile_ref, field_ref, sems,
 ):
     del rate_ref
-    total = parts_ref[0]
+    total = parts_ref[0].astype(F32)
     for i in range(1, 8):
-        total = total + parts_ref[i]
+        total = total + parts_ref[i].astype(F32)
     total = total * jnp.float32(1.0 / np.sqrt(np.float32(512)))
     for t in range(8):
-        field_out[pl.ds(t, 8, stride=8), :] = total[8 * t : 8 * t + 8]
+        field_ref[pl.ds(t, 8, stride=8), :] = total[8 * t : 8 * t + 8]
+    copies = [pltpu.make_async_copy(field_ref, field_out, sems.at[6])]
+    copies[0].start()
     now = jnp.sum(times_ref[...] * total, axis=0, keepdims=True)
     collect = one_hot(iota((256, 128), 0) % 128 // 16 == iota((256, 128), 1), BF16)
     lifted = mm(jnp.concatenate(halves(nodes_ref[...] * now), axis=1), collect)
     for c in range(6):
         tile_ref[c] = first_ref[c] + factor_ref[c, 0:1, :] * lifted
-    copy = pltpu.make_async_copy(tile_ref, rate_out.at[:, :, pl.ds(0, 128)], sem)
-    copy.start()
-    copy.wait()
+        copy = pltpu.make_async_copy(tile_ref.at[c], rate_out.at[c, :, pl.ds(0, 128)], sems.at[c])
+        copy.start()
+        copies.append(copy)
+    for copy in copies:
+        copy.wait()
 
 
 def call(kernel, out, in_specs, scratch=(), out_specs=None, grant=24, **options):
@@ -392,9 +398,12 @@
     beyond = lax.ppermute(incoming, "c", beside)
     parts = call(
         image_kernel,
-        vmem((8, 64, 128), F32),
+        vmem((8, 64, 128), BF16),
         [VMEM] * 3,
-        (pltpu.VMEM((1024, 256), BF16), pltpu.VMEM((8, 32, 128), F32)),
+        (
+            pltpu.VMEM((1024, 256), BF16), pltpu.VMEM((8, 32, 128), F32),
+            pltpu.VMEM((8, 64, 128), F32),
+        ),
     )(held(incoming), held(beyond), held(got))
     parts, on_chip, off_chip = lax.optimization_barrier((parts, on_chip, off_chip))
     rate, first, nodes, times, factor = call(
@@ -414,8 +423,11 @@
         finish_kernel,
         (shaped((6, 64, 256), F32), shaped((64, 128), F32)),
         [VMEM] * 5 + [anywhere],
-        (pltpu.VMEM((6, 64, 128), F32), pltpu.SemaphoreType.DMA),
-        out_specs=(anywhere, VMEM),
+        (
+            pltpu.VMEM((6, 64, 128), F32), pltpu.VMEM((64, 128), F32),
+            pltpu.SemaphoreType.DMA((7,)),
+        ),
+        out_specs=(anywhere, anywhere),
         input_output_aliases={5: 0},
     )(held(parts), held(first), held(nodes), held(times), held(factor), rate)
 

time: 79.1 us -> 77.8 us (0.984)
  no operation moved by 1% of the time
where the time goes in v8:
time: 77.8 us; the launch traced here: 77.5 us
  blocking collectives  49.3 us (63%)
  Pallas kernels  10.2 us (13%)
  waiting for transfers between devices  9.68 us (12%)
  starting transfers between devices  6.17 us (8%)
  between operations  1.42 us (2%)
    all_to_all x1, blocking collectives, per_device(): lax.all_to_all(message, AXES, 0, 0, axis_index_groups=SETS, tiled=True)  21.2 us
    all_to_all x1, blocking collectives, per_device(): partial = lax.all_to_all(partial, ('y', 'xl'), 0, 0, tiled=True)  16.2 us
    all_to_all x1, blocking collectives, per_device(): incoming = lax.all_to_all(incoming, ('y', 'xl'), 0, 0, tiled=True)  12 us
    all_to_all x1, waiting for transfers between devices, per_device(): lax.all_to_all(parts, AXES, 0, 0, axis_index_groups=SETS, tiled=True)  4.2 us
    ppermute x1, waiting for transfers between devices, per_device(): off_chip = lax.ppermute(off_chip, AXES, across)  3.53 us
    all_to_all x1, starting transfers between devices, per_device(): lax.all_to_all(parts, AXES, 0, 0, axis_index_groups=SETS, tiled=True)  3.51 us
    pallas_call x1, Pallas kernels, per_device(): call(element_kernel, (shaped((6, 64, 256), F32), vmem((6, 64, 128), F32),...  2.94 us
    ppermute x1, starting transfers between devices, per_device(): off_chip = lax.ppermute(off_chip, AXES, across)  2.57 us
  transfers between devices with their start and end apart: 4, of which 3 were waited for; matrix products, arithmetic and copies ran while one was open for 0% of the time, Pallas kernels for 7%

profile of v8, /device:TPU:0, one launch (start us, length us, event | category | flops | bytes accessed | tf_op | source)
XLA Modules:
  0.0 77.5 jit_solution(10084119400226360955)
XLA Ops:
  1.3 1.4 %shard_map.176 = (bf16[8,368,128]{2,1,0:T(8,128)(2,1)S(1)}, bf16[16,384]{1,0:T(8,128)(2,1)S(1)}, bf16[16,384]{1,0:T(8,128)(2,1)S(1)}) custom-call(s32[2,16]{1,0:T(2,128)} %send_ref.1, s32[1,1,16]{2,1,0:T(1,128)} %dest_ref.1, s32[1,1]{1,0:T(1,128)S(6)} %copy.21.count_ref, f32[6]{0:T(128)} %coef_ref.1, f32[6,64,256]{2,1,0:T(8,128)} %fields_ref.3, ...), custom_call_target="tpu_custom_call" | custom-call | tf_op jit(solution)/shard_map/pallas_call | solution.py:363
  2.7 21.2 %all_to_all.20.got_ref = bf16[8,368,128]{2,1,0:T(8,128)(2,1)S(1)} all-to-all(bf16[8,368,128]{2,1,0:T(8,128)(2,1)S(1)} %get-tuple-element.17), channel_id=1, replica_groups={{0,6,8,14,16,22,24,30},{1,7,9,15,17,23,25,31},{4,2,12,10,20,18,28,26},{..., dimensions={0} | all-to-all | bytes 1507328 | tf_op jit(solution)/shard_map/all_to_all | solution.py:377
  23.9 1.7 %shard_map.177 = (f32[8,256,128]{2,1,0:T(8,128)S(1)}, bf16[8,272,128]{2,1,0:T(8,128)(2,1)S(1)}) custom-call(bf16[8,368,128]{2,1,0:T(8,128)(2,1)S(1)} %all_to_all.20.got_ref, bf16[16,384]{1,0:T(8,128)(2,1)S(1)} %get-tuple-element.18.on_ref), custom_call_target="tpu_custom_call" | custom-call | tf_op jit(solution)/shard_map/pallas_call | solution.py:378
  25.6 0.1 collective-permute-start
  25.7 1.9 %collective-permute-done.came_ref = bf16[8,272,128]{2,1,0:T(8,128)(2,1)S(1)} collective-permute-done((bf16[8,272,128]{2,1,0:T(8,128)(2,1)S(1)}, bf16[8,272,128]{2,1,0:T(8,128)(2,1)S(1)}, u32[]{:S(2)}, u32[]{:S(2)}) %collective-permute-start) | collective-permute-done | bytes 557088 | tf_op jit(solution)/shard_map/ppermute | solution.py:384
  27.7 0.1 shard_map.178
  27.8 16.2 %all_to_all.21.got_ref = bf16[8,320,128]{2,1,0:T(8,128)(2,1)S(1)} all-to-all(bf16[8,320,128]{2,1,0:T(8,128)(2,1)S(1)} %get-tuple-element.21), channel_id=1, replica_groups=mesh['y'=4,'z'=4,'xl'=2,'xh'=2,'c'=2] {'y','xl'}, dimensions={0} | all-to-all | bytes 1310720 | tf_op jit(solution)/shard_map/all_to_all | solution.py:390
  43.9 0.7 shard_map.179
  44.6 12.0 %all_to_all.22.here_ref = bf16[8,256,128]{2,1,0:T(8,128)(2,1)S(1)} all-to-all(bf16[8,256,128]{2,1,0:T(8,128)(2,1)S(1)} %shard_map.179), channel_id=1, replica_groups=mesh['y'=4,'z'=4,'xl'=2,'xh'=2,'c'=2] {'y','xl'}, dimensions={0} | all-to-all | bytes 1048576 | tf_op jit(solution)/shard_map/all_to_all | solution.py:397
  56.6 0.0 collective-permute-start.1
  56.6 2.6 %collective-permute-start.2 = (bf16[16,384]{1,0:T(8,128)(2,1)S(1)}, bf16[16,384]{1,0:T(8,128)(2,1)S(1)}, u32[]{:S(2)}, u32[]{:S(2)}) collective-permute-start(bf16[16,384]{1,0:T(8,128)(2,1)S(1)} %get-tuple-element.23), channel_id=1, source_target_pairs={{0,127},{1,2},{2,1},{3,4},{4,3},{5,6},{6,5},{7,8},{8,7},{9,10},{10... | collective-permute-start | bytes 36872 | tf_op jit(solution)/shard_map/ppermute | solution.py:376
  59.2 0.0 collective-permute-done.1.there_ref
  59.2 0.0 copy-start
  59.2 2.4 %shard_map.180 = bf16[8,64,128]{2,1,0:T(8,128)(2,1)} custom-call(bf16[8,256,128]{2,1,0:T(8,128)(2,1)S(1)} %all_to_all.22.here_ref, bf16[8,256,128]{2,1,0:T(8,128)(2,1)S(1)} %collective-permute-done.1.there_ref, bf16[8,368,128]{2,1,0:T(8,128)(2,1)S(1)} %all_to_all.20.got_ref), custom_call_target="tpu_custom_call" | custom-call | tf_op jit(solution)/shard_map/pallas_call | solution.py:399
  61.6 3.5 %collective-permute-done.2.off_ref = bf16[16,384]{1,0:T(8,128)(2,1)S(1)} collective-permute-done((bf16[16,384]{1,0:T(8,128)(2,1)S(1)}, bf16[16,384]{1,0:T(8,128)(2,1)S(1)}, u32[]{:S(2)}, u32[]{:S(2)}) %collective-permute-start.2) | collective-permute-done | bytes 12320 | tf_op jit(solution)/shard_map/ppermute | solution.py:376
  65.1 0.0 copy-start.1
  65.2 0.0 copy-start.2
  65.2 0.0 copy-start.3
  65.2 0.0 copy-start.4
  65.2 0.0 copy-start.5
  65.2 0.0 copy-start.8
  65.2 3.5 %all-to-all-start.3 = ((bf16[8,64,128]{2,1,0:T(8,128)(2,1)}), bf16[8,64,128]{2,1,0:T(8,128)(2,1)S(1)}, u32[]{:S(2)}, u32[]{:S(2)}) async-start(bf16[8,64,128]{2,1,0:T(8,128)(2,1)} %shard_map.180), calls=%async_computation.3 | async-start | bytes 262144 | tf_op jit(solution)/shard_map/all_to_all | solution.py:421
  68.7 0.0 copy-start.6
  68.7 0.0 copy-start.7
  68.7 0.0 copy-done
  68.7 0.0 copy-done.1
  68.8 0.0 copy-done.2
  68.8 0.0 copy-done.3
  68.8 0.0 copy-done.4
  68.8 0.0 copy-done.5
  68.8 0.0 copy-done.8
  68.8 0.6 copy-done.6
  69.4 0.0 copy-done.7
  69.4 2.9 %shard_map.181 = (f32[6,64,256]{2,1,0:T(8,128)}, f32[6,64,128]{2,1,0:T(8,128)S(1)}, f32[64,128]{1,0:T(8,128)S(1)}, f32[64,128]{1,0:T(8,128)S(1)}, f32[6,8,128]{2,1,0:T(8,128)S(1)}) custom-call(f32[6,6,6]{2,1,0:T(8,128)S(1)} %copy-done.4, f32[6]{0:T(128)S(1)} %copy-done.7, f32[6,64,256]{2,1,0:T(8,128)S(1)} %copy-done, f32[1,256]{1,0:T(1,128)S(1)} %bitcast.4, ...), custom_call_target="tpu_custom_call" | custom-call | tf_op jit(solution)/shard_map/pallas_call | solution.py:409
  72.3 4.2 %all-to-all-done.3.parts_ref = bf16[8,64,128]{2,1,0:T(8,128)(2,1)S(1)} async-done(((bf16[8,64,128]{2,1,0:T(8,128)(2,1)}), bf16[8,64,128]{2,1,0:T(8,128)(2,1)S(1)}, u32[]{:S(2)}, u32[]{:S(2)}) %all-to-all-start.3) | async-done | bytes 131104 | tf_op jit(solution)/shard_map/all_to_all | solution.py:421
  76.5 0.9 %shard_map.182 = (f32[6,64,256]{2,1,0:T(8,128)}, f32[64,128]{1,0:T(8,128)}) custom-call(bf16[8,64,128]{2,1,0:T(8,128)(2,1)S(1)} %all-to-all-done.3.parts_ref, f32[6,64,128]{2,1,0:T(8,128)S(1)} %get-tuple-element.27.first_ref, f32[64,128]{1,0:T(8,128)S(1)} %get-tuple-element.28.nodes_ref, ...), custom_call_target="tpu_custom_call", output_to_operand_aliasing={{0}: (5, {})} | custom-call | tf_op jit(solution)/shard_map/pallas_call | solution.py:422
Async XLA Ops:
  25.6 2.0 %collective-permute-start = (bf16[8,272,128]{2,1,0:T(8,128)(2,1)S(1)}, bf16[8,272,128]{2,1,0:T(8,128)(2,1)S(1)}, u32[]{:S(2)}, u32[]{:S(2)}) collective-permute-start(bf16[8,272,128]{2,1,0:T(8,128)(2,1)S(1)} %get-tuple-element.20.send_ref), channel_id=1, source_target_pairs={{0,1},{1,0},{2,3},{3,2},{4,5},{5,4},{6,7},{7,6},{8,9},{9,8},{10,11... | collective-permute-start | bytes 1671176 | tf_op jit(solution)/shard_map/ppermute | solution.py:384
  56.6 2.6 %collective-permute-start.1 = (bf16[8,256,128]{2,1,0:T(8,128)(2,1)S(1)}, bf16[8,256,128]{2,1,0:T(8,128)(2,1)S(1)}, u32[]{:S(2)}, u32[]{:S(2)}) collective-permute-start(bf16[8,256,128]{2,1,0:T(8,128)(2,1)S(1)} %all_to_all.22.here_ref), channel_id=1, source_target_pairs={{0,1},{1,0},{2,3},{3,2},{4,5},{5,4},{6,7},{7,6},{8,9},{9,8},{10,11... | collective-permute-start | bytes 1572872 | tf_op jit(solution)/shard_map/ppermute | solution.py:398
  56.6 8.6 %collective-permute-start.2 = (bf16[16,384]{1,0:T(8,128)(2,1)S(1)}, bf16[16,384]{1,0:T(8,128)(2,1)S(1)}, u32[]{:S(2)}, u32[]{:S(2)}) collective-permute-start(bf16[16,384]{1,0:T(8,128)(2,1)S(1)} %get-tuple-element.23), channel_id=1, source_target_pairs={{0,127},{1,2},{2,1},{3,4},{4,3},{5,6},{6,5},{7,8},{8,7},{9,10},{10... | collective-permute-start | bytes 36872 | tf_op jit(solution)/shard_map/ppermute | solution.py:376
  59.2 9.6 %copy-start = (f32[6,64,256]{2,1,0:T(8,128)S(1)}, f32[6,64,256]{2,1,0:T(8,128)}, u32[]{:S(2)}) copy-start(f32[6,64,256]{2,1,0:T(8,128)} %fields_ref.3) | copy-start | bytes 1179652
  65.1 3.6 %copy-start.1 = (f32[6,16,64]{2,1,0:T(8,128)S(1)}, f32[6,16,64]{2,1,0:T(8,128)}, u32[]{:S(2)}) copy-start(f32[6,16,64]{2,1,0:T(8,128)} %interp_ref.3) | copy-start | bytes 73732
  65.2 3.6 %copy-start.2 = (f32[3,64,64]{2,1,0:T(8,128)S(1)}, f32[3,64,64]{2,1,0:T(8,128)}, u32[]{:S(2)}) copy-start(f32[3,64,64]{2,1,0:T(8,128)} %diff_ref.1) | copy-start | bytes 147460
  65.2 3.6 %copy-start.3 = (f32[6,64,16]{1,2,0:T(8,128)S(1)}, f32[6,64,16]{1,2,0:T(8,128)}, u32[]{:S(2)}) copy-start(f32[6,64,16]{1,2,0:T(8,128)} %param.21) | copy-start | bytes 73732
  65.2 3.6 %copy-start.4 = (f32[6,6,6]{2,1,0:T(8,128)S(1)}, f32[6,6,6]{2,1,0:T(8,128)}, u32[]{:S(2)}) copy-start(f32[6,6,6]{2,1,0:T(8,128)} %couple_ref.1) | copy-start | bytes 2596
  65.2 3.6 %copy-start.5 = (s32[6,256]{1,0:T(8,128)S(1)}, s32[6,256]{1,0:T(8,128)}, u32[]{:S(2)}) copy-start(s32[6,256]{1,0:T(8,128)} %links_ref.1) | copy-start | bytes 18436
  65.2 3.6 %copy-start.8 = (f32[64]{0:T(128)S(1)}, f32[64]{0:T(128)}, u32[]{:S(2)}) copy-start(f32[64]{0:T(128)} %param.27) | copy-start | bytes 772
  65.2 11.4 %all-to-all-start.3 = ((bf16[8,64,128]{2,1,0:T(8,128)(2,1)}), bf16[8,64,128]{2,1,0:T(8,128)(2,1)S(1)}, u32[]{:S(2)}, u32[]{:S(2)}) async-start(bf16[8,64,128]{2,1,0:T(8,128)(2,1)} %shard_map.180), calls=%async_computation.3 | async-start | bytes 262144 | tf_op jit(solution)/shard_map/all_to_all | solution.py:421
  68.7 0.7 copy-start.6
  68.7 0.7 copy-start.7

commit v9 on v8

--- a/solution.py
+++ b/solution.py
@@ -15,8 +15,8 @@
 SMEM = pl.BlockSpec(memory_space=pltpu.SMEM)
 ROW_C, ROW_W, ROW_T, ROWS = 256, 320, 352, 368
 SETS = [
-    [((((y * 4 + z) * 2 + (s ^ xh)) * 2 + xh) * 2) + c for z in range(4) for xh in range(2)]
-    for y in range(4)
+    [((((y * 4 + z) * 2 + (s ^ xh)) * 2 + xh) * 2) + c for y in range(4) for xh in range(2)]
+    for z in range(4)
     for s in range(2)
     for c in range(2)
 ]
@@ -105,12 +105,12 @@
         pick = one_hot(iota((32, 128), 1) == 4 * iota((32, 128), 0) + level, BF16)
         weights.append(mm(pick, weight_ref[...]).astype(BF16))
     for i in range(8):
-        z, xh = i // 2, i % 2
-        at = 256 * (z // 2)
+        y, xh = i // 2, i % 2
+        at = 256 * (y // 2)
         message_ref[i, 0:128, :] = projection_ref[:, at : at + 128]
         message_ref[i, 128:256, :] = projection_ref[:, at + 128 : at + 256]
         message_ref[i, ROW_C : ROW_C + 64, :] = currents
-        message_ref[i, ROW_W : ROW_W + 32, :] = weights[2 * xh + z % 2]
+        message_ref[i, ROW_W : ROW_W + 32, :] = weights[2 * xh + y % 2]
         message_ref[i, ROW_T:ROWS, :] = table
 
 
@@ -124,8 +124,8 @@
         w_ref[i] = got_ref[i, ROW_W : ROW_W + 32, :].astype(F32)
         p_ref[at : at + 128, 0:128] = got_ref[i, pl.ds(mine, 128), :]
         p_ref[at : at + 128, 128:256] = got_ref[i, pl.ds(theirs, 128), :]
-    for z in range(4):
-        send_ref[z, 256:272, :] = got_ref[2 * z + half, ROW_T:ROWS, :]
+    for y in range(4):
+        send_ref[y, 256:272, :] = got_ref[2 * y + half, ROW_T:ROWS, :]
     for i in range(3):
         send_ref[4 + i, 256:272, :] = on_ref[:, 128 * i : 128 * i + 128]
     for high in range(8):
@@ -146,10 +146,10 @@
 
 
 def joined_kernel(keep_ref, send_ref, came_ref, out_ref, on_ref):
-    has_tables = lax.axis_index("c") == lax.axis_index("z") % 2
+    has_tables = lax.axis_index("c") == lax.axis_index("y") % 2
     tables = []
-    for z in range(4):
-        here, there = send_ref[z, 256:272, :], came_ref[z, 256:272, :]
+    for y in range(4):
+        here, there = send_ref[y, 256:272, :], came_ref[y, 256:272, :]
         tables.append(jnp.where(has_tables, here.astype(F32), there.astype(F32)).astype(BF16))
     tables = jnp.concatenate(tables, axis=0)
     for r in range(8):
@@ -165,10 +165,9 @@
         total = total + got_ref[r, 0:256, :].astype(F32)
     rays = total.astype(BF16).astype(F32)
     for r in range(8):
-        y, xl = r // 2, r % 2
-        for z in range(4):
-            patch = 8 * y + 2 * z + xl
-            tile = got_ref[r, 256 + 16 * z : 272 + 16 * z, :].astype(F32)
+        for y in range(4):
+            patch = 8 * y + r
+            tile = got_ref[r, 256 + 16 * y : 272 + 16 * y, :].astype(F32)
             for h in range(2):
                 h_ref[h, pl.ds(patch, 8, stride=32), :] = tile[8 * h : 8 * h + 8]
     table = jnp.concatenate([h_ref[0], h_ref[1]], axis=1).astype(BF16)
@@ -387,14 +386,14 @@
         (vmem((8, 320, 128), BF16), vmem((16, 384), BF16)),
         [VMEM] * 3,
     )(held(keep), held(send), held(came))
-    partial = lax.all_to_all(partial, ("y", "xl"), 0, 0, tiled=True)
+    partial = lax.all_to_all(partial, ("z", "xl"), 0, 0, tiled=True)
     incoming = call(
         translate_kernel,
         vmem((8, 256, 128), BF16),
         [VMEM],
         (pltpu.VMEM((2, 256, 128), F32), pltpu.VMEM((256, 128), F32)),
     )(held(partial))
-    incoming = lax.all_to_all(incoming, ("y", "xl"), 0, 0, tiled=True)
+    incoming = lax.all_to_all(incoming, ("z", "xl"), 0, 0, tiled=True)
     beyond = lax.ppermute(incoming, "c", beside)
     parts = call(
         image_kernel,

time: 77.8 us -> 77.8 us (level)
    all_to_all x2, blocking collectives: 28.2 us -> 29 us  [the longest x1 17 us: per_device(): partial = lax.all_to_all(partial, ('z', 'xl'), 0, 0, tiled=True)]
    all_to_all x1, blocking collectives: 21.2 us -> 20.3 us  [per_device(): lax.all_to_all(message, AXES, 0, 0, axis_index_groups=SETS, tiled=True)]
where the time goes in v9:
time: 77.8 us; the launch traced here: 77.5 us
  blocking collectives  49.3 us (63%)
  Pallas kernels  10.2 us (13%)
  waiting for transfers between devices  9.68 us (12%)
  starting transfers between devices  6.17 us (8%)
  between operations  1.42 us (2%)
    all_to_all x1, blocking collectives, per_device(): lax.all_to_all(message, AXES, 0, 0, axis_index_groups=SETS, tiled=True)  20.3 us
    all_to_all x1, blocking collectives, per_device(): partial = lax.all_to_all(partial, ('z', 'xl'), 0, 0, tiled=True)  17 us
    all_to_all x1, blocking collectives, per_device(): incoming = lax.all_to_all(incoming, ('z', 'xl'), 0, 0, tiled=True)  12 us
    all_to_all x1, waiting for transfers between devices, per_device(): lax.all_to_all(parts, AXES, 0, 0, axis_index_groups=SETS, tiled=True)  4.2 us
    ppermute x1, waiting for transfers between devices, per_device(): off_chip = lax.ppermute(off_chip, AXES, across)  3.53 us
    all_to_all x1, starting transfers between devices, per_device(): lax.all_to_all(parts, AXES, 0, 0, axis_index_groups=SETS, tiled=True)  3.51 us
    pallas_call x1, Pallas kernels, per_device(): call(element_kernel, (shaped((6, 64, 256), F32), vmem((6, 64, 128), F32),...  2.94 us
    ppermute x1, starting transfers between devices, per_device(): off_chip = lax.ppermute(off_chip, AXES, across)  2.57 us
  transfers between devices with their start and end apart: 4, of which 3 were waited for; matrix products, arithmetic and copies ran while one was open for 0% of the time, Pallas kernels for 7%

profile of v9, /device:TPU:0, one launch (start us, length us, event | category | flops | bytes accessed | tf_op | source)
XLA Modules:
  0.0 77.5 jit_solution(1493928580130518699)
XLA Ops:
  1.3 1.4 %shard_map.176 = (bf16[8,368,128]{2,1,0:T(8,128)(2,1)S(1)}, bf16[16,384]{1,0:T(8,128)(2,1)S(1)}, bf16[16,384]{1,0:T(8,128)(2,1)S(1)}) custom-call(s32[2,16]{1,0:T(2,128)} %send_ref.1, s32[1,1,16]{2,1,0:T(1,128)} %dest_ref.1, s32[1,1]{1,0:T(1,128)S(6)} %copy.21.count_ref, f32[6]{0:T(128)} %coef_ref.1, f32[6,64,256]{2,1,0:T(8,128)} %fields_ref.3, ...), custom_call_target="tpu_custom_call" | custom-call | tf_op jit(solution)/shard_map/pallas_call | solution.py:362
  2.7 20.3 %all_to_all.20.got_ref = bf16[8,368,128]{2,1,0:T(8,128)(2,1)S(1)} all-to-all(bf16[8,368,128]{2,1,0:T(8,128)(2,1)S(1)} %get-tuple-element.17), channel_id=1, replica_groups={{0,6,32,38,64,70,96,102},{1,7,33,39,65,71,97,103},{4,2,36,34,68,66,100,..., dimensions={0} | all-to-all | bytes 1507328 | tf_op jit(solution)/shard_map/all_to_all | solution.py:376
  23.1 1.7 %shard_map.177 = (f32[8,256,128]{2,1,0:T(8,128)S(1)}, bf16[8,272,128]{2,1,0:T(8,128)(2,1)S(1)}) custom-call(bf16[8,368,128]{2,1,0:T(8,128)(2,1)S(1)} %all_to_all.20.got_ref, bf16[16,384]{1,0:T(8,128)(2,1)S(1)} %get-tuple-element.18.on_ref), custom_call_target="tpu_custom_call" | custom-call | tf_op jit(solution)/shard_map/pallas_call | solution.py:377
  24.8 0.1 collective-permute-start
  24.9 1.9 %collective-permute-done.came_ref = bf16[8,272,128]{2,1,0:T(8,128)(2,1)S(1)} collective-permute-done((bf16[8,272,128]{2,1,0:T(8,128)(2,1)S(1)}, bf16[8,272,128]{2,1,0:T(8,128)(2,1)S(1)}, u32[]{:S(2)}, u32[]{:S(2)}) %collective-permute-start) | collective-permute-done | bytes 557088 | tf_op jit(solution)/shard_map/ppermute | solution.py:383
  26.8 0.1 shard_map.178
  26.9 17.0 %all_to_all.21.got_ref = bf16[8,320,128]{2,1,0:T(8,128)(2,1)S(1)} all-to-all(bf16[8,320,128]{2,1,0:T(8,128)(2,1)S(1)} %get-tuple-element.21), channel_id=1, replica_groups=mesh['y'=4,'z'=4,'xl'=2,'xh'=2,'c'=2] {'z','xl'}, dimensions={0} | all-to-all | bytes 1310720 | tf_op jit(solution)/shard_map/all_to_all | solution.py:389
  43.9 0.7 shard_map.179
  44.6 12.0 %all_to_all.22.here_ref = bf16[8,256,128]{2,1,0:T(8,128)(2,1)S(1)} all-to-all(bf16[8,256,128]{2,1,0:T(8,128)(2,1)S(1)} %shard_map.179), channel_id=1, replica_groups=mesh['y'=4,'z'=4,'xl'=2,'xh'=2,'c'=2] {'z','xl'}, dimensions={0} | all-to-all | bytes 1048576 | tf_op jit(solution)/shard_map/all_to_all | solution.py:396
  56.6 0.0 collective-permute-start.1
  56.6 2.6 %collective-permute-start.2 = (bf16[16,384]{1,0:T(8,128)(2,1)S(1)}, bf16[16,384]{1,0:T(8,128)(2,1)S(1)}, u32[]{:S(2)}, u32[]{:S(2)}) collective-permute-start(bf16[16,384]{1,0:T(8,128)(2,1)S(1)} %get-tuple-element.23), channel_id=1, source_target_pairs={{0,127},{1,2},{2,1},{3,4},{4,3},{5,6},{6,5},{7,8},{8,7},{9,10},{10... | collective-permute-start | bytes 36872 | tf_op jit(solution)/shard_map/ppermute | solution.py:375
  59.2 0.0 collective-permute-done.1.there_ref
  59.2 0.0 copy-start
  59.2 2.4 %shard_map.180 = bf16[8,64,128]{2,1,0:T(8,128)(2,1)} custom-call(bf16[8,256,128]{2,1,0:T(8,128)(2,1)S(1)} %all_to_all.22.here_ref, bf16[8,256,128]{2,1,0:T(8,128)(2,1)S(1)} %collective-permute-done.1.there_ref, bf16[8,368,128]{2,1,0:T(8,128)(2,1)S(1)} %all_to_all.20.got_ref), custom_call_target="tpu_custom_call" | custom-call | tf_op jit(solution)/shard_map/pallas_call | solution.py:398
  61.6 3.5 %collective-permute-done.2.off_ref = bf16[16,384]{1,0:T(8,128)(2,1)S(1)} collective-permute-done((bf16[16,384]{1,0:T(8,128)(2,1)S(1)}, bf16[16,384]{1,0:T(8,128)(2,1)S(1)}, u32[]{:S(2)}, u32[]{:S(2)}) %collective-permute-start.2) | collective-permute-done | bytes 12320 | tf_op jit(solution)/shard_map/ppermute | solution.py:375
  65.1 0.0 copy-start.1
  65.2 0.0 copy-start.2
  65.2 0.0 copy-start.3
  65.2 0.0 copy-start.4
  65.2 0.0 copy-start.5
  65.2 0.0 copy-start.8
  65.2 3.5 %all-to-all-start.3 = ((bf16[8,64,128]{2,1,0:T(8,128)(2,1)}), bf16[8,64,128]{2,1,0:T(8,128)(2,1)S(1)}, u32[]{:S(2)}, u32[]{:S(2)}) async-start(bf16[8,64,128]{2,1,0:T(8,128)(2,1)} %shard_map.180), calls=%async_computation.3 | async-start | bytes 262144 | tf_op jit(solution)/shard_map/all_to_all | solution.py:420
  68.7 0.0 copy-start.6
  68.7 0.0 copy-start.7
  68.7 0.0 copy-done
  68.7 0.0 copy-done.1
  68.8 0.0 copy-done.2
  68.8 0.0 copy-done.3
  68.8 0.0 copy-done.4
  68.8 0.0 copy-done.5
  68.8 0.0 copy-done.8
  68.8 0.6 copy-done.6
  69.4 0.0 copy-done.7
  69.4 2.9 %shard_map.181 = (f32[6,64,256]{2,1,0:T(8,128)}, f32[6,64,128]{2,1,0:T(8,128)S(1)}, f32[64,128]{1,0:T(8,128)S(1)}, f32[64,128]{1,0:T(8,128)S(1)}, f32[6,8,128]{2,1,0:T(8,128)S(1)}) custom-call(f32[6,6,6]{2,1,0:T(8,128)S(1)} %copy-done.4, f32[6]{0:T(128)S(1)} %copy-done.7, f32[6,64,256]{2,1,0:T(8,128)S(1)} %copy-done, f32[1,256]{1,0:T(1,128)S(1)} %bitcast.4, ...), custom_call_target="tpu_custom_call" | custom-call | tf_op jit(solution)/shard_map/pallas_call | solution.py:408
  72.3 4.2 %all-to-all-done.3.parts_ref = bf16[8,64,128]{2,1,0:T(8,128)(2,1)S(1)} async-done(((bf16[8,64,128]{2,1,0:T(8,128)(2,1)}), bf16[8,64,128]{2,1,0:T(8,128)(2,1)S(1)}, u32[]{:S(2)}, u32[]{:S(2)}) %all-to-all-start.3) | async-done | bytes 131104 | tf_op jit(solution)/shard_map/all_to_all | solution.py:420
  76.5 0.9 %shard_map.182 = (f32[6,64,256]{2,1,0:T(8,128)}, f32[64,128]{1,0:T(8,128)}) custom-call(bf16[8,64,128]{2,1,0:T(8,128)(2,1)S(1)} %all-to-all-done.3.parts_ref, f32[6,64,128]{2,1,0:T(8,128)S(1)} %get-tuple-element.27.first_ref, f32[64,128]{1,0:T(8,128)S(1)} %get-tuple-element.28.nodes_ref, ...), custom_call_target="tpu_custom_call", output_to_operand_aliasing={{0}: (5, {})} | custom-call | tf_op jit(solution)/shard_map/pallas_call | solution.py:421
Async XLA Ops:
  24.8 2.0 %collective-permute-start = (bf16[8,272,128]{2,1,0:T(8,128)(2,1)S(1)}, bf16[8,272,128]{2,1,0:T(8,128)(2,1)S(1)}, u32[]{:S(2)}, u32[]{:S(2)}) collective-permute-start(bf16[8,272,128]{2,1,0:T(8,128)(2,1)S(1)} %get-tuple-element.20.send_ref), channel_id=1, source_target_pairs={{0,1},{1,0},{2,3},{3,2},{4,5},{5,4},{6,7},{7,6},{8,9},{9,8},{10,11... | collective-permute-start | bytes 1671176 | tf_op jit(solution)/shard_map/ppermute | solution.py:383
  56.6 2.6 %collective-permute-start.1 = (bf16[8,256,128]{2,1,0:T(8,128)(2,1)S(1)}, bf16[8,256,128]{2,1,0:T(8,128)(2,1)S(1)}, u32[]{:S(2)}, u32[]{:S(2)}) collective-permute-start(bf16[8,256,128]{2,1,0:T(8,128)(2,1)S(1)} %all_to_all.22.here_ref), channel_id=1, source_target_pairs={{0,1},{1,0},{2,3},{3,2},{4,5},{5,4},{6,7},{7,6},{8,9},{9,8},{10,11... | collective-permute-start | bytes 1572872 | tf_op jit(solution)/shard_map/ppermute | solution.py:397
  56.6 8.6 %collective-permute-start.2 = (bf16[16,384]{1,0:T(8,128)(2,1)S(1)}, bf16[16,384]{1,0:T(8,128)(2,1)S(1)}, u32[]{:S(2)}, u32[]{:S(2)}) collective-permute-start(bf16[16,384]{1,0:T(8,128)(2,1)S(1)} %get-tuple-element.23), channel_id=1, source_target_pairs={{0,127},{1,2},{2,1},{3,4},{4,3},{5,6},{6,5},{7,8},{8,7},{9,10},{10... | collective-permute-start | bytes 36872 | tf_op jit(solution)/shard_map/ppermute | solution.py:375
  59.2 9.6 %copy-start = (f32[6,64,256]{2,1,0:T(8,128)S(1)}, f32[6,64,256]{2,1,0:T(8,128)}, u32[]{:S(2)}) copy-start(f32[6,64,256]{2,1,0:T(8,128)} %fields_ref.3) | copy-start | bytes 1179652
  65.1 3.6 %copy-start.1 = (f32[6,16,64]{2,1,0:T(8,128)S(1)}, f32[6,16,64]{2,1,0:T(8,128)}, u32[]{:S(2)}) copy-start(f32[6,16,64]{2,1,0:T(8,128)} %interp_ref.3) | copy-start | bytes 73732
  65.2 3.6 %copy-start.2 = (f32[3,64,64]{2,1,0:T(8,128)S(1)}, f32[3,64,64]{2,1,0:T(8,128)}, u32[]{:S(2)}) copy-start(f32[3,64,64]{2,1,0:T(8,128)} %diff_ref.1) | copy-start | bytes 147460
  65.2 3.6 %copy-start.3 = (f32[6,64,16]{1,2,0:T(8,128)S(1)}, f32[6,64,16]{1,2,0:T(8,128)}, u32[]{:S(2)}) copy-start(f32[6,64,16]{1,2,0:T(8,128)} %param.21) | copy-start | bytes 73732
  65.2 3.6 %copy-start.4 = (f32[6,6,6]{2,1,0:T(8,128)S(1)}, f32[6,6,6]{2,1,0:T(8,128)}, u32[]{:S(2)}) copy-start(f32[6,6,6]{2,1,0:T(8,128)} %couple_ref.1) | copy-start | bytes 2596
  65.2 3.6 %copy-start.5 = (s32[6,256]{1,0:T(8,128)S(1)}, s32[6,256]{1,0:T(8,128)}, u32[]{:S(2)}) copy-start(s32[6,256]{1,0:T(8,128)} %links_ref.1) | copy-start | bytes 18436
  65.2 3.6 %copy-start.8 = (f32[64]{0:T(128)S(1)}, f32[64]{0:T(128)}, u32[]{:S(2)}) copy-start(f32[64]{0:T(128)} %param.27) | copy-start | bytes 772
  65.2 11.4 %all-to-all-start.3 = ((bf16[8,64,128]{2,1,0:T(8,128)(2,1)}), bf16[8,64,128]{2,1,0:T(8,128)(2,1)S(1)}, u32[]{:S(2)}, u32[]{:S(2)}) async-start(bf16[8,64,128]{2,1,0:T(8,128)(2,1)} %shard_map.180), calls=%async_computation.3 | async-start | bytes 262144 | tf_op jit(solution)/shard_map/all_to_all | solution.py:420
  68.7 0.7 copy-start.6
  68.7 0.7 copy-start.7

commit v10 on v8

--- a/solution.py
+++ b/solution.py
@@ -13,7 +13,7 @@
 AXES = ("y", "z", "xl", "xh", "c")
 VMEM = pl.BlockSpec(memory_space=pltpu.VMEM)
 SMEM = pl.BlockSpec(memory_space=pltpu.SMEM)
-ROW_C, ROW_W, ROW_T, ROWS = 256, 320, 352, 368
+ROW_C, ROW_W, ROW_T, ROWS = 128, 192, 256, 272
 SETS = [
     [((((y * 4 + z) * 2 + (s ^ xh)) * 2 + xh) * 2) + c for z in range(4) for xh in range(2)]
     for y in range(4)
@@ -106,28 +106,22 @@
         weights.append(mm(pick, weight_ref[...]).astype(BF16))
     for i in range(8):
         z, xh = i // 2, i % 2
-        at = 256 * (z // 2)
-        message_ref[i, 0:128, :] = projection_ref[:, at : at + 128]
-        message_ref[i, 128:256, :] = projection_ref[:, at + 128 : at + 256]
+        message_ref[i, 0:128, :] = projection_ref[:, 128 * z : 128 * z + 128]
         message_ref[i, ROW_C : ROW_C + 64, :] = currents
-        message_ref[i, ROW_W : ROW_W + 32, :] = weights[2 * xh + z % 2]
+        message_ref[i, ROW_W : ROW_W + 32, :] = weights[2 * xh]
+        message_ref[i, ROW_W + 32 : ROW_W + 64, :] = weights[2 * xh + 1]
         message_ref[i, ROW_T:ROWS, :] = table
 
 
-def rays_kernel(got_ref, on_ref, keep_ref, send_ref, c_ref, w_ref, p_ref):
-    core, half = lax.axis_index("c"), lax.axis_index("xh")
-    mine = pl.multiple_of(128 * core, 128)
-    theirs = pl.multiple_of(128 * (1 - core), 128)
+def level_weights(got_ref, i, level):
+    return got_ref[i, pl.ds(pl.multiple_of(ROW_W + 32 * level, 32), 32), :].astype(F32)
+
+
+def partial_rays(got_ref, level, out_ref, c_ref, w_ref, p_ref):
     for i in range(8):
-        at = 128 * i
         c_ref[i] = got_ref[i, ROW_C : ROW_C + 64, :].astype(F32)
-        w_ref[i] = got_ref[i, ROW_W : ROW_W + 32, :].astype(F32)
-        p_ref[at : at + 128, 0:128] = got_ref[i, pl.ds(mine, 128), :]
-        p_ref[at : at + 128, 128:256] = got_ref[i, pl.ds(theirs, 128), :]
-    for z in range(4):
-        send_ref[z, 256:272, :] = got_ref[2 * z + half, ROW_T:ROWS, :]
-    for i in range(3):
-        send_ref[4 + i, 256:272, :] = on_ref[:, 128 * i : 128 * i + 128]
+        w_ref[i] = level_weights(got_ref, i, level)
+        p_ref[128 * i : 128 * i + 128, :] = got_ref[i, 0:128, :]
     for high in range(8):
         rows = []
         for t in range(8 * high, 8 * high + 8):
@@ -137,26 +131,31 @@
                 row.append((w_ref[i].reshape(4, 8, 128) * c[None]).reshape(32, 128))
             rows.append(jnp.concatenate(row, axis=1).astype(BF16))
         product = mm(jnp.concatenate(rows, axis=0), p_ref[...])
-        part = [product[32 * t : 32 * t + 32] for t in range(8)]
-        kept = lane_blocks_swapped([x[:, 0:128] for x in part])
-        sent = lane_blocks_swapped([x[:, 128:256].astype(BF16) for x in part])
+        parts = [product[32 * t : 32 * t + 32].astype(out_ref.dtype) for t in range(8)]
+        parts = lane_blocks_swapped(parts)
         for r in range(8):
-            keep_ref[r, 32 * high : 32 * high + 32, :] = kept[r]
-            send_ref[r, 32 * high : 32 * high + 32, :] = sent[r]
-
-
-def joined_kernel(keep_ref, send_ref, came_ref, out_ref, on_ref):
-    has_tables = lax.axis_index("c") == lax.axis_index("z") % 2
-    tables = []
+            out_ref[r, 32 * high : 32 * high + 32, :] = parts[r]
+
+
+def sent_kernel(got_ref, on_ref, send_ref, c_ref, w_ref, p_ref):
+    for i in range(3):
+        send_ref[i, 256:272, :] = on_ref[:, 128 * i : 128 * i + 128]
+    partial_rays(got_ref, 1 - lax.axis_index("c"), send_ref, c_ref, w_ref, p_ref)
+
+
+def kept_kernel(got_ref, keep_ref, table_ref, c_ref, w_ref, p_ref):
+    half = lax.axis_index("xh")
     for z in range(4):
-        here, there = send_ref[z, 256:272, :], came_ref[z, 256:272, :]
-        tables.append(jnp.where(has_tables, here.astype(F32), there.astype(F32)).astype(BF16))
-    tables = jnp.concatenate(tables, axis=0)
+        table_ref[16 * z : 16 * z + 16, :] = got_ref[2 * z + half, ROW_T:ROWS, :]
+    partial_rays(got_ref, lax.axis_index("c"), keep_ref, c_ref, w_ref, p_ref)
+
+
+def joined_kernel(keep_ref, table_ref, came_ref, out_ref, on_ref):
     for r in range(8):
         out_ref[r, 0:256, :] = (keep_ref[r] + came_ref[r, 0:256, :].astype(F32)).astype(BF16)
-        out_ref[r, 256:320, :] = tables
+        out_ref[r, 256:320, :] = table_ref[...]
     for i in range(3):
-        on_ref[:, 128 * i : 128 * i + 128] = came_ref[4 + i, 256:272, :]
+        on_ref[:, 128 * i : 128 * i + 128] = came_ref[i, 256:272, :]
 
 
 def translate_kernel(got_ref, out_ref, h_ref, s_ref):
@@ -193,26 +192,21 @@
         out_ref[r] = incoming
 
 
-def image_kernel(here_ref, there_ref, got_ref, out_ref, p_ref, w_ref, sum_ref):
-    core = lax.axis_index("c")
-    mine = pl.multiple_of(128 * core, 128)
-    theirs = pl.multiple_of(128 * (1 - core), 128)
+def add_images(incoming_ref, got_ref, level, before_ref, sum_ref, p_ref, w_ref):
     for i in range(8):
-        at = 128 * i
-        p_ref[at : at + 128, 0:128] = got_ref[i, pl.ds(mine, 128), :]
-        p_ref[at : at + 128, 128:256] = got_ref[i, pl.ds(theirs, 128), :]
-        w_ref[i] = got_ref[i, ROW_W : ROW_W + 32, :].astype(F32)
+        p_ref[128 * i : 128 * i + 128, :] = got_ref[i, 0:128, :]
+        w_ref[i] = level_weights(got_ref, i, level)
     for chunk in range(2):
         at = 128 * chunk
-        rows = []
-        for ref in (here_ref, there_ref):
-            parts = [ref[r, at : at + 128, :] for r in range(8)]
-            rows.append(jnp.concatenate(lane_blocks_swapped(parts), axis=0))
-        rows = jnp.concatenate(rows, axis=1)
+        parts = [incoming_ref[r, at : at + 128, :] for r in range(8)]
+        rows = jnp.concatenate(lane_blocks_swapped(parts), axis=0)
+        start = sum_ref if chunk > 0 else before_ref
         for i in range(4):
             image = mm(rows, p_ref[256 * i : 256 * i + 256, :], NT)
             weight = [
-                jnp.concatenate([w_ref[2 * i + s, pl.ds(q, 8, stride=0), :] for s in range(2)], axis=1)
+                jnp.concatenate(
+                    [w_ref[2 * i + s, pl.ds(q, 8, stride=0), :] for s in range(2)], axis=1
+                )
                 for q in range(16 * chunk, 16 * chunk + 16)
             ]
             for t in range(8):
@@ -222,9 +216,17 @@
                     total = total + image[at : at + 8] * weight[q]
                 for s in range(2):
                     part = total[:, 128 * s : 128 * s + 128]
-                    if chunk > 0:
-                        part = part + sum_ref[2 * i + s, 8 * t : 8 * t + 8, :]
+                    if start is not None:
+                        part = part + start[2 * i + s, 8 * t : 8 * t + 8, :]
                     sum_ref[2 * i + s, 8 * t : 8 * t + 8, :] = part
+
+
+def near_kernel(here_ref, got_ref, sum_ref, p_ref, w_ref):
+    add_images(here_ref, got_ref, lax.axis_index("c"), None, sum_ref, p_ref, w_ref)
+
+
+def far_kernel(there_ref, got_ref, before_ref, out_ref, p_ref, w_ref, sum_ref):
+    add_images(there_ref, got_ref, 1 - lax.axis_index("c"), before_ref, sum_ref, p_ref, w_ref)
     for i in range(8):
         out_ref[i] = sum_ref[i].astype(BF16)
 
@@ -375,18 +377,22 @@
     anywhere = pl.BlockSpec(memory_space=pl.ANY)
     off_chip = lax.ppermute(off_chip, AXES, across)
     got = lax.all_to_all(message, AXES, 0, 0, axis_index_groups=SETS, tiled=True)
-    keep, send = call(
-        rays_kernel,
-        (vmem((8, 256, 128), F32), vmem((8, 272, 128), BF16)),
-        [VMEM] * 2,
-        (pltpu.VMEM((8, 64, 128), F32), pltpu.VMEM((8, 32, 128), F32), pltpu.VMEM((1024, 256), BF16)),
+    blocks = (pltpu.VMEM((1024, 128), BF16), pltpu.VMEM((8, 32, 128), F32))
+    send = call(
+        sent_kernel, vmem((8, 272, 128), BF16), [VMEM] * 2,
+        (pltpu.VMEM((8, 64, 128), F32),) + blocks[::-1],
     )(held(got), held(on_chip))
     came = lax.ppermute(send, "c", beside)
+    got, send = lax.optimization_barrier((got, send))
+    keep, table = call(
+        kept_kernel, (vmem((8, 256, 128), F32), vmem((64, 128), BF16)), [VMEM],
+        (pltpu.VMEM((8, 64, 128), F32),) + blocks[::-1],
+    )(held(got))
     partial, on_chip = call(
         joined_kernel,
         (vmem((8, 320, 128), BF16), vmem((16, 384), BF16)),
         [VMEM] * 3,
-    )(held(keep), held(send), held(came))
+    )(held(keep), held(table), held(came))
     partial = lax.all_to_all(partial, ("y", "xl"), 0, 0, tiled=True)
     incoming = call(
         translate_kernel,
@@ -396,15 +402,13 @@
     )(held(partial))
     incoming = lax.all_to_all(incoming, ("y", "xl"), 0, 0, tiled=True)
     beyond = lax.ppermute(incoming, "c", beside)
+    near = call(near_kernel, vmem((8, 64, 128), F32), [VMEM] * 2, blocks)(
+        held(incoming), held(got)
+    )
     parts = call(
-        image_kernel,
-        vmem((8, 64, 128), BF16),
-        [VMEM] * 3,
-        (
-            pltpu.VMEM((1024, 256), BF16), pltpu.VMEM((8, 32, 128), F32),
-            pltpu.VMEM((8, 64, 128), F32),
-        ),
-    )(held(incoming), held(beyond), held(got))
+        far_kernel, vmem((8, 64, 128), BF16), [VMEM] * 3,
+        blocks + (pltpu.VMEM((8, 64, 128), F32),),
+    )(held(beyond), held(got), held(near))
     parts, on_chip, off_chip = lax.optimization_barrier((parts, on_chip, off_chip))
     rate, first, nodes, times, factor = call(
         element_kernel,

time: 77.8 us -> 75.7 us (0.973)
  Pallas kernels: 10.2 us -> 13.1 us
  waiting for transfers between devices: 9.68 us -> 6.78 us
  blocking collectives: 49.3 us -> 47.4 us
    pallas_call x2 -> x4, Pallas kernels: 4.17 us -> 6.99 us  [the longest x1 2.35 us: per_device(): call(far_kernel, vmem((8, 64, 128), BF16), [VMEM] * 3, blocks + (pltpu.VM...]
    all_to_all x1, blocking collectives: 21.2 us -> 19.3 us  [per_device(): lax.all_to_all(message, AXES, 0, 0, axis_index_groups=SETS, tiled=True)]
    ppermute x1, waiting for transfers between devices: 1.94 us -> 0.46 us  [per_device(): came = lax.ppermute(send, 'c', beside)]
    ppermute x1, waiting for transfers between devices: 3.53 us -> 2.12 us  [per_device(): off_chip = lax.ppermute(off_chip, AXES, across)]
  transfers between devices with their start and end apart: 4 -> 4, of which waited for: 3 -> 3; matrix products, arithmetic and copies ran while one was open for 0% -> 0% of each run, Pallas kernels for 7% -> 11%
where the time goes in v10:
time: 75.7 us; the launch traced here: 75.3 us
  blocking collectives  47.4 us (63%)
  Pallas kernels  13.1 us (17%)
  waiting for transfers between devices  6.78 us (9%)
  starting transfers between devices  5.96 us (8%)
  between operations  1.44 us (2%)
    all_to_all x1, blocking collectives, per_device(): lax.all_to_all(message, AXES, 0, 0, axis_index_groups=SETS, tiled=True)  19.3 us
    all_to_all x1, blocking collectives, per_device(): partial = lax.all_to_all(partial, ('y', 'xl'), 0, 0, tiled=True)  16.2 us
    all_to_all x1, blocking collectives, per_device(): incoming = lax.all_to_all(incoming, ('y', 'xl'), 0, 0, tiled=True)  12 us
    all_to_all x1, waiting for transfers between devices, per_device(): lax.all_to_all(parts, AXES, 0, 0, axis_index_groups=SETS, tiled=True)  4.2 us
    all_to_all x1, starting transfers between devices, per_device(): lax.all_to_all(parts, AXES, 0, 0, axis_index_groups=SETS, tiled=True)  3.51 us
    pallas_call x1, Pallas kernels, per_device(): call(element_kernel, (shaped((6, 64, 256), F32), vmem((6, 64, 128), F32),...  2.95 us
    ppermute x1, starting transfers between devices, per_device(): off_chip = lax.ppermute(off_chip, AXES, across)  2.35 us
    pallas_call x1, Pallas kernels, per_device(): call(far_kernel, vmem((8, 64, 128), BF16), [VMEM] * 3, blocks + (pltpu.VM...  2.35 us
  transfers between devices with their start and end apart: 4, of which 3 were waited for; matrix products, arithmetic and copies ran while one was open for 0% of the time, Pallas kernels for 11%

profile of v10, /device:TPU:0, one launch (start us, length us, event | category | flops | bytes accessed | tf_op | source)
XLA Modules:
  0.0 75.3 jit_solution(8327678679042941463)
XLA Ops:
  1.3 1.4 %shard_map.176 = (bf16[8,272,128]{2,1,0:T(8,128)(2,1)S(1)}, bf16[16,384]{1,0:T(8,128)(2,1)S(1)}, bf16[16,384]{1,0:T(8,128)(2,1)S(1)}) custom-call(s32[2,16]{1,0:T(2,128)} %send_ref.1, s32[1,1,16]{2,1,0:T(1,128)} %dest_ref.1, s32[1,1]{1,0:T(1,128)S(6)} %copy.21.count_ref, f32[6]{0:T(128)} %coef_ref.1, f32[6,64,256]{2,1,0:T(8,128)} %fields_ref.3, ...), custom_call_target="tpu_custom_call" | custom-call | tf_op jit(solution)/shard_map/pallas_call | solution.py:365
  2.7 19.3 %all_to_all.20.got_ref = bf16[8,272,128]{2,1,0:T(8,128)(2,1)S(1)} all-to-all(bf16[8,272,128]{2,1,0:T(8,128)(2,1)S(1)} %get-tuple-element.18), channel_id=1, replica_groups={{0,6,8,14,16,22,24,30},{1,7,9,15,17,23,25,31},{4,2,12,10,20,18,28,26},{..., dimensions={0} | all-to-all | bytes 1114112 | tf_op jit(solution)/shard_map/all_to_all | solution.py:379
  22.0 1.5 %shard_map.177 = bf16[8,272,128]{2,1,0:T(8,128)(2,1)S(1)} custom-call(bf16[8,272,128]{2,1,0:T(8,128)(2,1)S(1)} %all_to_all.20.got_ref, bf16[16,384]{1,0:T(8,128)(2,1)S(1)} %get-tuple-element.19.on_ref), custom_call_target="tpu_custom_call" | custom-call | tf_op jit(solution)/shard_map/pallas_call | solution.py:381
  23.5 0.1 collective-permute-start
  23.6 1.5 %shard_map.178 = (f32[8,256,128]{2,1,0:T(8,128)S(1)}, bf16[64,128]{1,0:T(8,128)(2,1)S(1)}) custom-call(bf16[8,272,128]{2,1,0:T(8,128)(2,1)S(1)} %all_to_all.20.got_ref), custom_call_target="tpu_custom_call" | custom-call | tf_op jit(solution)/shard_map/pallas_call | solution.py:387
  25.0 0.5 collective-permute-done.came_ref
  25.5 0.1 shard_map.179
  25.6 16.2 %all_to_all.21.got_ref = bf16[8,320,128]{2,1,0:T(8,128)(2,1)S(1)} all-to-all(bf16[8,320,128]{2,1,0:T(8,128)(2,1)S(1)} %get-tuple-element.23), channel_id=1, replica_groups=mesh['y'=4,'z'=4,'xl'=2,'xh'=2,'c'=2] {'y','xl'}, dimensions={0} | all-to-all | bytes 1310720 | tf_op jit(solution)/shard_map/all_to_all | solution.py:396
  41.8 0.7 shard_map.180
  42.5 12.0 %all_to_all.22.here_ref = bf16[8,256,128]{2,1,0:T(8,128)(2,1)S(1)} all-to-all(bf16[8,256,128]{2,1,0:T(8,128)(2,1)S(1)} %shard_map.180), channel_id=1, replica_groups=mesh['y'=4,'z'=4,'xl'=2,'xh'=2,'c'=2] {'y','xl'}, dimensions={0} | all-to-all | bytes 1048576 | tf_op jit(solution)/shard_map/all_to_all | solution.py:403
  54.5 0.0 collective-permute-start.1
  54.5 2.4 %collective-permute-start.2 = (bf16[16,384]{1,0:T(8,128)(2,1)S(1)}, bf16[16,384]{1,0:T(8,128)(2,1)S(1)}, u32[]{:S(2)}, u32[]{:S(2)}) collective-permute-start(bf16[16,384]{1,0:T(8,128)(2,1)S(1)} %get-tuple-element.25), channel_id=1, source_target_pairs={{0,127},{1,2},{2,1},{3,4},{4,3},{5,6},{6,5},{7,8},{8,7},{9,10},{10... | collective-permute-start | bytes 36872 | tf_op jit(solution)/shard_map/ppermute | solution.py:378
  56.8 1.7 %shard_map.181.before_ref = f32[8,64,128]{2,1,0:T(8,128)S(1)} custom-call(bf16[8,256,128]{2,1,0:T(8,128)(2,1)S(1)} %all_to_all.22.here_ref, bf16[8,272,128]{2,1,0:T(8,128)(2,1)S(1)} %all_to_all.20.got_ref), custom_call_target="tpu_custom_call" | custom-call | tf_op jit(solution)/shard_map/pallas_call | solution.py:405
  58.5 0.0 collective-permute-done.1.there_ref
  58.5 0.0 copy-start
  58.6 2.3 %shard_map.182 = bf16[8,64,128]{2,1,0:T(8,128)(2,1)} custom-call(bf16[8,256,128]{2,1,0:T(8,128)(2,1)S(1)} %collective-permute-done.1.there_ref, bf16[8,272,128]{2,1,0:T(8,128)(2,1)S(1)} %all_to_all.20.got_ref, f32[8,64,128]{2,1,0:T(8,128)S(1)} %shard_map.181.before_ref), custom_call_target="tpu_custom_call" | custom-call | tf_op jit(solution)/shard_map/pallas_call | solution.py:408
  60.9 2.1 %collective-permute-done.2.off_ref = bf16[16,384]{1,0:T(8,128)(2,1)S(1)} collective-permute-done((bf16[16,384]{1,0:T(8,128)(2,1)S(1)}, bf16[16,384]{1,0:T(8,128)(2,1)S(1)}, u32[]{:S(2)}, u32[]{:S(2)}) %collective-permute-start.2) | collective-permute-done | bytes 12320 | tf_op jit(solution)/shard_map/ppermute | solution.py:378
  63.0 0.0 copy-start.1
  63.0 0.0 copy-start.2
  63.0 0.0 copy-start.3
  63.0 0.0 copy-start.4
  63.0 0.0 copy-start.5
  63.1 0.0 copy-start.8
  63.1 3.5 %all-to-all-start.3 = ((bf16[8,64,128]{2,1,0:T(8,128)(2,1)}), bf16[8,64,128]{2,1,0:T(8,128)(2,1)S(1)}, u32[]{:S(2)}, u32[]{:S(2)}) async-start(bf16[8,64,128]{2,1,0:T(8,128)(2,1)} %shard_map.182), calls=%async_computation.3 | async-start | bytes 262144 | tf_op jit(solution)/shard_map/all_to_all | solution.py:425
  66.6 0.0 copy-start.6
  66.6 0.0 copy-start.7
  66.6 0.0 copy-done
  66.6 0.0 copy-done.1
  66.6 0.0 copy-done.2
  66.6 0.0 copy-done.3
  66.6 0.0 copy-done.4
  66.7 0.0 copy-done.5
  66.7 0.0 copy-done.8
  66.7 0.6 copy-done.6
  67.3 0.0 copy-done.7
  67.3 2.9 %shard_map.183 = (f32[6,64,256]{2,1,0:T(8,128)}, f32[6,64,128]{2,1,0:T(8,128)S(1)}, f32[64,128]{1,0:T(8,128)S(1)}, f32[64,128]{1,0:T(8,128)S(1)}, f32[6,8,128]{2,1,0:T(8,128)S(1)}) custom-call(f32[6,6,6]{2,1,0:T(8,128)S(1)} %copy-done.4, f32[6]{0:T(128)S(1)} %copy-done.7, f32[6,64,256]{2,1,0:T(8,128)S(1)} %copy-done, f32[1,256]{1,0:T(1,128)S(1)} %bitcast.4, ...), custom_call_target="tpu_custom_call" | custom-call | tf_op jit(solution)/shard_map/pallas_call | solution.py:413
  70.2 4.2 %all-to-all-done.3.parts_ref = bf16[8,64,128]{2,1,0:T(8,128)(2,1)S(1)} async-done(((bf16[8,64,128]{2,1,0:T(8,128)(2,1)}), bf16[8,64,128]{2,1,0:T(8,128)(2,1)S(1)}, u32[]{:S(2)}, u32[]{:S(2)}) %all-to-all-start.3) | async-done | bytes 131104 | tf_op jit(solution)/shard_map/all_to_all | solution.py:425
  74.4 0.9 %shard_map.184 = (f32[6,64,256]{2,1,0:T(8,128)}, f32[64,128]{1,0:T(8,128)}) custom-call(bf16[8,64,128]{2,1,0:T(8,128)(2,1)S(1)} %all-to-all-done.3.parts_ref, f32[6,64,128]{2,1,0:T(8,128)S(1)} %get-tuple-element.29.first_ref, f32[64,128]{1,0:T(8,128)S(1)} %get-tuple-element.30.nodes_ref, ...), custom_call_target="tpu_custom_call", output_to_operand_aliasing={{0}: (5, {})} | custom-call | tf_op jit(solution)/shard_map/pallas_call | solution.py:426
Async XLA Ops:
  23.5 2.0 %collective-permute-start = (bf16[8,272,128]{2,1,0:T(8,128)(2,1)S(1)}, bf16[8,272,128]{2,1,0:T(8,128)(2,1)S(1)}, u32[]{:S(2)}, u32[]{:S(2)}) collective-permute-start(bf16[8,272,128]{2,1,0:T(8,128)(2,1)S(1)} %shard_map.177), channel_id=1, source_target_pairs={{0,1},{1,0},{2,3},{3,2},{4,5},{5,4},{6,7},{7,6},{8,9},{9,8},{10,11... | collective-permute-start | bytes 1671176 | tf_op jit(solution)/shard_map/ppermute | solution.py:385
  54.5 4.1 %collective-permute-start.1 = (bf16[8,256,128]{2,1,0:T(8,128)(2,1)S(1)}, bf16[8,256,128]{2,1,0:T(8,128)(2,1)S(1)}, u32[]{:S(2)}, u32[]{:S(2)}) collective-permute-start(bf16[8,256,128]{2,1,0:T(8,128)(2,1)S(1)} %all_to_all.22.here_ref), channel_id=1, source_target_pairs={{0,1},{1,0},{2,3},{3,2},{4,5},{5,4},{6,7},{7,6},{8,9},{9,8},{10,11... | collective-permute-start | bytes 1572872 | tf_op jit(solution)/shard_map/ppermute | solution.py:404
  54.5 8.6 %collective-permute-start.2 = (bf16[16,384]{1,0:T(8,128)(2,1)S(1)}, bf16[16,384]{1,0:T(8,128)(2,1)S(1)}, u32[]{:S(2)}, u32[]{:S(2)}) collective-permute-start(bf16[16,384]{1,0:T(8,128)(2,1)S(1)} %get-tuple-element.25), channel_id=1, source_target_pairs={{0,127},{1,2},{2,1},{3,4},{4,3},{5,6},{6,5},{7,8},{8,7},{9,10},{10... | collective-permute-start | bytes 36872 | tf_op jit(solution)/shard_map/ppermute | solution.py:378
  58.5 8.1 %copy-start = (f32[6,64,256]{2,1,0:T(8,128)S(1)}, f32[6,64,256]{2,1,0:T(8,128)}, u32[]{:S(2)}) copy-start(f32[6,64,256]{2,1,0:T(8,128)} %fields_ref.3) | copy-start | bytes 1179652
  63.0 3.6 %copy-start.1 = (f32[6,16,64]{2,1,0:T(8,128)S(1)}, f32[6,16,64]{2,1,0:T(8,128)}, u32[]{:S(2)}) copy-start(f32[6,16,64]{2,1,0:T(8,128)} %interp_ref.3) | copy-start | bytes 73732
  63.0 3.6 %copy-start.2 = (f32[3,64,64]{2,1,0:T(8,128)S(1)}, f32[3,64,64]{2,1,0:T(8,128)}, u32[]{:S(2)}) copy-start(f32[3,64,64]{2,1,0:T(8,128)} %diff_ref.1) | copy-start | bytes 147460
  63.0 3.6 %copy-start.3 = (f32[6,64,16]{1,2,0:T(8,128)S(1)}, f32[6,64,16]{1,2,0:T(8,128)}, u32[]{:S(2)}) copy-start(f32[6,64,16]{1,2,0:T(8,128)} %param.21) | copy-start | bytes 73732
  63.0 3.6 %copy-start.4 = (f32[6,6,6]{2,1,0:T(8,128)S(1)}, f32[6,6,6]{2,1,0:T(8,128)}, u32[]{:S(2)}) copy-start(f32[6,6,6]{2,1,0:T(8,128)} %couple_ref.1) | copy-start | bytes 2596
  63.0 3.6 %copy-start.5 = (s32[6,256]{1,0:T(8,128)S(1)}, s32[6,256]{1,0:T(8,128)}, u32[]{:S(2)}) copy-start(s32[6,256]{1,0:T(8,128)} %links_ref.1) | copy-start | bytes 18436
  63.1 3.6 %copy-start.8 = (f32[64]{0:T(128)S(1)}, f32[64]{0:T(128)}, u32[]{:S(2)}) copy-start(f32[64]{0:T(128)} %param.27) | copy-start | bytes 772
  63.1 11.4 %all-to-all-start.3 = ((bf16[8,64,128]{2,1,0:T(8,128)(2,1)}), bf16[8,64,128]{2,1,0:T(8,128)(2,1)S(1)}, u32[]{:S(2)}, u32[]{:S(2)}) async-start(bf16[8,64,128]{2,1,0:T(8,128)(2,1)} %shard_map.182), calls=%async_computation.3 | async-start | bytes 262144 | tf_op jit(solution)/shard_map/all_to_all | solution.py:425
  66.6 0.7 copy-start.6
  66.6 0.7 copy-start.7

commit v11 on v10

--- a/solution.py
+++ b/solution.py
@@ -162,7 +162,7 @@
     total = got_ref[0, 0:256, :].astype(F32)
     for r in range(1, 8):
         total = total + got_ref[r, 0:256, :].astype(F32)
-    rays = total.astype(BF16).astype(F32)
+    rays = total.astype(BF16)
     for r in range(8):
         y, xl = r // 2, r % 2
         for z in range(4):
@@ -178,9 +178,9 @@
         rows = [by_high[t]]
         for b in range(1, 8):
             here = pltpu.roll(by_high[t], 16 * b, 1)
-            before = pltpu.roll(by_high[t - 1], 16 * b, 1) if t > 0 else jnp.zeros((32, 128), F32)
+            before = pltpu.roll(by_high[t - 1], 16 * b, 1) if t > 0 else jnp.zeros((32, 128), BF16)
             rows.append(jnp.where(lane < 16 * b, before, here))
-        columns.append(jnp.concatenate(rows, axis=0).astype(BF16))
+        columns.append(jnp.concatenate(rows, axis=0))
     lagged = [mm(table, column, TN) for column in columns]
     for t in range(8):
         incoming = lagged[t][0:32]
@@ -192,7 +192,7 @@
         out_ref[r] = incoming
 
 
-def add_images(incoming_ref, got_ref, level, before_ref, sum_ref, p_ref, w_ref):
+def add_images(incoming_ref, got_ref, level, before_ref, sum_ref, p_ref, w_ref, done=None):
     for i in range(8):
         p_ref[128 * i : 128 * i + 128, :] = got_ref[i, 0:128, :]
         w_ref[i] = level_weights(got_ref, i, level)
@@ -219,16 +219,29 @@
                     if start is not None:
                         part = part + start[2 * i + s, 8 * t : 8 * t + 8, :]
                     sum_ref[2 * i + s, 8 * t : 8 * t + 8, :] = part
+            if done is not None and chunk == 1:
+                done(i)
 
 
 def near_kernel(here_ref, got_ref, sum_ref, p_ref, w_ref):
     add_images(here_ref, got_ref, lax.axis_index("c"), None, sum_ref, p_ref, w_ref)
 
 
-def far_kernel(there_ref, got_ref, before_ref, out_ref, p_ref, w_ref, sum_ref):
-    add_images(there_ref, got_ref, 1 - lax.axis_index("c"), before_ref, sum_ref, p_ref, w_ref)
-    for i in range(8):
-        out_ref[i] = sum_ref[i].astype(BF16)
+def far_kernel(
+    there_ref, got_ref, before_ref, out_ref, p_ref, w_ref, sum_ref, stage_ref, sems,
+):
+    copies = []
+
+    def done(i):
+        at = pl.ds(2 * i, 2)
+        stage_ref[at] = sum_ref[at].astype(BF16)
+        copies.append(pltpu.make_async_copy(stage_ref.at[at], out_ref.at[at], sems.at[i]))
+        copies[-1].start()
+
+    level = 1 - lax.axis_index("c")
+    add_images(there_ref, got_ref, level, before_ref, sum_ref, p_ref, w_ref, done)
+    for copy in copies:
+        copy.wait()
 
 
 def element_kernel(
@@ -406,8 +419,12 @@
         held(incoming), held(got)
     )
     parts = call(
-        far_kernel, vmem((8, 64, 128), BF16), [VMEM] * 3,
-        blocks + (pltpu.VMEM((8, 64, 128), F32),),
+        far_kernel, shaped((8, 64, 128), BF16), [VMEM] * 3,
+        blocks + (
+            pltpu.VMEM((8, 64, 128), F32), pltpu.VMEM((8, 64, 128), BF16),
+            pltpu.SemaphoreType.DMA((4,)),
+        ),
+        out_specs=anywhere,
     )(held(beyond), held(got), held(near))
     parts, on_chip, off_chip = lax.optimization_barrier((parts, on_chip, off_chip))
     rate, first, nodes, times, factor = call(

time: 75.7 us -> 75.7 us (level)
  no operation moved by 1% of the time
where the time goes in v11:
time: 75.7 us; the launch traced here: 75.3 us
  blocking collectives  47.4 us (63%)
  Pallas kernels  13.1 us (17%)
  waiting for transfers between devices  6.74 us (9%)
  starting transfers between devices  5.96 us (8%)
  between operations  1.45 us (2%)
    all_to_all x1, blocking collectives, per_device(): lax.all_to_all(message, AXES, 0, 0, axis_index_groups=SETS, tiled=True)  19.3 us
    all_to_all x1, blocking collectives, per_device(): partial = lax.all_to_all(partial, ('y', 'xl'), 0, 0, tiled=True)  16.2 us
    all_to_all x1, blocking collectives, per_device(): incoming = lax.all_to_all(incoming, ('y', 'xl'), 0, 0, tiled=True)  12 us
    all_to_all x1, waiting for transfers between devices, per_device(): lax.all_to_all(parts, AXES, 0, 0, axis_index_groups=SETS, tiled=True)  4.2 us
    all_to_all x1, starting transfers between devices, per_device(): lax.all_to_all(parts, AXES, 0, 0, axis_index_groups=SETS, tiled=True)  3.51 us
    pallas_call x1, Pallas kernels, per_device(): call(element_kernel, (shaped((6, 64, 256), F32), vmem((6, 64, 128), F32),...  2.95 us
    pallas_call x1, Pallas kernels, per_device(): call(far_kernel, shaped((8, 64, 128), BF16), [VMEM] * 3, blocks + (pltpu....  2.38 us
    ppermute x1, starting transfers between devices, per_device(): off_chip = lax.ppermute(off_chip, AXES, across)  2.36 us
  transfers between devices with their start and end apart: 4, of which 3 were waited for; matrix products, arithmetic and copies ran while one was open for 0% of the time, Pallas kernels for 11%

profile of v11, /device:TPU:0, one launch (start us, length us, event | category | flops | bytes accessed | tf_op | source)
XLA Modules:
  0.0 75.3 jit_solution(989507228826849612)
XLA Ops:
  1.3 1.4 %shard_map.176 = (bf16[8,272,128]{2,1,0:T(8,128)(2,1)S(1)}, bf16[16,384]{1,0:T(8,128)(2,1)S(1)}, bf16[16,384]{1,0:T(8,128)(2,1)S(1)}) custom-call(s32[2,16]{1,0:T(2,128)} %send_ref.1, s32[1,1,16]{2,1,0:T(1,128)} %dest_ref.1, s32[1,1]{1,0:T(1,128)S(6)} %copy.21.count_ref, f32[6]{0:T(128)} %coef_ref.1, f32[6,64,256]{2,1,0:T(8,128)} %fields_ref.3, ...), custom_call_target="tpu_custom_call" | custom-call | tf_op jit(solution)/shard_map/pallas_call | solution.py:378
  2.7 19.3 %all_to_all.20.got_ref = bf16[8,272,128]{2,1,0:T(8,128)(2,1)S(1)} all-to-all(bf16[8,272,128]{2,1,0:T(8,128)(2,1)S(1)} %get-tuple-element.18), channel_id=1, replica_groups={{0,6,8,14,16,22,24,30},{1,7,9,15,17,23,25,31},{4,2,12,10,20,18,28,26},{..., dimensions={0} | all-to-all | bytes 1114112 | tf_op jit(solution)/shard_map/all_to_all | solution.py:392
  22.0 1.5 %shard_map.177 = bf16[8,272,128]{2,1,0:T(8,128)(2,1)S(1)} custom-call(bf16[8,272,128]{2,1,0:T(8,128)(2,1)S(1)} %all_to_all.20.got_ref, bf16[16,384]{1,0:T(8,128)(2,1)S(1)} %get-tuple-element.19.on_ref), custom_call_target="tpu_custom_call" | custom-call | tf_op jit(solution)/shard_map/pallas_call | solution.py:394
  23.5 0.1 collective-permute-start
  23.6 1.5 %shard_map.178 = (f32[8,256,128]{2,1,0:T(8,128)S(1)}, bf16[64,128]{1,0:T(8,128)(2,1)S(1)}) custom-call(bf16[8,272,128]{2,1,0:T(8,128)(2,1)S(1)} %all_to_all.20.got_ref), custom_call_target="tpu_custom_call" | custom-call | tf_op jit(solution)/shard_map/pallas_call | solution.py:400
  25.0 0.5 collective-permute-done.came_ref
  25.5 0.1 shard_map.179
  25.6 16.2 %all_to_all.21.got_ref = bf16[8,320,128]{2,1,0:T(8,128)(2,1)S(1)} all-to-all(bf16[8,320,128]{2,1,0:T(8,128)(2,1)S(1)} %get-tuple-element.23), channel_id=1, replica_groups=mesh['y'=4,'z'=4,'xl'=2,'xh'=2,'c'=2] {'y','xl'}, dimensions={0} | all-to-all | bytes 1310720 | tf_op jit(solution)/shard_map/all_to_all | solution.py:409
  41.8 0.7 shard_map.180
  42.5 12.0 %all_to_all.22.here_ref = bf16[8,256,128]{2,1,0:T(8,128)(2,1)S(1)} all-to-all(bf16[8,256,128]{2,1,0:T(8,128)(2,1)S(1)} %shard_map.180), channel_id=1, replica_groups=mesh['y'=4,'z'=4,'xl'=2,'xh'=2,'c'=2] {'y','xl'}, dimensions={0} | all-to-all | bytes 1048576 | tf_op jit(solution)/shard_map/all_to_all | solution.py:416
  54.5 0.0 collective-permute-start.1
  54.5 2.4 %collective-permute-start.2 = (bf16[16,384]{1,0:T(8,128)(2,1)S(1)}, bf16[16,384]{1,0:T(8,128)(2,1)S(1)}, u32[]{:S(2)}, u32[]{:S(2)}) collective-permute-start(bf16[16,384]{1,0:T(8,128)(2,1)S(1)} %get-tuple-element.25), channel_id=1, source_target_pairs={{0,127},{1,2},{2,1},{3,4},{4,3},{5,6},{6,5},{7,8},{8,7},{9,10},{10... | collective-permute-start | bytes 36872 | tf_op jit(solution)/shard_map/ppermute | solution.py:391
  56.8 1.7 %shard_map.181.before_ref = f32[8,64,128]{2,1,0:T(8,128)S(1)} custom-call(bf16[8,256,128]{2,1,0:T(8,128)(2,1)S(1)} %all_to_all.22.here_ref, bf16[8,272,128]{2,1,0:T(8,128)(2,1)S(1)} %all_to_all.20.got_ref), custom_call_target="tpu_custom_call" | custom-call | tf_op jit(solution)/shard_map/pallas_call | solution.py:418
  58.5 0.0 collective-permute-done.1.there_ref
  58.5 0.0 copy-start
  58.6 2.4 %shard_map.182 = bf16[8,64,128]{2,1,0:T(8,128)(2,1)} custom-call(bf16[8,256,128]{2,1,0:T(8,128)(2,1)S(1)} %collective-permute-done.1.there_ref, bf16[8,272,128]{2,1,0:T(8,128)(2,1)S(1)} %all_to_all.20.got_ref, f32[8,64,128]{2,1,0:T(8,128)S(1)} %shard_map.181.before_ref), custom_call_target="tpu_custom_call" | custom-call | tf_op jit(solution)/shard_map/pallas_call | solution.py:421
  60.9 2.1 %collective-permute-done.2.off_ref = bf16[16,384]{1,0:T(8,128)(2,1)S(1)} collective-permute-done((bf16[16,384]{1,0:T(8,128)(2,1)S(1)}, bf16[16,384]{1,0:T(8,128)(2,1)S(1)}, u32[]{:S(2)}, u32[]{:S(2)}) %collective-permute-start.2) | collective-permute-done | bytes 12320 | tf_op jit(solution)/shard_map/ppermute | solution.py:391
  63.0 0.0 copy-start.1
  63.0 0.0 copy-start.2
  63.0 0.0 copy-start.3
  63.0 0.0 copy-start.4
  63.0 0.0 copy-start.5
  63.0 0.0 copy-start.8
  63.1 3.5 %all-to-all-start.3 = ((bf16[8,64,128]{2,1,0:T(8,128)(2,1)}), bf16[8,64,128]{2,1,0:T(8,128)(2,1)S(1)}, u32[]{:S(2)}, u32[]{:S(2)}) async-start(bf16[8,64,128]{2,1,0:T(8,128)(2,1)} %shard_map.182), calls=%async_computation.3 | async-start | bytes 262144 | tf_op jit(solution)/shard_map/all_to_all | solution.py:442
  66.6 0.0 copy-start.6
  66.6 0.0 copy-start.7
  66.6 0.0 copy-done
  66.6 0.0 copy-done.1
  66.6 0.0 copy-done.2
  66.6 0.0 copy-done.3
  66.6 0.0 copy-done.4
  66.7 0.0 copy-done.5
  66.7 0.0 copy-done.8
  66.7 0.6 copy-done.6
  67.3 0.0 copy-done.7
  67.3 2.9 %shard_map.183 = (f32[6,64,256]{2,1,0:T(8,128)}, f32[6,64,128]{2,1,0:T(8,128)S(1)}, f32[64,128]{1,0:T(8,128)S(1)}, f32[64,128]{1,0:T(8,128)S(1)}, f32[6,8,128]{2,1,0:T(8,128)S(1)}) custom-call(f32[6,6,6]{2,1,0:T(8,128)S(1)} %copy-done.4, f32[6]{0:T(128)S(1)} %copy-done.7, f32[6,64,256]{2,1,0:T(8,128)S(1)} %copy-done, f32[1,256]{1,0:T(1,128)S(1)} %bitcast.4, ...), custom_call_target="tpu_custom_call" | custom-call | tf_op jit(solution)/shard_map/pallas_call | solution.py:430
  70.2 4.2 %all-to-all-done.3.parts_ref = bf16[8,64,128]{2,1,0:T(8,128)(2,1)S(1)} async-done(((bf16[8,64,128]{2,1,0:T(8,128)(2,1)}), bf16[8,64,128]{2,1,0:T(8,128)(2,1)S(1)}, u32[]{:S(2)}, u32[]{:S(2)}) %all-to-all-start.3) | async-done | bytes 131104 | tf_op jit(solution)/shard_map/all_to_all | solution.py:442
  74.4 0.9 %shard_map.184 = (f32[6,64,256]{2,1,0:T(8,128)}, f32[64,128]{1,0:T(8,128)}) custom-call(bf16[8,64,128]{2,1,0:T(8,128)(2,1)S(1)} %all-to-all-done.3.parts_ref, f32[6,64,128]{2,1,0:T(8,128)S(1)} %get-tuple-element.29.first_ref, f32[64,128]{1,0:T(8,128)S(1)} %get-tuple-element.30.nodes_ref, ...), custom_call_target="tpu_custom_call", output_to_operand_aliasing={{0}: (5, {})} | custom-call | tf_op jit(solution)/shard_map/pallas_call | solution.py:443
Async XLA Ops:
  23.5 2.0 %collective-permute-start = (bf16[8,272,128]{2,1,0:T(8,128)(2,1)S(1)}, bf16[8,272,128]{2,1,0:T(8,128)(2,1)S(1)}, u32[]{:S(2)}, u32[]{:S(2)}) collective-permute-start(bf16[8,272,128]{2,1,0:T(8,128)(2,1)S(1)} %shard_map.177), channel_id=1, source_target_pairs={{0,1},{1,0},{2,3},{3,2},{4,5},{5,4},{6,7},{7,6},{8,9},{9,8},{10,11... | collective-permute-start | bytes 1671176 | tf_op jit(solution)/shard_map/ppermute | solution.py:398
  54.5 4.1 %collective-permute-start.1 = (bf16[8,256,128]{2,1,0:T(8,128)(2,1)S(1)}, bf16[8,256,128]{2,1,0:T(8,128)(2,1)S(1)}, u32[]{:S(2)}, u32[]{:S(2)}) collective-permute-start(bf16[8,256,128]{2,1,0:T(8,128)(2,1)S(1)} %all_to_all.22.here_ref), channel_id=1, source_target_pairs={{0,1},{1,0},{2,3},{3,2},{4,5},{5,4},{6,7},{7,6},{8,9},{9,8},{10,11... | collective-permute-start | bytes 1572872 | tf_op jit(solution)/shard_map/ppermute | solution.py:417
  54.5 8.6 %collective-permute-start.2 = (bf16[16,384]{1,0:T(8,128)(2,1)S(1)}, bf16[16,384]{1,0:T(8,128)(2,1)S(1)}, u32[]{:S(2)}, u32[]{:S(2)}) collective-permute-start(bf16[16,384]{1,0:T(8,128)(2,1)S(1)} %get-tuple-element.25), channel_id=1, source_target_pairs={{0,127},{1,2},{2,1},{3,4},{4,3},{5,6},{6,5},{7,8},{8,7},{9,10},{10... | collective-permute-start | bytes 36872 | tf_op jit(solution)/shard_map/ppermute | solution.py:391
  58.5 8.1 %copy-start = (f32[6,64,256]{2,1,0:T(8,128)S(1)}, f32[6,64,256]{2,1,0:T(8,128)}, u32[]{:S(2)}) copy-start(f32[6,64,256]{2,1,0:T(8,128)} %fields_ref.3) | copy-start | bytes 1179652
  63.0 3.6 %copy-start.1 = (f32[6,16,64]{2,1,0:T(8,128)S(1)}, f32[6,16,64]{2,1,0:T(8,128)}, u32[]{:S(2)}) copy-start(f32[6,16,64]{2,1,0:T(8,128)} %interp_ref.3) | copy-start | bytes 73732
  63.0 3.6 %copy-start.2 = (f32[3,64,64]{2,1,0:T(8,128)S(1)}, f32[3,64,64]{2,1,0:T(8,128)}, u32[]{:S(2)}) copy-start(f32[3,64,64]{2,1,0:T(8,128)} %diff_ref.1) | copy-start | bytes 147460
  63.0 3.6 %copy-start.3 = (f32[6,64,16]{1,2,0:T(8,128)S(1)}, f32[6,64,16]{1,2,0:T(8,128)}, u32[]{:S(2)}) copy-start(f32[6,64,16]{1,2,0:T(8,128)} %param.21) | copy-start | bytes 73732
  63.0 3.6 %copy-start.4 = (f32[6,6,6]{2,1,0:T(8,128)S(1)}, f32[6,6,6]{2,1,0:T(8,128)}, u32[]{:S(2)}) copy-start(f32[6,6,6]{2,1,0:T(8,128)} %couple_ref.1) | copy-start | bytes 2596
  63.0 3.6 %copy-start.5 = (s32[6,256]{1,0:T(8,128)S(1)}, s32[6,256]{1,0:T(8,128)}, u32[]{:S(2)}) copy-start(s32[6,256]{1,0:T(8,128)} %links_ref.1) | copy-start | bytes 18436
  63.0 3.6 %copy-start.8 = (f32[64]{0:T(128)S(1)}, f32[64]{0:T(128)}, u32[]{:S(2)}) copy-start(f32[64]{0:T(128)} %param.27) | copy-start | bytes 772
  63.1 11.4 %all-to-all-start.3 = ((bf16[8,64,128]{2,1,0:T(8,128)(2,1)}), bf16[8,64,128]{2,1,0:T(8,128)(2,1)S(1)}, u32[]{:S(2)}, u32[]{:S(2)}) async-start(bf16[8,64,128]{2,1,0:T(8,128)(2,1)} %shard_map.182), calls=%async_computation.3 | async-start | bytes 262144 | tf_op jit(solution)/shard_map/all_to_all | solution.py:442
  66.6 0.7 copy-start.6
  66.6 0.7 copy-start.7

commit v12 on v10

--- a/solution.py
+++ b/solution.py
@@ -119,8 +119,8 @@
 
 def partial_rays(got_ref, level, out_ref, c_ref, w_ref, p_ref):
     for i in range(8):
-        c_ref[i] = got_ref[i, ROW_C : ROW_C + 64, :].astype(F32)
-        w_ref[i] = level_weights(got_ref, i, level)
+        c_ref[i, 0:64, :] = got_ref[i, ROW_C : ROW_C + 64, :].astype(F32)
+        w_ref[i, 0:32, :] = level_weights(got_ref, i, level)
         p_ref[128 * i : 128 * i + 128, :] = got_ref[i, 0:128, :]
     for high in range(8):
         rows = []
@@ -128,7 +128,7 @@
             row = []
             for i in range(8):
                 c = c_ref[i, pl.ds(t, 8, stride=0), :]
-                row.append((w_ref[i].reshape(4, 8, 128) * c[None]).reshape(32, 128))
+                row.append((w_ref[i, 0:32, :].reshape(4, 8, 128) * c[None]).reshape(32, 128))
             rows.append(jnp.concatenate(row, axis=1).astype(BF16))
         product = mm(jnp.concatenate(rows, axis=0), p_ref[...])
         parts = [product[32 * t : 32 * t + 32].astype(out_ref.dtype) for t in range(8)]
@@ -170,7 +170,7 @@
             tile = got_ref[r, 256 + 16 * z : 272 + 16 * z, :].astype(F32)
             for h in range(2):
                 h_ref[h, pl.ds(patch, 8, stride=32), :] = tile[8 * h : 8 * h + 8]
-    table = jnp.concatenate([h_ref[0], h_ref[1]], axis=1).astype(BF16)
+    table = jnp.concatenate([h_ref[0, 0:256, :], h_ref[1, 0:256, :]], axis=1).astype(BF16)
     by_high = [rays[32 * t : 32 * t + 32] for t in range(8)]
     lane = iota((32, 128), 1)
     columns = []
@@ -187,7 +187,7 @@
         for a in range(1, t + 1):
             incoming = incoming + lagged[t - a][32 * a : 32 * a + 32]
         s_ref[pl.ds(t, 32, stride=8), :] = incoming
-    incoming = s_ref[...].astype(BF16)
+    incoming = s_ref[0:256, :].astype(BF16)
     for r in range(8):
         out_ref[r] = incoming
 
@@ -195,7 +195,7 @@
 def add_images(incoming_ref, got_ref, level, before_ref, sum_ref, p_ref, w_ref):
     for i in range(8):
         p_ref[128 * i : 128 * i + 128, :] = got_ref[i, 0:128, :]
-        w_ref[i] = level_weights(got_ref, i, level)
+        w_ref[i, 0:32, :] = level_weights(got_ref, i, level)
     for chunk in range(2):
         at = 128 * chunk
         parts = [incoming_ref[r, at : at + 128, :] for r in range(8)]
@@ -318,7 +318,7 @@
     total = total * jnp.float32(1.0 / np.sqrt(np.float32(512)))
     for t in range(8):
         field_ref[pl.ds(t, 8, stride=8), :] = total[8 * t : 8 * t + 8]
-    copies = [pltpu.make_async_copy(field_ref, field_out, sems.at[6])]
+    copies = [pltpu.make_async_copy(field_ref.at[pl.ds(0, 64)], field_out, sems.at[6])]
     copies[0].start()
     now = jnp.sum(times_ref[...] * total, axis=0, keepdims=True)
     collect = one_hot(iota((256, 128), 0) % 128 // 16 == iota((256, 128), 1), BF16)
@@ -377,16 +377,16 @@
     anywhere = pl.BlockSpec(memory_space=pl.ANY)
     off_chip = lax.ppermute(off_chip, AXES, across)
     got = lax.all_to_all(message, AXES, 0, 0, axis_index_groups=SETS, tiled=True)
-    blocks = (pltpu.VMEM((1024, 128), BF16), pltpu.VMEM((8, 32, 128), F32))
+    blocks = (pltpu.VMEM((1024, 128), BF16), pltpu.VMEM((8, 40, 128), F32))
     send = call(
         sent_kernel, vmem((8, 272, 128), BF16), [VMEM] * 2,
-        (pltpu.VMEM((8, 64, 128), F32),) + blocks[::-1],
+        (pltpu.VMEM((8, 72, 128), F32),) + blocks[::-1],
     )(held(got), held(on_chip))
     came = lax.ppermute(send, "c", beside)
     got, send = lax.optimization_barrier((got, send))
     keep, table = call(
         kept_kernel, (vmem((8, 256, 128), F32), vmem((64, 128), BF16)), [VMEM],
-        (pltpu.VMEM((8, 64, 128), F32),) + blocks[::-1],
+        (pltpu.VMEM((8, 72, 128), F32),) + blocks[::-1],
     )(held(got))
     partial, on_chip = call(
         joined_kernel,
@@ -398,7 +398,7 @@
         translate_kernel,
         vmem((8, 256, 128), BF16),
         [VMEM],
-        (pltpu.VMEM((2, 256, 128), F32), pltpu.VMEM((256, 128), F32)),
+        (pltpu.VMEM((2, 288, 128), F32), pltpu.VMEM((264, 128), F32)),
     )(held(partial))
     incoming = lax.all_to_all(incoming, ("y", "xl"), 0, 0, tiled=True)
     beyond = lax.ppermute(incoming, "c", beside)
@@ -428,7 +428,7 @@
         (shaped((6, 64, 256), F32), shaped((64, 128), F32)),
         [VMEM] * 5 + [anywhere],
         (
-            pltpu.VMEM((6, 64, 128), F32), pltpu.VMEM((64, 128), F32),
+            pltpu.VMEM((6, 64, 128), F32), pltpu.VMEM((72, 128), F32),
             pltpu.SemaphoreType.DMA((7,)),
         ),
         out_specs=(anywhere, anywhere),

time: 75.7 us -> 75.7 us (level)
  no operation moved by 1% of the time
where the time goes in v12:
time: 75.7 us; the launch traced here: 75.3 us
  blocking collectives  47.4 us (63%)
  Pallas kernels  13.1 us (17%)
  waiting for transfers between devices  6.79 us (9%)
  starting transfers between devices  5.96 us (8%)
  between operations  1.44 us (2%)
    all_to_all x1, blocking collectives, per_device(): lax.all_to_all(message, AXES, 0, 0, axis_index_groups=SETS, tiled=True)  19.3 us
    all_to_all x1, blocking collectives, per_device(): partial = lax.all_to_all(partial, ('y', 'xl'), 0, 0, tiled=True)  16.2 us
    all_to_all x1, blocking collectives, per_device(): incoming = lax.all_to_all(incoming, ('y', 'xl'), 0, 0, tiled=True)  12 us
    all_to_all x1, waiting for transfers between devices, per_device(): lax.all_to_all(parts, AXES, 0, 0, axis_index_groups=SETS, tiled=True)  4.2 us
    all_to_all x1, starting transfers between devices, per_device(): lax.all_to_all(parts, AXES, 0, 0, axis_index_groups=SETS, tiled=True)  3.51 us
    pallas_call x1, Pallas kernels, per_device(): call(element_kernel, (shaped((6, 64, 256), F32), vmem((6, 64, 128), F32),...  2.95 us
    ppermute x1, starting transfers between devices, per_device(): off_chip = lax.ppermute(off_chip, AXES, across)  2.36 us
    pallas_call x1, Pallas kernels, per_device(): call(far_kernel, vmem((8, 64, 128), BF16), [VMEM] * 3, blocks + (pltpu.VM...  2.35 us
  transfers between devices with their start and end apart: 4, of which 3 were waited for; matrix products, arithmetic and copies ran while one was open for 0% of the time, Pallas kernels for 11%

profile of v12, /device:TPU:0, one launch (start us, length us, event | category | flops | bytes accessed | tf_op | source)
XLA Modules:
  0.0 75.3 jit_solution(14198185419974909166)
XLA Ops:
  1.3 1.4 %shard_map.176 = (bf16[8,272,128]{2,1,0:T(8,128)(2,1)S(1)}, bf16[16,384]{1,0:T(8,128)(2,1)S(1)}, bf16[16,384]{1,0:T(8,128)(2,1)S(1)}) custom-call(s32[2,16]{1,0:T(2,128)} %send_ref.1, s32[1,1,16]{2,1,0:T(1,128)} %dest_ref.1, s32[1,1]{1,0:T(1,128)S(6)} %copy.21.count_ref, f32[6]{0:T(128)} %coef_ref.1, f32[6,64,256]{2,1,0:T(8,128)} %fields_ref.3, ...), custom_call_target="tpu_custom_call" | custom-call | tf_op jit(solution)/shard_map/pallas_call | solution.py:365
  2.7 19.3 %all_to_all.20.got_ref = bf16[8,272,128]{2,1,0:T(8,128)(2,1)S(1)} all-to-all(bf16[8,272,128]{2,1,0:T(8,128)(2,1)S(1)} %get-tuple-element.18), channel_id=1, replica_groups={{0,6,8,14,16,22,24,30},{1,7,9,15,17,23,25,31},{4,2,12,10,20,18,28,26},{..., dimensions={0} | all-to-all | bytes 1114112 | tf_op jit(solution)/shard_map/all_to_all | solution.py:379
  22.0 1.5 %shard_map.177 = bf16[8,272,128]{2,1,0:T(8,128)(2,1)S(1)} custom-call(bf16[8,272,128]{2,1,0:T(8,128)(2,1)S(1)} %all_to_all.20.got_ref, bf16[16,384]{1,0:T(8,128)(2,1)S(1)} %get-tuple-element.19.on_ref), custom_call_target="tpu_custom_call" | custom-call | tf_op jit(solution)/shard_map/pallas_call | solution.py:381
  23.5 0.1 collective-permute-start
  23.6 1.5 %shard_map.178 = (f32[8,256,128]{2,1,0:T(8,128)S(1)}, bf16[64,128]{1,0:T(8,128)(2,1)S(1)}) custom-call(bf16[8,272,128]{2,1,0:T(8,128)(2,1)S(1)} %all_to_all.20.got_ref), custom_call_target="tpu_custom_call" | custom-call | tf_op jit(solution)/shard_map/pallas_call | solution.py:387
  25.0 0.5 collective-permute-done.came_ref
  25.5 0.1 shard_map.179
  25.6 16.2 %all_to_all.21.got_ref = bf16[8,320,128]{2,1,0:T(8,128)(2,1)S(1)} all-to-all(bf16[8,320,128]{2,1,0:T(8,128)(2,1)S(1)} %get-tuple-element.23), channel_id=1, replica_groups=mesh['y'=4,'z'=4,'xl'=2,'xh'=2,'c'=2] {'y','xl'}, dimensions={0} | all-to-all | bytes 1310720 | tf_op jit(solution)/shard_map/all_to_all | solution.py:396
  41.8 0.7 shard_map.180
  42.5 12.0 %all_to_all.22.here_ref = bf16[8,256,128]{2,1,0:T(8,128)(2,1)S(1)} all-to-all(bf16[8,256,128]{2,1,0:T(8,128)(2,1)S(1)} %shard_map.180), channel_id=1, replica_groups=mesh['y'=4,'z'=4,'xl'=2,'xh'=2,'c'=2] {'y','xl'}, dimensions={0} | all-to-all | bytes 1048576 | tf_op jit(solution)/shard_map/all_to_all | solution.py:403
  54.5 0.0 collective-permute-start.1
  54.5 2.4 %collective-permute-start.2 = (bf16[16,384]{1,0:T(8,128)(2,1)S(1)}, bf16[16,384]{1,0:T(8,128)(2,1)S(1)}, u32[]{:S(2)}, u32[]{:S(2)}) collective-permute-start(bf16[16,384]{1,0:T(8,128)(2,1)S(1)} %get-tuple-element.25), channel_id=1, source_target_pairs={{0,127},{1,2},{2,1},{3,4},{4,3},{5,6},{6,5},{7,8},{8,7},{9,10},{10... | collective-permute-start | bytes 36872 | tf_op jit(solution)/shard_map/ppermute | solution.py:378
  56.8 1.7 %shard_map.181.before_ref = f32[8,64,128]{2,1,0:T(8,128)S(1)} custom-call(bf16[8,256,128]{2,1,0:T(8,128)(2,1)S(1)} %all_to_all.22.here_ref, bf16[8,272,128]{2,1,0:T(8,128)(2,1)S(1)} %all_to_all.20.got_ref), custom_call_target="tpu_custom_call" | custom-call | tf_op jit(solution)/shard_map/pallas_call | solution.py:405
  58.5 0.0 collective-permute-done.1.there_ref
  58.5 0.0 copy-start
  58.6 2.3 %shard_map.182 = bf16[8,64,128]{2,1,0:T(8,128)(2,1)} custom-call(bf16[8,256,128]{2,1,0:T(8,128)(2,1)S(1)} %collective-permute-done.1.there_ref, bf16[8,272,128]{2,1,0:T(8,128)(2,1)S(1)} %all_to_all.20.got_ref, f32[8,64,128]{2,1,0:T(8,128)S(1)} %shard_map.181.before_ref), custom_call_target="tpu_custom_call" | custom-call | tf_op jit(solution)/shard_map/pallas_call | solution.py:408
  60.9 2.1 %collective-permute-done.2.off_ref = bf16[16,384]{1,0:T(8,128)(2,1)S(1)} collective-permute-done((bf16[16,384]{1,0:T(8,128)(2,1)S(1)}, bf16[16,384]{1,0:T(8,128)(2,1)S(1)}, u32[]{:S(2)}, u32[]{:S(2)}) %collective-permute-start.2) | collective-permute-done | bytes 12320 | tf_op jit(solution)/shard_map/ppermute | solution.py:378
  63.0 0.0 copy-start.1
  63.0 0.0 copy-start.2
  63.0 0.0 copy-start.3
  63.0 0.0 copy-start.4
  63.0 0.0 copy-start.5
  63.0 0.0 copy-start.8
  63.1 3.5 %all-to-all-start.3 = ((bf16[8,64,128]{2,1,0:T(8,128)(2,1)}), bf16[8,64,128]{2,1,0:T(8,128)(2,1)S(1)}, u32[]{:S(2)}, u32[]{:S(2)}) async-start(bf16[8,64,128]{2,1,0:T(8,128)(2,1)} %shard_map.182), calls=%async_computation.3 | async-start | bytes 262144 | tf_op jit(solution)/shard_map/all_to_all | solution.py:425
  66.6 0.0 copy-start.6
  66.6 0.0 copy-start.7
  66.6 0.0 copy-done
  66.6 0.0 copy-done.1
  66.6 0.0 copy-done.2
  66.6 0.0 copy-done.3
  66.6 0.0 copy-done.4
  66.7 0.0 copy-done.5
  66.7 0.0 copy-done.8
  66.7 0.6 copy-done.6
  67.3 0.0 copy-done.7
  67.3 2.9 %shard_map.183 = (f32[6,64,256]{2,1,0:T(8,128)}, f32[6,64,128]{2,1,0:T(8,128)S(1)}, f32[64,128]{1,0:T(8,128)S(1)}, f32[64,128]{1,0:T(8,128)S(1)}, f32[6,8,128]{2,1,0:T(8,128)S(1)}) custom-call(f32[6,6,6]{2,1,0:T(8,128)S(1)} %copy-done.4, f32[6]{0:T(128)S(1)} %copy-done.7, f32[6,64,256]{2,1,0:T(8,128)S(1)} %copy-done, f32[1,256]{1,0:T(1,128)S(1)} %bitcast.4, ...), custom_call_target="tpu_custom_call" | custom-call | tf_op jit(solution)/shard_map/pallas_call | solution.py:413
  70.2 4.2 %all-to-all-done.3.parts_ref = bf16[8,64,128]{2,1,0:T(8,128)(2,1)S(1)} async-done(((bf16[8,64,128]{2,1,0:T(8,128)(2,1)}), bf16[8,64,128]{2,1,0:T(8,128)(2,1)S(1)}, u32[]{:S(2)}, u32[]{:S(2)}) %all-to-all-start.3) | async-done | bytes 131104 | tf_op jit(solution)/shard_map/all_to_all | solution.py:425
  74.4 0.9 %shard_map.184 = (f32[6,64,256]{2,1,0:T(8,128)}, f32[64,128]{1,0:T(8,128)}) custom-call(bf16[8,64,128]{2,1,0:T(8,128)(2,1)S(1)} %all-to-all-done.3.parts_ref, f32[6,64,128]{2,1,0:T(8,128)S(1)} %get-tuple-element.29.first_ref, f32[64,128]{1,0:T(8,128)S(1)} %get-tuple-element.30.nodes_ref, ...), custom_call_target="tpu_custom_call", output_to_operand_aliasing={{0}: (5, {})} | custom-call | tf_op jit(solution)/shard_map/pallas_call | solution.py:426
Async XLA Ops:
  23.5 2.0 %collective-permute-start = (bf16[8,272,128]{2,1,0:T(8,128)(2,1)S(1)}, bf16[8,272,128]{2,1,0:T(8,128)(2,1)S(1)}, u32[]{:S(2)}, u32[]{:S(2)}) collective-permute-start(bf16[8,272,128]{2,1,0:T(8,128)(2,1)S(1)} %shard_map.177), channel_id=1, source_target_pairs={{0,1},{1,0},{2,3},{3,2},{4,5},{5,4},{6,7},{7,6},{8,9},{9,8},{10,11... | collective-permute-start | bytes 1671176 | tf_op jit(solution)/shard_map/ppermute | solution.py:385
  54.5 4.1 %collective-permute-start.1 = (bf16[8,256,128]{2,1,0:T(8,128)(2,1)S(1)}, bf16[8,256,128]{2,1,0:T(8,128)(2,1)S(1)}, u32[]{:S(2)}, u32[]{:S(2)}) collective-permute-start(bf16[8,256,128]{2,1,0:T(8,128)(2,1)S(1)} %all_to_all.22.here_ref), channel_id=1, source_target_pairs={{0,1},{1,0},{2,3},{3,2},{4,5},{5,4},{6,7},{7,6},{8,9},{9,8},{10,11... | collective-permute-start | bytes 1572872 | tf_op jit(solution)/shard_map/ppermute | solution.py:404
  54.5 8.6 %collective-permute-start.2 = (bf16[16,384]{1,0:T(8,128)(2,1)S(1)}, bf16[16,384]{1,0:T(8,128)(2,1)S(1)}, u32[]{:S(2)}, u32[]{:S(2)}) collective-permute-start(bf16[16,384]{1,0:T(8,128)(2,1)S(1)} %get-tuple-element.25), channel_id=1, source_target_pairs={{0,127},{1,2},{2,1},{3,4},{4,3},{5,6},{6,5},{7,8},{8,7},{9,10},{10... | collective-permute-start | bytes 36872 | tf_op jit(solution)/shard_map/ppermute | solution.py:378
  58.5 8.1 %copy-start = (f32[6,64,256]{2,1,0:T(8,128)S(1)}, f32[6,64,256]{2,1,0:T(8,128)}, u32[]{:S(2)}) copy-start(f32[6,64,256]{2,1,0:T(8,128)} %fields_ref.3) | copy-start | bytes 1179652
  63.0 3.6 %copy-start.1 = (f32[6,16,64]{2,1,0:T(8,128)S(1)}, f32[6,16,64]{2,1,0:T(8,128)}, u32[]{:S(2)}) copy-start(f32[6,16,64]{2,1,0:T(8,128)} %interp_ref.3) | copy-start | bytes 73732
  63.0 3.6 %copy-start.2 = (f32[3,64,64]{2,1,0:T(8,128)S(1)}, f32[3,64,64]{2,1,0:T(8,128)}, u32[]{:S(2)}) copy-start(f32[3,64,64]{2,1,0:T(8,128)} %diff_ref.1) | copy-start | bytes 147460
  63.0 3.6 %copy-start.3 = (f32[6,64,16]{1,2,0:T(8,128)S(1)}, f32[6,64,16]{1,2,0:T(8,128)}, u32[]{:S(2)}) copy-start(f32[6,64,16]{1,2,0:T(8,128)} %param.21) | copy-start | bytes 73732
  63.0 3.6 %copy-start.4 = (f32[6,6,6]{2,1,0:T(8,128)S(1)}, f32[6,6,6]{2,1,0:T(8,128)}, u32[]{:S(2)}) copy-start(f32[6,6,6]{2,1,0:T(8,128)} %couple_ref.1) | copy-start | bytes 2596
  63.0 3.6 %copy-start.5 = (s32[6,256]{1,0:T(8,128)S(1)}, s32[6,256]{1,0:T(8,128)}, u32[]{:S(2)}) copy-start(s32[6,256]{1,0:T(8,128)} %links_ref.1) | copy-start | bytes 18436
  63.0 3.6 %copy-start.8 = (f32[64]{0:T(128)S(1)}, f32[64]{0:T(128)}, u32[]{:S(2)}) copy-start(f32[64]{0:T(128)} %param.27) | copy-start | bytes 772
  63.1 11.4 %all-to-all-start.3 = ((bf16[8,64,128]{2,1,0:T(8,128)(2,1)}), bf16[8,64,128]{2,1,0:T(8,128)(2,1)S(1)}, u32[]{:S(2)}, u32[]{:S(2)}) async-start(bf16[8,64,128]{2,1,0:T(8,128)(2,1)} %shard_map.182), calls=%async_computation.3 | async-start | bytes 262144 | tf_op jit(solution)/shard_map/all_to_all | solution.py:425
  66.6 0.7 copy-start.6
  66.6 0.7 copy-start.7
